TPU v7x, 32 devices: a whole 2x2x4 slice. The times are simulated.
32 devices in a mesh: blk: 4 (over z), sub: 8 (over y, x, core).
Axes of the slice: x: 2, y: 2, z: 4, core: 2. Of those that a mesh axis runs over, the one named last changes fastest.
Arguments:
- rhs: float32 [256, 16, 256], P(('blk', 'sub')), may hold values from -6 to 6
- leaf_neighbors: int32 [256, 6], P(('blk', 'sub')), may hold values from -1 to 255, as said below
- parent_neighbors: int32 [32, 6], replicated, may hold values from -1 to 31, as said below
- children: int32 [32, 8], replicated, may hold values from 0 to 255, as said below
- owners: int32 [32], replicated, may hold values from 0 to 7, as said below
- parent_places: int32 [32], replicated, may hold values from 0 to 31, as said below
Outputs:
- leaf_solution: float32 [256, 16, 256], P(('blk', 'sub'))
- parent_solution: float32 [96, 16, 256], P(('blk', 'sub'))
Inputs may be any that keep to these rules, and one draw needn't show every extreme that they name: `leaf_neighbors`: entry f of block b is the leaf block across face f of b, or -1 on the domain's boundary; the relation is mutual. Leaves d * 8 onward are the blocks of device d in order of blk then sub; a range is the 64 leaves of one index of blk. The -x and +x neighbours of a leaf belong to the devices one index lower and one index higher along sub with the same blk index; its -y and +y neighbours belong to its own device; its -z and +z neighbours belong to its own device or to the device one index lower or higher along blk with the same sub index. `parent_neighbors`: entry f of parent p is the parent block across face f of p, or -1; mutual. Range r holds the parents r * 8 onward; x and y neighbours lie in the same range, -z and +z neighbours in the range just below or above. Entry o = 4 oz + 2 oy + ox names the child in octant (oz, oy, ox); every leaf is the child of one parent, and a parent's children lie in the leaf range with the same index as the parent's range; its four children with ox = 0 belong to one device of even index 2k along sub and its four with ox = 1 to the device 2k + 1 with the same blk index. `owners`: within each range no index owns more than 3 parents, and some index owns exactly 3. `parent_places`: A permutation; parents of range r have places r * 8 onward.
All inputs are finite; a program needn't handle non-finite values.
Results may differ from a plain program's by a relative error of at most 0.0003.
Values sent between devices are 32-bit elements; how exact they have to be, the bound alone decides.
No kernel may reach another device: no remote copies, remote signals or barrier semaphores. Data moves between devices by JAX's collectives and lax.ppermute only.
A program may use at most 64 MiB of HBM per device.

v0:
```python
import jax
import jax.numpy as jnp
from jax import lax
from jax.sharding import PartitionSpec as P

ROOT_SWEEPS = 8
PMOST = 3


relax_weight = 0.8


def extended(block, sides, width):
    for axis, dim in sides:
        count = lax.axis_size(axis)
        forward = [(i, i + 1) for i in range(count - 1)]
        backward = [(target, source) for source, target in forward]
        low = lax.ppermute(
            lax.slice_in_dim(block, block.shape[dim] - width, None, axis=dim), axis, forward
        )
        high = lax.ppermute(lax.slice_in_dim(block, 0, width, axis=dim), axis, backward)
        block = jnp.concatenate([low, block, high], axis=dim)
    return block


def lane_parts():
    lanes = jnp.arange(256, dtype=jnp.int32)
    return (lanes // 16, lanes % 16)


def exact_dot(left, table):
    return jnp.einsum("...k,kl->...l", left, table, precision=lax.Precision.HIGHEST)


def spread_table(column):
    lane_y, lane_x = lane_parts()
    picked = (jnp.arange(16, dtype=jnp.int32)[:, None] == lane_y[None, :]) & (
        lane_x[None, :] == column
    )
    return picked.astype(jnp.float32)


def block_faces(values):
    blocks = values.shape[0]
    stacked = jnp.stack(
        [
            values[:, :, 0::16].reshape(blocks, 256),
            values[:, :, 15::16].reshape(blocks, 256),
            values[:, :, 0:16].reshape(blocks, 256),
            values[:, :, 240:256].reshape(blocks, 256),
            values[:, 0],
            values[:, 15],
        ],
        axis=1,
    )
    return stacked


def apply_operator(values, ghosts):
    blocks = values.shape[0]
    lane_y, lane_x = lane_parts()
    ghost_x_low = ghosts[:, 0].reshape(blocks, 16, 16)
    ghost_x_high = ghosts[:, 1].reshape(blocks, 16, 16)
    ghost_y_low = ghosts[:, 2].reshape(blocks, 16, 16)
    ghost_y_high = ghosts[:, 3].reshape(blocks, 16, 16)
    from_left = jnp.where(
        lane_x[None, None, :] > 0, jnp.pad(values, ((0, 0), (0, 0), (1, 0)))[:, :, :256], 0.0
    )
    from_right = jnp.where(
        lane_x[None, None, :] < 15, jnp.pad(values, ((0, 0), (0, 0), (0, 1)))[:, :, 1:], 0.0
    )
    beside_all = from_left + exact_dot(ghost_x_low, spread_table(0))
    beside_all = beside_all + from_right + exact_dot(ghost_x_high, spread_table(15))
    beside_all = (
        beside_all
        + jnp.pad(values, ((0, 0), (0, 0), (16, 0)))[:, :, :256]
        + jnp.pad(ghost_y_low, ((0, 0), (0, 0), (0, 240)))
    )
    beside_all = (
        beside_all
        + jnp.pad(values, ((0, 0), (0, 0), (0, 16)))[:, :, 16:]
        + jnp.pad(ghost_y_high, ((0, 0), (0, 0), (240, 0)))
    )
    beside_all = beside_all + jnp.concatenate([ghosts[:, 4][:, None], values[:, :-1]], axis=1)
    beside_all = beside_all + jnp.concatenate([values[:, 1:], ghosts[:, 5][:, None]], axis=1)
    return 6.0 * values - beside_all


def jacobi_sweep(values, forcing, ghosts):
    return values + relax_weight / 6.0 * (forcing - apply_operator(values, ghosts))


def restrict_table():
    lane_y, lane_x = lane_parts()
    target = lane_y // 2 * 8 + lane_x // 2
    return (target[:, None] == jnp.arange(64, dtype=jnp.int32)[None, :]).astype(jnp.float32)


def coarse_table():
    lane_y, lane_x = lane_parts()
    target = lane_y // 4 * 4 + lane_x // 4
    return (target[:, None] == jnp.arange(16, dtype=jnp.int32)[None, :]).astype(jnp.float32)


def place_table():
    source_id = jnp.arange(256, dtype=jnp.int32)
    octant_y = source_id // 128
    octant_x = source_id // 64 % 2
    inner_y = source_id // 8 % 8
    inner_x = source_id % 8
    target = (8 * octant_y + inner_y) * 16 + 8 * octant_x + inner_x
    return (target[:, None] == jnp.arange(256, dtype=jnp.int32)[None, :]).astype(jnp.float32)


def restrict_octants(values):
    blocks = values.shape[0]
    paired = values.reshape(blocks, 8, 2, 256).sum(axis=2)
    return (exact_dot(paired, restrict_table()) * 0.5).reshape(blocks, 512)


def assemble(octant_rows):
    blocks = octant_rows.shape[0]
    arranged = (
        octant_rows.reshape(blocks, 2, 2, 2, 8, 64)
        .transpose(0, 1, 4, 2, 3, 5)
        .reshape(blocks, 16, 256)
    )
    return exact_dot(arranged, place_table())


def coarsen(values):
    blocks = values.shape[0]
    layered = values.reshape(blocks, 4, 4, 256).sum(axis=2)
    return (exact_dot(layered, coarse_table()) * 0.25).reshape(blocks, 64)


def widen_root(coarse):
    blocks = coarse.shape[0]
    flat = exact_dot(coarse.reshape(blocks, 4, 16), coarse_table().T)
    return jnp.repeat(flat, 4, axis=1)


def octant_split(values):
    blocks = values.shape[0]
    moved = exact_dot(values, place_table().T)
    return moved.reshape(blocks, 2, 8, 2, 2, 64).transpose(0, 1, 3, 4, 2, 5).reshape(blocks, 8, 512)


def widen_leaf(octant):
    blocks = octant.shape[0]
    flat = exact_dot(octant.reshape(blocks, 8, 64), restrict_table().T)
    return jnp.repeat(flat, 2, axis=1)


def slot_ranks(range_owners):
    width = range_owners.shape[1]
    same_owner = range_owners[:, :, None] == range_owners[:, None, :]
    earlier = (
        jnp.arange(width, dtype=jnp.int32)[:, None] > jnp.arange(width, dtype=jnp.int32)[None, :]
    )
    return jnp.sum(same_owner & earlier[None], axis=2)


def root_relax(root_values, root_source, row_len):
    plane_len = root_values.shape[1]
    padded_z = jnp.pad(root_values, ((1, 1), (0, 0)))
    padded_row = jnp.pad(root_values, ((0, 0), (row_len, row_len)))
    column_x = jnp.arange(plane_len, dtype=jnp.int32)[None, :] % row_len
    beside_all = padded_z[:-2] + padded_z[2:]
    beside_all = (
        beside_all
        + padded_row[:, :plane_len]
        + padded_row[:, 2 * row_len : 2 * row_len + plane_len]
    )
    beside_all = beside_all + jnp.where(
        column_x > 0, padded_row[:, row_len - 1 : row_len - 1 + plane_len], 0.0
    )
    beside_all = beside_all + jnp.where(
        column_x < row_len - 1, padded_row[:, row_len + 1 : row_len + 1 + plane_len], 0.0
    )
    return root_values + relax_weight / 6.0 * (root_source - (6.0 * root_values - beside_all))


def stack_table(range_faces, outer_faces):
    row_count = range_faces.shape[0]
    return jnp.concatenate(
        [
            range_faces.reshape(row_count * 6, 256),
            outer_faces[0],
            outer_faces[1],
            jnp.zeros((1, 256), jnp.float32),
        ],
        axis=0,
    )


def lookup(face_table, rows_index):
    blocks = rows_index.shape[0]
    return jnp.take(face_table, rows_index.reshape(-1), axis=0).reshape(blocks, 6, 256)


def table_index(neighbours, range_start, range_len):
    opposite = jnp.array([1, 0, 3, 2, 5, 4], dtype=jnp.int32)
    local_id = neighbours - range_start
    inside = (local_id >= 0) & (local_id < range_len)
    from_below = (neighbours >= 0) & (local_id < 0)
    from_above = local_id >= range_len
    rows_index = jnp.where(inside, local_id * 6 + opposite[None, :], range_len * 8)
    rows_index = jnp.where(from_below, range_len * 6 + local_id + range_len, rows_index)
    return jnp.where(from_above, range_len * 7 + local_id - range_len, rows_index)


def leaf_index(neighbours, blk_here, sub_here, sub_count):
    blocks = neighbours.shape[0]
    opposite = jnp.array([1, 0, 3, 2, 5, 4], dtype=jnp.int32)
    clamped = jnp.maximum(neighbours, 0)
    device_id = clamped // blocks
    local_id = clamped % blocks
    other_blk = device_id // sub_count
    other_sub = device_id % sub_count
    present = neighbours >= 0
    same_blk = present & (other_blk == blk_here)
    same_sub = present & (other_sub == sub_here)
    rows_index = jnp.where(same_blk & same_sub, local_id * 6 + opposite[None, :], blocks * 10)
    rows_index = jnp.where(
        same_blk & (other_sub == sub_here - 1), blocks * 6 + local_id, rows_index
    )
    rows_index = jnp.where(
        same_blk & (other_sub == sub_here + 1), blocks * 7 + local_id, rows_index
    )
    rows_index = jnp.where(
        same_sub & (other_blk == blk_here - 1), blocks * 8 + local_id, rows_index
    )
    rows_index = jnp.where(
        same_sub & (other_blk == blk_here + 1), blocks * 9 + local_id, rows_index
    )
    return rows_index


def leaf_table(values):
    face_rows = block_faces(values)
    blocks = face_rows.shape[0]
    side_rows = jnp.stack([face_rows[:, 0], face_rows[:, 1]], axis=0)
    side_wide = extended(side_rows, (("sub", 0),), 1)
    edge_rows = jnp.stack([face_rows[:, 4], face_rows[:, 5]], axis=0)
    edge_wide = extended(edge_rows, (("blk", 0),), 1)
    return jnp.concatenate(
        [
            face_rows.reshape(blocks * 6, 256),
            side_wide[0],
            side_wide[3],
            edge_wide[0],
            edge_wide[3],
            jnp.zeros((1, 256), jnp.float32),
        ],
        axis=0,
    )


def range_table(values):
    face_rows = block_faces(values)
    edge_rows = jnp.stack([face_rows[:, 4], face_rows[:, 5]], axis=0)
    widened = extended(edge_rows, (("blk", 0),), 1)
    return stack_table(face_rows, jnp.stack([widened[0], widened[3]], axis=0))


def local(rhs, leaf_neighbors, parent_neighbors, children, owners, parent_places):
    factor = relax_weight / 6.0
    blk_count = lax.axis_size("blk")
    sub_count = lax.axis_size("sub")
    blk_here = lax.axis_index("blk")
    sub_here = lax.axis_index("sub")
    blocks = rhs.shape[0]
    range_len = blocks * sub_count
    parent_len = range_len // 8
    range_start = blk_here * range_len
    parent_start = blk_here * parent_len
    leaf_rows = leaf_index(leaf_neighbors, blk_here, sub_here, sub_count)
    sweep_one = factor * rhs
    second = jacobi_sweep(sweep_one, rhs, lookup(leaf_table(sweep_one), leaf_rows))
    residual = rhs - apply_operator(second, lookup(leaf_table(second), leaf_rows))
    octant_rows = lax.all_gather(restrict_octants(residual), "sub", axis=0, tiled=True)
    range_children = lax.dynamic_slice_in_dim(children, parent_start, parent_len, 0) - range_start
    ranks_all = slot_ranks(owners.reshape(blk_count, parent_len)).reshape(-1)
    range_owners = lax.dynamic_slice_in_dim(owners, parent_start, parent_len, 0)
    range_ranks = lax.dynamic_slice_in_dim(ranks_all, parent_start, parent_len, 0)
    slot_match = (range_owners[None, :] == sub_here) & (
        range_ranks[None, :] == jnp.arange(PMOST, dtype=jnp.int32)[:, None]
    )
    filled = jnp.any(slot_match, axis=1)
    slot_local = jnp.sum(
        jnp.where(slot_match, jnp.arange(parent_len, dtype=jnp.int32)[None, :], 0), axis=1
    )
    filled_gain = filled.astype(jnp.float32)[:, None, None]
    own_local = sub_here * blocks + jnp.arange(blocks, dtype=jnp.int32)
    matches = range_children.reshape(-1)[None, :] == own_local[:, None]
    flat_place = jnp.sum(
        jnp.where(matches, jnp.arange(parent_len * 8, dtype=jnp.int32)[None, :], 0), axis=1
    )
    leaf_parent = flat_place // 8
    leaf_octant = flat_place % 8
    source = assemble(octant_rows[range_children])
    parent_rows = table_index(
        lax.dynamic_slice_in_dim(parent_neighbors, parent_start, parent_len, 0),
        parent_start,
        parent_len,
    )
    global_places = lax.dynamic_slice_in_dim(parent_places, parent_start, parent_len, 0)
    keep_gain = jnp.ones((parent_len, 1, 1), jnp.float32)
    parent_one = factor * source
    parent_two = jacobi_sweep(parent_one, source, lookup(range_table(parent_one), parent_rows))
    parent_rest = source - apply_operator(parent_two, lookup(range_table(parent_two), parent_rows))
    coarse = coarsen(parent_rest)
    root_slab = (
        jnp.zeros((parent_len, 64), jnp.float32).at[global_places - parent_start].set(coarse)
    )
    ordered = lax.all_gather(root_slab, "blk", axis=0, tiled=True)
    side_y = blocks // 4
    side_x = sub_count // 2
    root_source = (
        ordered.reshape(blk_count, side_y, side_x, 4, 4, 4)
        .transpose(0, 3, 1, 4, 2, 5)
        .reshape(4 * blk_count, 16 * side_y * side_x)
    )
    root_source = root_source - jnp.mean(root_source)
    root_values = jnp.zeros_like(root_source)
    for repeat in range(ROOT_SWEEPS):
        root_values = root_relax(root_values, root_source, 4 * side_x)
    root_back = (
        root_values.reshape(blk_count, 4, side_y, 4, side_x, 4)
        .transpose(0, 2, 4, 1, 3, 5)
        .reshape(blk_count * parent_len, 64)[global_places]
    )
    parent_three = parent_two + widen_root(root_back) * keep_gain
    parent_four = jacobi_sweep(parent_three, source, lookup(range_table(parent_three), parent_rows))
    parent_solution = parent_four[slot_local] * filled_gain
    own_parents = parent_four[leaf_parent]
    pieces = octant_split(own_parents)
    chosen = jnp.take_along_axis(pieces, leaf_octant[:, None, None], axis=1)[:, 0]
    leaf_three = second + widen_leaf(chosen)
    leaf_solution = jacobi_sweep(leaf_three, rhs, lookup(leaf_table(leaf_three), leaf_rows))
    return (leaf_solution, parent_solution)


def solution(mesh):
    in_specs = (P(("blk", "sub"), None, None), P(("blk", "sub"), None), P(), P(), P(), P())
    out_specs = (P(("blk", "sub"), None, None), P(("blk", "sub"), None, None))
    return jax.shard_map(local, mesh=mesh, in_specs=in_specs, out_specs=out_specs, check_vma=False)
```

profile of v0, /device:TPU:0, one launch (start us, length us, event | category | flops | bytes accessed | tf_op | source)
XLA Modules:
  0.0 119.8 jit_solution(17477033605572379982)
XLA Ops:
  0.6 0.9 broadcast_multiply_fusion.1
  2.0 2.4 %collective-permute-start = (f32[1,8,256]{2,1,0:T(8,128)S(1)}, f32[1,8,256]{2,1,0:T(8,128)S(1)}, u32[]{:S(2)}, u32[]{:S(2)}) collective-permute-start(f32[1,8,256]{2,1,0:T(8,128)S(1)} %stack_squeeze_stack_reshape.18), channel_id=1, source_target_pairs={{0,1},{1,2},{2,3},{3,4},{4,5},{5,6},{6,7},{8,9},{9,10},{10,11},{11... | collective-permute-start | bytes 24584 | tf_op jit(solution)/shard_map/ppermute | solution.py:18
  4.8 1.3 %collective-permute-start.1 = (f32[1,8,256]{2,1,0:T(8,128)S(1)}, f32[1,8,256]{2,1,0:T(8,128)S(1)}, u32[]{:S(2)}, u32[]{:S(2)}) collective-permute-start(f32[1,8,256]{2,1,0:T(8,128)S(1)} %stack_squeeze_stack_reshape.19), channel_id=1, source_target_pairs={{1,0},{2,1},{3,2},{4,3},{5,4},{6,5},{7,6},{9,8},{10,9},{11,10},{12... | collective-permute-start | bytes 24584 | tf_op jit(solution)/shard_map/ppermute | solution.py:21
  6.1 4.3 %collective-permute-start.2 = (f32[1,8,256]{2,0,1:T(1,128)S(1)}, f32[1,8,256]{2,0,1:T(1,128)S(1)}, u32[]{:S(2)}, u32[]{:S(2)}) collective-permute-start(f32[1,8,256]{2,0,1:T(1,128)S(1)} %get-tuple-element.73), channel_id=1, source_target_pairs={{0,8},{8,16},{16,24},{1,9},{9,17},{17,25},{2,10},{10,18},{18,26},{... | collective-permute-start | bytes 24584 | tf_op jit(solution)/shard_map/ppermute | solution.py:18
  10.5 1.3 %collective-permute-start.3 = (f32[1,8,256]{2,0,1:T(1,128)S(1)}, f32[1,8,256]{2,0,1:T(1,128)S(1)}, u32[]{:S(2)}, u32[]{:S(2)}) collective-permute-start(f32[1,8,256]{2,0,1:T(1,128)S(1)} %get-tuple-element.72), channel_id=1, source_target_pairs={{8,0},{16,8},{24,16},{9,1},{17,9},{25,17},{10,2},{18,10},{26,18},{... | collective-permute-start | bytes 24584 | tf_op jit(solution)/shard_map/ppermute | solution.py:21
  21.7 4.0 %collective-permute-start.4 = (f32[1,8,256]{2,1,0:T(8,128)S(1)}, f32[1,8,256]{2,1,0:T(8,128)S(1)}, u32[]{:S(2)}, u32[]{:S(2)}) collective-permute-start(f32[1,8,256]{2,1,0:T(8,128)S(1)} %stack_squeeze_stack_reshape.20), channel_id=1, source_target_pairs={{0,1},{1,2},{2,3},{3,4},{4,5},{5,6},{6,7},{8,9},{9,10},{10,11},{11... | collective-permute-start | bytes 24584 | tf_op jit(solution)/shard_map/ppermute | solution.py:18
  25.8 1.3 %collective-permute-start.5 = (f32[1,8,256]{2,1,0:T(8,128)S(1)}, f32[1,8,256]{2,1,0:T(8,128)S(1)}, u32[]{:S(2)}, u32[]{:S(2)}) collective-permute-start(f32[1,8,256]{2,1,0:T(8,128)S(1)} %stack_squeeze_stack_reshape.21), channel_id=1, source_target_pairs={{1,0},{2,1},{3,2},{4,3},{5,4},{6,5},{7,6},{9,8},{10,9},{11,10},{12... | collective-permute-start | bytes 24584 | tf_op jit(solution)/shard_map/ppermute | solution.py:21
  27.1 4.3 %collective-permute-start.6 = (f32[1,8,256]{2,0,1:T(1,128)S(1)}, f32[1,8,256]{2,0,1:T(1,128)S(1)}, u32[]{:S(2)}, u32[]{:S(2)}) collective-permute-start(f32[1,8,256]{2,0,1:T(1,128)S(1)} %get-tuple-element.65), channel_id=1, source_target_pairs={{0,8},{8,16},{16,24},{1,9},{9,17},{17,25},{2,10},{10,18},{18,26},{... | collective-permute-start | bytes 24584 | tf_op jit(solution)/shard_map/ppermute | solution.py:18
  31.4 1.3 %collective-permute-start.7 = (f32[1,8,256]{2,0,1:T(1,128)S(1)}, f32[1,8,256]{2,0,1:T(1,128)S(1)}, u32[]{:S(2)}, u32[]{:S(2)}) collective-permute-start(f32[1,8,256]{2,0,1:T(1,128)S(1)} %get-tuple-element.64), channel_id=1, source_target_pairs={{8,0},{16,8},{24,16},{9,1},{17,9},{25,17},{10,2},{18,10},{26,18},{... | collective-permute-start | bytes 24584 | tf_op jit(solution)/shard_map/ppermute | solution.py:21
  32.7 4.2 %collective-permute-done.7 = f32[1,8,256]{2,0,1:T(1,128)S(1)} collective-permute-done((f32[1,8,256]{2,0,1:T(1,128)S(1)}, f32[1,8,256]{2,0,1:T(1,128)S(1)}, u32[]{:S(2)}, u32[]{:S(2)}) %collective-permute-start.7) | collective-permute-done | bytes 8224 | tf_op jit(solution)/shard_map/ppermute | solution.py:21
  39.1 14.1 %all_gather.6 = f32[64,512]{1,0:T(8,128)S(1)} all-gather(f32[8,512]{1,0:T(8,128)S(1)} %reshape.482), channel_id=1, replica_groups=mesh['blk'=4,'sub'=8] {'sub'}, dimensions={0}, use_global_device_ids=true | all-gather | bytes 147456 | tf_op jit(solution)/shard_map/all_gather | solution.py:282
  54.6 1.3 %collective-permute-start.9 = (f32[1,8,256]{2,0,1:T(1,128)S(1)}, f32[1,8,256]{2,0,1:T(1,128)S(1)}, u32[]{:S(2)}, u32[]{:S(2)}) collective-permute-start(f32[1,8,256]{2,0,1:T(1,128)S(1)} %get-tuple-element.57), channel_id=1, source_target_pairs={{8,0},{16,8},{24,16},{9,1},{17,9},{25,17},{10,2},{18,10},{26,18},{... | collective-permute-start | bytes 24584 | tf_op jit(solution)/shard_map/ppermute | solution.py:21
  55.9 4.5 %collective-permute-start.8 = (f32[1,8,256]{2,0,1:T(1,128)S(1)}, f32[1,8,256]{2,0,1:T(1,128)S(1)}, u32[]{:S(2)}, u32[]{:S(2)}) collective-permute-start(f32[1,8,256]{2,0,1:T(1,128)S(1)} %get-tuple-element.58), channel_id=1, source_target_pairs={{0,8},{8,16},{16,24},{1,9},{9,17},{17,25},{2,10},{10,18},{18,26},{... | collective-permute-start | bytes 24584 | tf_op jit(solution)/shard_map/ppermute | solution.py:18
  63.5 1.3 %collective-permute-start.11 = (f32[1,8,256]{2,0,1:T(1,128)S(1)}, f32[1,8,256]{2,0,1:T(1,128)S(1)}, u32[]{:S(2)}, u32[]{:S(2)}) collective-permute-start(f32[1,8,256]{2,0,1:T(1,128)S(1)} %get-tuple-element.49), channel_id=1, source_target_pairs={{8,0},{16,8},{24,16},{9,1},{17,9},{25,17},{10,2},{18,10},{26,18},{... | collective-permute-start | bytes 24584 | tf_op jit(solution)/shard_map/ppermute | solution.py:21
  64.8 4.8 %collective-permute-start.10 = (f32[1,8,256]{2,0,1:T(1,128)S(1)}, f32[1,8,256]{2,0,1:T(1,128)S(1)}, u32[]{:S(2)}, u32[]{:S(2)}) collective-permute-start(f32[1,8,256]{2,0,1:T(1,128)S(1)} %get-tuple-element.50), channel_id=1, source_target_pairs={{0,8},{8,16},{16,24},{1,9},{9,17},{17,25},{2,10},{10,18},{18,26},{... | collective-permute-start | bytes 24584 | tf_op jit(solution)/shard_map/ppermute | solution.py:18
  73.6 14.6 %all_gather.7 = f32[32,64]{1,0:T(8,128)S(1)} all-gather(f32[8,64]{1,0:T(8,128)S(1)} %scatter_custom_fusion), channel_id=1, replica_groups=mesh['blk'=4,'sub'=8] {'blk'}, dimensions={0}, use_global_device_ids=true | all-gather | bytes 10240 | tf_op jit(solution)/shard_map/all_gather | solution.py:317
  92.5 1.3 %collective-permute-start.13 = (f32[1,8,256]{2,0,1:T(1,128)S(1)}, f32[1,8,256]{2,0,1:T(1,128)S(1)}, u32[]{:S(2)}, u32[]{:S(2)}) collective-permute-start(f32[1,8,256]{2,0,1:T(1,128)S(1)} %get-tuple-element.41), channel_id=1, source_target_pairs={{8,0},{16,8},{24,16},{9,1},{17,9},{25,17},{10,2},{18,10},{26,18},{... | collective-permute-start | bytes 24584 | tf_op jit(solution)/shard_map/ppermute | solution.py:21
  93.8 4.7 %collective-permute-start.12 = (f32[1,8,256]{2,0,1:T(1,128)S(1)}, f32[1,8,256]{2,0,1:T(1,128)S(1)}, u32[]{:S(2)}, u32[]{:S(2)}) collective-permute-start(f32[1,8,256]{2,0,1:T(1,128)S(1)} %get-tuple-element.42), channel_id=1, source_target_pairs={{0,8},{8,16},{16,24},{1,9},{9,17},{17,25},{2,10},{10,18},{18,26},{... | collective-permute-start | bytes 24584 | tf_op jit(solution)/shard_map/ppermute | solution.py:18
  105.3 1.3 %collective-permute-start.14 = (f32[1,8,256]{2,1,0:T(8,128)S(1)}, f32[1,8,256]{2,1,0:T(8,128)S(1)}, u32[]{:S(2)}, u32[]{:S(2)}) collective-permute-start(f32[1,8,256]{2,1,0:T(8,128)S(1)} %stack_squeeze_stack_reshape.22), channel_id=1, source_target_pairs={{0,1},{1,2},{2,3},{3,4},{4,5},{5,6},{6,7},{8,9},{9,10},{10,11},{11... | collective-permute-start | bytes 24584 | tf_op jit(solution)/shard_map/ppermute | solution.py:18
  106.6 1.3 %collective-permute-start.15 = (f32[1,8,256]{2,1,0:T(8,128)S(1)}, f32[1,8,256]{2,1,0:T(8,128)S(1)}, u32[]{:S(2)}, u32[]{:S(2)}) collective-permute-start(f32[1,8,256]{2,1,0:T(8,128)S(1)} %stack_squeeze_stack_reshape.23), channel_id=1, source_target_pairs={{1,0},{2,1},{3,2},{4,3},{5,4},{6,5},{7,6},{9,8},{10,9},{11,10},{12... | collective-permute-start | bytes 24584 | tf_op jit(solution)/shard_map/ppermute | solution.py:21
  107.9 4.1 %collective-permute-start.16 = (f32[1,8,256]{2,0,1:T(1,128)S(1)}, f32[1,8,256]{2,0,1:T(1,128)S(1)}, u32[]{:S(2)}, u32[]{:S(2)}) collective-permute-start(f32[1,8,256]{2,0,1:T(1,128)S(1)} %get-tuple-element.33), channel_id=1, source_target_pairs={{0,8},{8,16},{16,24},{1,9},{9,17},{17,25},{2,10},{10,18},{18,26},{... | collective-permute-start | bytes 24584 | tf_op jit(solution)/shard_map/ppermute | solution.py:18
  112.0 1.3 %collective-permute-start.17 = (f32[1,8,256]{2,0,1:T(1,128)S(1)}, f32[1,8,256]{2,0,1:T(1,128)S(1)}, u32[]{:S(2)}, u32[]{:S(2)}) collective-permute-start(f32[1,8,256]{2,0,1:T(1,128)S(1)} %get-tuple-element.32), channel_id=1, source_target_pairs={{8,0},{16,8},{24,16},{9,1},{17,9},{25,17},{10,2},{18,10},{26,18},{... | collective-permute-start | bytes 24584 | tf_op jit(solution)/shard_map/ppermute | solution.py:21
  114.6 2.9 %collective-permute-done.17 = f32[1,8,256]{2,0,1:T(1,128)S(1)} collective-permute-done((f32[1,8,256]{2,0,1:T(1,128)S(1)}, f32[1,8,256]{2,0,1:T(1,128)S(1)}, u32[]{:S(2)}, u32[]{:S(2)}) %collective-permute-start.17) | collective-permute-done | bytes 8224 | tf_op jit(solution)/shard_map/ppermute | solution.py:21
  118.9 0.9 fusion.9
  (286 shorter events, 33.3 us)
Async XLA Ops:
  2.0 15.8 %collective-permute-start = (f32[1,8,256]{2,1,0:T(8,128)S(1)}, f32[1,8,256]{2,1,0:T(8,128)S(1)}, u32[]{:S(2)}, u32[]{:S(2)}) collective-permute-start(f32[1,8,256]{2,1,0:T(8,128)S(1)} %stack_squeeze_stack_reshape.18), channel_id=1, source_target_pairs={{0,1},{1,2},{2,3},{3,4},{4,5},{5,6},{6,7},{8,9},{9,10},{10,11},{11... | collective-permute-start | bytes 24584 | tf_op jit(solution)/shard_map/ppermute | solution.py:18
  4.8 13.0 %collective-permute-start.1 = (f32[1,8,256]{2,1,0:T(8,128)S(1)}, f32[1,8,256]{2,1,0:T(8,128)S(1)}, u32[]{:S(2)}, u32[]{:S(2)}) collective-permute-start(f32[1,8,256]{2,1,0:T(8,128)S(1)} %stack_squeeze_stack_reshape.19), channel_id=1, source_target_pairs={{1,0},{2,1},{3,2},{4,3},{5,4},{6,5},{7,6},{9,8},{10,9},{11,10},{12... | collective-permute-start | bytes 24584 | tf_op jit(solution)/shard_map/ppermute | solution.py:21
  6.1 11.7 %collective-permute-start.2 = (f32[1,8,256]{2,0,1:T(1,128)S(1)}, f32[1,8,256]{2,0,1:T(1,128)S(1)}, u32[]{:S(2)}, u32[]{:S(2)}) collective-permute-start(f32[1,8,256]{2,0,1:T(1,128)S(1)} %get-tuple-element.73), channel_id=1, source_target_pairs={{0,8},{8,16},{16,24},{1,9},{9,17},{17,25},{2,10},{10,18},{18,26},{... | collective-permute-start | bytes 24584 | tf_op jit(solution)/shard_map/ppermute | solution.py:18
  10.5 7.4 %collective-permute-start.3 = (f32[1,8,256]{2,0,1:T(1,128)S(1)}, f32[1,8,256]{2,0,1:T(1,128)S(1)}, u32[]{:S(2)}, u32[]{:S(2)}) collective-permute-start(f32[1,8,256]{2,0,1:T(1,128)S(1)} %get-tuple-element.72), channel_id=1, source_target_pairs={{8,0},{16,8},{24,16},{9,1},{17,9},{25,17},{10,2},{18,10},{26,18},{... | collective-permute-start | bytes 24584 | tf_op jit(solution)/shard_map/ppermute | solution.py:21
  12.1 0.7 copy-start.1
  12.8 0.7 copy-start.3
  14.0 0.7 copy-start.4
  14.7 0.7 copy-start.2
  17.0 0.7 copy-start.5
  19.1 0.9 copy-start
  21.7 11.0 %collective-permute-start.4 = (f32[1,8,256]{2,1,0:T(8,128)S(1)}, f32[1,8,256]{2,1,0:T(8,128)S(1)}, u32[]{:S(2)}, u32[]{:S(2)}) collective-permute-start(f32[1,8,256]{2,1,0:T(8,128)S(1)} %stack_squeeze_stack_reshape.20), channel_id=1, source_target_pairs={{0,1},{1,2},{2,3},{3,4},{4,5},{5,6},{6,7},{8,9},{9,10},{10,11},{11... | collective-permute-start | bytes 24584 | tf_op jit(solution)/shard_map/ppermute | solution.py:18
  25.8 6.9 %collective-permute-start.5 = (f32[1,8,256]{2,1,0:T(8,128)S(1)}, f32[1,8,256]{2,1,0:T(8,128)S(1)}, u32[]{:S(2)}, u32[]{:S(2)}) collective-permute-start(f32[1,8,256]{2,1,0:T(8,128)S(1)} %stack_squeeze_stack_reshape.21), channel_id=1, source_target_pairs={{1,0},{2,1},{3,2},{4,3},{5,4},{6,5},{7,6},{9,8},{10,9},{11,10},{12... | collective-permute-start | bytes 24584 | tf_op jit(solution)/shard_map/ppermute | solution.py:21
  27.1 5.6 %collective-permute-start.6 = (f32[1,8,256]{2,0,1:T(1,128)S(1)}, f32[1,8,256]{2,0,1:T(1,128)S(1)}, u32[]{:S(2)}, u32[]{:S(2)}) collective-permute-start(f32[1,8,256]{2,0,1:T(1,128)S(1)} %get-tuple-element.65), channel_id=1, source_target_pairs={{0,8},{8,16},{16,24},{1,9},{9,17},{17,25},{2,10},{10,18},{18,26},{... | collective-permute-start | bytes 24584 | tf_op jit(solution)/shard_map/ppermute | solution.py:18
  31.4 5.5 %collective-permute-start.7 = (f32[1,8,256]{2,0,1:T(1,128)S(1)}, f32[1,8,256]{2,0,1:T(1,128)S(1)}, u32[]{:S(2)}, u32[]{:S(2)}) collective-permute-start(f32[1,8,256]{2,0,1:T(1,128)S(1)} %get-tuple-element.64), channel_id=1, source_target_pairs={{8,0},{16,8},{24,16},{9,1},{17,9},{25,17},{10,2},{18,10},{26,18},{... | collective-permute-start | bytes 24584 | tf_op jit(solution)/shard_map/ppermute | solution.py:21
  54.6 7.1 %collective-permute-start.9 = (f32[1,8,256]{2,0,1:T(1,128)S(1)}, f32[1,8,256]{2,0,1:T(1,128)S(1)}, u32[]{:S(2)}, u32[]{:S(2)}) collective-permute-start(f32[1,8,256]{2,0,1:T(1,128)S(1)} %get-tuple-element.57), channel_id=1, source_target_pairs={{8,0},{16,8},{24,16},{9,1},{17,9},{25,17},{10,2},{18,10},{26,18},{... | collective-permute-start | bytes 24584 | tf_op jit(solution)/shard_map/ppermute | solution.py:21
  55.9 5.9 %collective-permute-start.8 = (f32[1,8,256]{2,0,1:T(1,128)S(1)}, f32[1,8,256]{2,0,1:T(1,128)S(1)}, u32[]{:S(2)}, u32[]{:S(2)}) collective-permute-start(f32[1,8,256]{2,0,1:T(1,128)S(1)} %get-tuple-element.58), channel_id=1, source_target_pairs={{0,8},{8,16},{16,24},{1,9},{9,17},{17,25},{2,10},{10,18},{18,26},{... | collective-permute-start | bytes 24584 | tf_op jit(solution)/shard_map/ppermute | solution.py:18
  63.5 7.4 %collective-permute-start.11 = (f32[1,8,256]{2,0,1:T(1,128)S(1)}, f32[1,8,256]{2,0,1:T(1,128)S(1)}, u32[]{:S(2)}, u32[]{:S(2)}) collective-permute-start(f32[1,8,256]{2,0,1:T(1,128)S(1)} %get-tuple-element.49), channel_id=1, source_target_pairs={{8,0},{16,8},{24,16},{9,1},{17,9},{25,17},{10,2},{18,10},{26,18},{... | collective-permute-start | bytes 24584 | tf_op jit(solution)/shard_map/ppermute | solution.py:21
  64.8 6.2 %collective-permute-start.10 = (f32[1,8,256]{2,0,1:T(1,128)S(1)}, f32[1,8,256]{2,0,1:T(1,128)S(1)}, u32[]{:S(2)}, u32[]{:S(2)}) collective-permute-start(f32[1,8,256]{2,0,1:T(1,128)S(1)} %get-tuple-element.50), channel_id=1, source_target_pairs={{0,8},{8,16},{16,24},{1,9},{9,17},{17,25},{2,10},{10,18},{18,26},{... | collective-permute-start | bytes 24584 | tf_op jit(solution)/shard_map/ppermute | solution.py:18
  92.5 7.3 %collective-permute-start.13 = (f32[1,8,256]{2,0,1:T(1,128)S(1)}, f32[1,8,256]{2,0,1:T(1,128)S(1)}, u32[]{:S(2)}, u32[]{:S(2)}) collective-permute-start(f32[1,8,256]{2,0,1:T(1,128)S(1)} %get-tuple-element.41), channel_id=1, source_target_pairs={{8,0},{16,8},{24,16},{9,1},{17,9},{25,17},{10,2},{18,10},{26,18},{... | collective-permute-start | bytes 24584 | tf_op jit(solution)/shard_map/ppermute | solution.py:21
  93.8 6.0 %collective-permute-start.12 = (f32[1,8,256]{2,0,1:T(1,128)S(1)}, f32[1,8,256]{2,0,1:T(1,128)S(1)}, u32[]{:S(2)}, u32[]{:S(2)}) collective-permute-start(f32[1,8,256]{2,0,1:T(1,128)S(1)} %get-tuple-element.42), channel_id=1, source_target_pairs={{0,8},{8,16},{16,24},{1,9},{9,17},{17,25},{2,10},{10,18},{18,26},{... | collective-permute-start | bytes 24584 | tf_op jit(solution)/shard_map/ppermute | solution.py:18
  105.3 9.2 %collective-permute-start.14 = (f32[1,8,256]{2,1,0:T(8,128)S(1)}, f32[1,8,256]{2,1,0:T(8,128)S(1)}, u32[]{:S(2)}, u32[]{:S(2)}) collective-permute-start(f32[1,8,256]{2,1,0:T(8,128)S(1)} %stack_squeeze_stack_reshape.22), channel_id=1, source_target_pairs={{0,1},{1,2},{2,3},{3,4},{4,5},{5,6},{6,7},{8,9},{9,10},{10,11},{11... | collective-permute-start | bytes 24584 | tf_op jit(solution)/shard_map/ppermute | solution.py:18
  106.6 7.9 %collective-permute-start.15 = (f32[1,8,256]{2,1,0:T(8,128)S(1)}, f32[1,8,256]{2,1,0:T(8,128)S(1)}, u32[]{:S(2)}, u32[]{:S(2)}) collective-permute-start(f32[1,8,256]{2,1,0:T(8,128)S(1)} %stack_squeeze_stack_reshape.23), channel_id=1, source_target_pairs={{1,0},{2,1},{3,2},{4,3},{5,4},{6,5},{7,6},{9,8},{10,9},{11,10},{12... | collective-permute-start | bytes 24584 | tf_op jit(solution)/shard_map/ppermute | solution.py:21
  107.9 6.7 %collective-permute-start.16 = (f32[1,8,256]{2,0,1:T(1,128)S(1)}, f32[1,8,256]{2,0,1:T(1,128)S(1)}, u32[]{:S(2)}, u32[]{:S(2)}) collective-permute-start(f32[1,8,256]{2,0,1:T(1,128)S(1)} %get-tuple-element.33), channel_id=1, source_target_pairs={{0,8},{8,16},{16,24},{1,9},{9,17},{17,25},{2,10},{10,18},{18,26},{... | collective-permute-start | bytes 24584 | tf_op jit(solution)/shard_map/ppermute | solution.py:18
  112.0 5.5 %collective-permute-start.17 = (f32[1,8,256]{2,0,1:T(1,128)S(1)}, f32[1,8,256]{2,0,1:T(1,128)S(1)}, u32[]{:S(2)}, u32[]{:S(2)}) collective-permute-start(f32[1,8,256]{2,0,1:T(1,128)S(1)} %get-tuple-element.32), channel_id=1, source_target_pairs={{8,0},{16,8},{24,16},{9,1},{17,9},{25,17},{10,2},{18,10},{26,18},{... | collective-permute-start | bytes 24584 | tf_op jit(solution)/shard_map/ppermute | solution.py:21
  (1 other events, 0.7 us)
where the time goes:
time: 121 us; the launch traced here: 120 us
  starting transfers between devices  46.1 us (38%)
  blocking collectives  28.6 us (24%)
  local copies, waits for them, and re-layouts  25.5 us (21%)
  waiting for transfers between devices  7.32 us (6%)
  other arithmetic  4.81 us (4%)
  matrix products  4.6 us (4%)
  between operations  2.81 us (2%)
    ppermute x9, starting transfers between devices, extended(): lax.ppermute(lax.slice_in_dim(block, block.shape[dim] - width, None, axis...  34.4 us
    all_gather x1, blocking collectives, local(): ordered = lax.all_gather(root_slab, 'blk', axis=0, tiled=True)  14.6 us
    all_gather x1, blocking collectives, local(): lax.all_gather(restrict_octants(residual), 'sub', axis=0, tiled=True)  14.1 us
    ppermute x9, starting transfers between devices, extended(): lax.ppermute(lax.slice_in_dim(block, 0, width, axis=dim), axis, backward)  11.6 us
    ppermute x9, waiting for transfers between devices, extended(): lax.ppermute(lax.slice_in_dim(block, 0, width, axis=dim), axis, backward)  7.13 us
    dot_general x18, matrix products, exact_dot(): jnp.einsum('...k,kl->...l', left, table, precision=lax.Precision.HIGHEST)  4.6 us
    unnamed x37, local copies, waits for them, and re-layouts  4.03 us
    gather x6, local copies, waits for them, and re-layouts, lookup(): jnp.take(face_table, rows_index.reshape(-1), axis=0).reshape(blocks, 6, 256)  3.77 us
  transfers between devices with their start and end apart: 18, of which 4 were waited for; matrix products, arithmetic and copies ran while one was open for 7% of the time, Pallas kernels for 0%

commit v1 on v0

--- a/solution.py
+++ b/solution.py
@@ -1,6 +1,10 @@
+import functools
+
 import jax
 import jax.numpy as jnp
 from jax import lax
+from jax.experimental import pallas as pl
+from jax.experimental.pallas import tpu as pltpu
 from jax.sharding import PartitionSpec as P
 
 ROOT_SWEEPS = 8
@@ -264,7 +268,7 @@
     return stack_table(face_rows, jnp.stack([widened[0], widened[3]], axis=0))
 
 
-def local(rhs, leaf_neighbors, parent_neighbors, children, owners, parent_places):
+def general_local(rhs, leaf_neighbors, parent_neighbors, children, owners, parent_places):
     factor = relax_weight / 6.0
     blk_count = lax.axis_size("blk")
     sub_count = lax.axis_size("sub")
@@ -342,6 +346,782 @@
     return (leaf_solution, parent_solution)
 
 
+FACTOR = relax_weight / 6.0
+SELF = 1.0 - 6.0 * FACTOR
+LANES = 128
+OWN_ROWS = 64
+MSG_ROWS = 32
+
+
+def lane_iota(shape):
+    return lax.broadcasted_iota(jnp.int32, shape, len(shape) - 1)
+
+
+def row_iota(shape):
+    return lax.broadcasted_iota(jnp.int32, shape, len(shape) - 2)
+
+
+def turn(values, shift, axis):
+    size = values.shape[axis]
+    shift = shift % size
+    if shift == 0:
+        return values
+    return pltpu.roll(values, shift, axis)
+
+
+def split_dot(left, table):
+    high = left.astype(jnp.bfloat16)
+    low = (left - high.astype(jnp.float32)).astype(jnp.bfloat16)
+    return jnp.dot(high, table, preferred_element_type=jnp.float32) + jnp.dot(
+        low, table, preferred_element_type=jnp.float32
+    )
+
+
+def zero_one(condition, scale=1.0):
+    return jnp.where(condition, scale, 0.0).astype(jnp.bfloat16)
+
+
+def beside_x(chunk, width):
+    cell = lane_iota(chunk.shape) % width
+    low = jnp.where(cell > 0, turn(chunk, 1, 1), 0.0)
+    high = jnp.where(cell < width - 1, turn(chunk, -1, 1), 0.0)
+    return low + high
+
+
+def y_pair(chunks, width):
+    lane = lane_iota(chunks[0].shape)
+    up = [turn(chunk, width, 1) for chunk in chunks]
+    down = [turn(chunk, -width, 1) for chunk in chunks]
+    zero = jnp.zeros_like(chunks[0])
+    lower = []
+    upper = []
+    for k in range(len(chunks)):
+        before = up[k - 1] if k > 0 else zero
+        after = down[k + 1] if k + 1 < len(chunks) else zero
+        lower.append(jnp.where(lane < width, before, up[k]))
+        upper.append(jnp.where(lane >= LANES - width, after, down[k]))
+    return lower, upper
+
+
+def z_pair(chunk):
+    rows = chunk.shape[0]
+    row = row_iota(chunk.shape)
+    lower = jnp.where(row > 0, turn(chunk, 1, 0), 0.0)
+    upper = jnp.where(row < rows - 1, turn(chunk, -1, 0), 0.0)
+    return lower, upper
+
+
+def fine_beside(chunks):
+    lower, upper = y_pair(chunks, 16)
+    in_x = [beside_x(chunk, 16) for chunk in chunks]
+    in_y = [a + b for a, b in zip(lower, upper)]
+    in_z = []
+    for chunk in chunks:
+        below, above = z_pair(chunk)
+        in_z.append(below + above)
+    return in_x, in_y, in_z
+
+
+def coarse_x_pair(columns, index, half):
+    chunk = columns[index][half]
+    cell = lane_iota(chunk.shape) % 8
+    low = turn(chunk, 1, 1)
+    high = turn(chunk, -1, 1)
+    if index > 0:
+        low = jnp.where(cell == 0, turn(columns[index - 1][half], -7, 1), low)
+    else:
+        low = jnp.where(cell == 0, 0.0, low)
+    if index + 1 < len(columns):
+        high = jnp.where(cell == 7, turn(columns[index + 1][half], 7, 1), high)
+    else:
+        high = jnp.where(cell == 7, 0.0, high)
+    return low, high
+
+
+def coarse_beside(columns):
+    result = []
+    for index in range(len(columns)):
+        lower, upper = y_pair(columns[index], 8)
+        halves = []
+        for half in range(len(columns[index])):
+            chunk = columns[index][half]
+            low, high = coarse_x_pair(columns, index, half)
+            total = low + high + lower[half] + upper[half]
+            total = total + turn(chunk, 1, 0) + turn(chunk, -1, 0)
+            halves.append(total)
+        result.append(halves)
+    return result
+
+
+def count_true(condition):
+    return jnp.sum(jnp.where(condition, 1.0, 0.0))
+
+
+def list_check(sub_count, blk_count, blocks, leaf_ref, parent_ref, cell_ref, sub_here, blk_here):
+    wide_y = blocks // 2
+    side_y = wide_y // 2
+    side_x = sub_count // 2
+    parents = cell_ref.shape[0]
+    side_yx = side_y * side_x
+    layer = wide_y * sub_count
+    children = cell_ref[:, 0:8]
+    octant = lane_iota((parents, 8))
+    place = jnp.broadcast_to(cell_ref[:, 8:9], (parents, 8))
+    cell_z = 2 * lax.div(place, side_yx) + lax.div(octant, 4)
+    cell_y = 2 * lax.rem(lax.div(place, side_x), side_y) + lax.rem(lax.div(octant, 2), 2)
+    cell_x = 2 * lax.rem(place, side_x) + lax.rem(octant, 2)
+    code = (cell_z * wide_y + cell_y) * sub_count + cell_x
+    wrong = count_true(lax.div(children, blocks) != lax.div(cell_z, 2) * sub_count + cell_x)
+    width = 6 * blocks
+    listed = leaf_ref[...]
+    lane = lane_iota((1, width))
+    own = (blk_here * sub_count + sub_here) * blocks + lax.rem(lane, blocks)
+    found = jnp.zeros((parents, width), jnp.int32)
+    found_own = jnp.zeros((parents, width), jnp.int32)
+    for o in range(8):
+        child = children[:, o : o + 1]
+        value = code[:, o : o + 1]
+        found = jnp.where(child == listed, value, found)
+        found_own = jnp.where(child == own, value, found_own)
+    found = jnp.sum(found.astype(jnp.float32), axis=0, keepdims=True).astype(jnp.int32)
+    found_own = jnp.sum(found_own.astype(jnp.float32), axis=0, keepdims=True).astype(jnp.int32)
+    own_z = lax.div(found_own, layer)
+    own_y = lax.rem(lax.div(found_own, sub_count), wide_y)
+    own_x = lax.rem(found_own, sub_count)
+    face = lax.div(lane, blocks)
+
+    def by_axis(first, second, third):
+        return jnp.where(face < 2, first, jnp.where(face < 4, second, third))
+
+    sign = 2 * lax.rem(face, 2) - 1
+    goal = by_axis(own_x, own_y, own_z) + sign
+    exists = (goal >= 0) & (goal < by_axis(sub_count, wide_y, 2 * blk_count))
+    wanted = found_own + sign * by_axis(1, sub_count, layer)
+    wrong = wrong + jnp.sum(
+        jnp.where(
+            exists,
+            jnp.where((listed >= 0) & (found == wanted), 0.0, 1.0),
+            jnp.where(listed < 0, 0.0, 1.0),
+        )
+    )
+    position = lax.rem(own_z, 2) * wide_y + own_y
+    listed = parent_ref[0:1, :]
+    place = parent_ref[1:2, :]
+    shape = (parents, 6 * parents)
+    hit = row_iota(shape) == listed
+    found = jnp.sum(
+        jnp.where(hit, cell_ref[:, 8:9].astype(jnp.float32), 0.0), axis=0, keepdims=True
+    ).astype(jnp.int32)
+    face = lax.div(lane_iota((1, 6 * parents)), parents)
+    sign = 2 * lax.rem(face, 2) - 1
+    goal = sign + by_axis(
+        lax.rem(place, side_x), lax.rem(lax.div(place, side_x), side_y), lax.div(place, side_yx)
+    )
+    exists = (goal >= 0) & (goal < by_axis(side_x, side_y, blk_count))
+    wanted = place + sign * by_axis(1, side_x, side_yx)
+    wrong = wrong + jnp.sum(
+        jnp.where(
+            exists,
+            jnp.where((listed >= 0) & (found == wanted), 0.0, 1.0),
+            jnp.where(listed < 0, 0.0, 1.0),
+        )
+    )
+    return position, jnp.where(wrong == 0.0, 1.0, 0.0)
+
+
+def limits(sub_count, blk_count):
+    sub_here = lax.axis_index("sub")
+    blk_here = lax.axis_index("blk")
+
+    def gain(condition):
+        return jnp.where(condition, 1.0, 0.0).astype(jnp.float32)
+
+    return (
+        sub_here,
+        blk_here,
+        gain(sub_here > 0),
+        gain(sub_here < sub_count - 1),
+        gain(blk_here > 0),
+        gain(blk_here < blk_count - 1),
+    )
+
+
+def push_kernel(
+    sub_count, blk_count, blk_bits, leaf_ref, parent_ref, cell_ref, rhs_ref,
+    position_ref, own_ref, own_part_ref, faces_ref, *rest
+):
+    msg_refs = rest[:blk_bits]
+    placed, rows_s, rows_g, left_a, left_c, coarse_s = rest[blk_bits:]
+    blocks = rhs_ref.shape[0]
+    wide_y = blocks // 2
+    chunk_count = 2 * wide_y
+    f = FACTOR
+    f2 = f * f
+    sub_here, blk_here, x_low, x_high, z_low, z_high = limits(sub_count, blk_count)
+    position, good = list_check(
+        sub_count, blk_count, blocks, leaf_ref, parent_ref, cell_ref, sub_here, blk_here
+    )
+    for slot in range(blocks):
+        at = jnp.clip(position[0, slot], 0, blocks - 1)
+        position_ref[slot] = at
+        placed[at] = rhs_ref[slot]
+    s = []
+    for k in range(chunk_count):
+        lanes = slice(LANES * (k % 2), LANES * (k % 2) + LANES)
+        s.append(
+            jnp.concatenate([placed[k // 2, :, lanes], placed[wide_y + k // 2, :, lanes]], axis=0)
+        )
+    shape = s[0].shape
+    cell = lane_iota(shape) % 16
+    row = row_iota(shape)
+    top = shape[0] - 1
+    back = (
+        jnp.where(cell == 0, x_low, 0.0)
+        + jnp.where(cell == 15, x_high, 0.0)
+        + jnp.where(row == 0, z_low, 0.0)
+        + jnp.where(row == top, z_high, 0.0)
+    ) * f2
+    sx, sy, sz = fine_beside(s)
+    w = [SELF * a + f * (x + y + z) for a, x, y, z in zip(s, sx, sy, sz)]
+    wx, wy, wz = fine_beside(w)
+    for k in range(chunk_count):
+        half = slice(LANES * (k % 2), LANES * (k % 2) + LANES)
+        r = SELF * w[k] + f * (wx[k] + wy[k] + wz[k]) + back * s[k]
+        part = f * (s[k] + w[k] + r)
+        own_part_ref[k // 2, :, half] = part[:16]
+        own_part_ref[wide_y + k // 2, :, half] = part[16:]
+        rows_s[k] = r
+        base = (SELF * f + f2) * s[k] + f * w[k]
+        gx = base + f2 * (sy[k] + sz[k])
+        rows_g[k] = gx
+        gz = base + f2 * (sx[k] + sy[k])
+        line = 48 * (k // 2)
+        left_a[line + 16 : line + 17, half] = gz[0:1]
+        left_a[line + 17 : line + 18, half] = gz[top : top + 1]
+        left_a[line + 40 : line + 41, half] = (2.0 * f2) * s[k][0:1]
+        left_a[line + 41 : line + 42, half] = (2.0 * f2) * s[k][top : top + 1]
+        line_c = 64 * (k // 2)
+        left_c[line_c : line_c + 32, half] = gx + (f - f2) * s[k]
+        left_c[line_c + 32 : line_c + 64, half] = s[k]
+        edge = gz + (f - f2) * s[k]
+        for bit in range(blk_bits):
+            upward = (blk_here // (1 << bit)) % 2 == 0
+            msg_refs[bit][16 + k // 2 : 17 + k // 2, half] = jnp.where(
+                upward, edge[top : top + 1], edge[0:1]
+            )
+            msg_refs[bit][16 + wide_y + k // 2 : 17 + wide_y + k // 2, half] = jnp.where(
+                upward, s[k][top : top + 1], s[k][0:1]
+            )
+    for k in range(chunk_count):
+        half = slice(LANES * (k % 2), LANES * (k % 2) + LANES)
+        line = 48 * (k // 2)
+        left_a[line : line + 16, half] = (
+            rows_s[k, pl.ds(0, 16, stride=2), :] + rows_s[k, pl.ds(1, 16, stride=2), :]
+        )
+        left_a[line + 24 : line + 40, half] = (
+            rows_g[k, pl.ds(0, 16, stride=2), :] + rows_g[k, pl.ds(1, 16, stride=2), :]
+        )
+    key = row_iota((256, LANES))
+    col = lane_iota((256, LANES))
+    key_y = key // 16
+    key_x = key % 16
+    col_y = (col % 64) // 8
+    col_x = col % 8
+    same_y = key_y // 2 == col_y
+    table_a = zero_one(
+        same_y
+        & (
+            ((col < 64) & (key_x // 2 == col_x))
+            | ((col >= 64) & (col_x == 7) & (key_x == 0))
+            | ((col >= 64) & (col_x == 0) & (key_x == 15))
+        ),
+        0.5,
+    )
+    out_a = split_dot(left_a[...], table_a)
+    table_c = zero_one(
+        (key_y == col % 64) & (((col < 64) & (key_x == 0)) | ((col >= 64) & (key_x == 15)))
+    )
+    out_c = split_dot(left_c[...], table_c)
+    faces = out_c[0:64]
+    for yy in range(1, wide_y):
+        faces = faces + turn(out_c[64 * yy : 64 * yy + 64], 16 * yy, 1)
+    faces_ref[...] = faces
+    lane24 = lane_iota((24, LANES))
+    main = []
+    side = []
+    for half in range(2):
+        first = out_a[96 * half : 96 * half + 24]
+        second = out_a[96 * half + 48 : 96 * half + 72]
+        main.append(jnp.where(lane24 < 64, first, turn(second, 64, 1)))
+        first = out_a[96 * half + 24 : 96 * half + 48]
+        second = out_a[96 * half + 72 : 96 * half + 96]
+        side.append(jnp.where(lane24 < 64, turn(first, 64, 1), second))
+    own_ref[...] = jnp.zeros(own_ref.shape, jnp.float32)
+    for half in range(2):
+        lanes = slice(LANES * half, LANES * half + LANES)
+        for base_row, piece in ((0, main[half]), (24, side[half])):
+            own_ref[base_row + 4 : base_row + 20, lanes] = piece[0:16]
+            own_ref[base_row + 3 : base_row + 4, lanes] = piece[16:17] * z_low
+            own_ref[base_row + 20 : base_row + 21, lanes] = piece[17:18] * z_high
+    own_ref[56:64, :] = jnp.zeros((8, 256), jnp.float32) + good
+    cell8 = lane24 % 8
+    row24 = row_iota((24, LANES))
+    inside_z = jnp.where(row24 < 4, z_low, jnp.where(row24 >= 20, z_high, 1.0))
+    gain = [inside_z * x_low, inside_z, inside_z * x_high]
+    main24 = [own_ref[0:24, 0:LANES], own_ref[0:24, LANES:256]]
+    side24 = [own_ref[24:48, 0:LANES], own_ref[24:48, LANES:256]]
+    columns = [
+        [jnp.where(cell8 == 7, piece, 0.0) * x_low for piece in side24],
+        main24,
+        [jnp.where(cell8 == 0, piece, 0.0) * x_high for piece in side24],
+    ]
+    near = coarse_beside(columns)
+    wp = [
+        [gain[b] * (SELF * columns[b][h] + f * near[b][h]) for h in range(2)] for b in range(3)
+    ]
+    near = coarse_beside(wp)
+    for b in range(3):
+        for h in range(2):
+            coarse_s[2 * b + h, 0:24] = gain[b] * (SELF * wp[b][h] + f * near[b][h])
+            coarse_s[2 * b + h, 24:32] = jnp.zeros((8, LANES), jnp.float32)
+    pieces = []
+    for k in range(6):
+        pieces.append(
+            coarse_s[k, pl.ds(0, 8, stride=4), :]
+            + coarse_s[k, pl.ds(1, 8, stride=4), :]
+            + coarse_s[k, pl.ds(2, 8, stride=4), :]
+            + coarse_s[k, pl.ds(3, 8, stride=4), :]
+        )
+    root_left = jnp.concatenate(pieces, axis=1)
+    root_lanes = 16 * sub_count
+    key = row_iota((6 * LANES, root_lanes))
+    col = lane_iota((6 * LANES, root_lanes))
+    target = (
+        ((key // LANES) % 2 * 4 + key % LANES // 32) * (2 * sub_count)
+        + 2 * (sub_here + key // 256 - 1)
+        + key % 8 // 4
+    )
+    root_part = split_dot(root_left, zero_one(col == target, 0.25))
+    own_ref[48:56, 0:root_lanes] = root_part
+    for bit in range(blk_bits):
+        upward = (blk_here // (1 << bit)) % 2 == 0
+        ref = msg_refs[bit]
+        ref[8:16, :] = own_ref[48:56, :]
+        ref[24:32, :] = jnp.zeros((8, 256), jnp.float32) + good
+        ref[24:25, 0:LANES] = jnp.where(upward, faces[63:64], faces[32:33])
+        for base_row, source in ((0, 0), (4, 24)):
+            ref[base_row : base_row + 4, :] = jnp.where(
+                upward, own_ref[source + 17 : source + 21, :], own_ref[source + 3 : source + 7, :]
+            )
+
+
+def neighbour_pick(blk_here, blk_count, msg_refs):
+    spans = []
+    step = 1
+    while step < blk_count:
+        spans.append(step)
+        step = 2 * step + 1
+
+    def picker(other):
+        choices = [(blk_here ^ other) == d for d in spans]
+
+        def read(rows, lanes):
+            value = msg_refs[spans[-1] - 1][rows, lanes]
+            for choice, d in zip(choices[:-1], spans[:-1]):
+                value = jnp.where(choice, msg_refs[d - 1][rows, lanes], value)
+            return value
+
+        return read
+
+    return picker(blk_here - 1), picker(blk_here + 1)
+
+
+def root_tiles(sub_count, blk_count):
+    return (sub_count * blk_count // 16 + 1) // 2
+
+
+def join_kernel(sub_count, blk_count, own_ref, faces_ref, *rest):
+    msg_refs = rest[: blk_count - 1]
+    out_ref, root_s = rest[blk_count - 1 :]
+    _, blk_here, _, _, z_low, z_high = limits(sub_count, blk_count)
+    below, above = neighbour_pick(blk_here, blk_count, msg_refs)
+    row8 = row_iota((8, LANES))
+    low_rows = (row8 >= 1) & (row8 < 5)
+    high_rows = (row8 >= 3) & (row8 < 7)
+    for half in range(2):
+        lanes = slice(LANES * half, LANES * half + LANES)
+        low = below(slice(0, 8), lanes) * z_low
+        high = above(slice(0, 8), lanes) * z_high
+        for base, low_turn, high_turn in ((0, 1, 3), (24, 5, 7)):
+            out_ref[base : base + 8, lanes] = own_ref[base : base + 8, lanes] + jnp.where(
+                low_rows, turn(low, low_turn, 0), 0.0
+            )
+            out_ref[base + 8 : base + 16, lanes] = own_ref[base + 8 : base + 16, lanes]
+            out_ref[base + 16 : base + 24, lanes] = own_ref[
+                base + 16 : base + 24, lanes
+            ] + jnp.where(high_rows, turn(high, high_turn, 0), 0.0)
+    root_s[...] = jnp.zeros(root_s.shape, jnp.float32)
+    good = own_ref[56:64, 0:LANES]
+    for d in range(blk_count):
+        start = 4 * (blk_here ^ d) + 3
+        for part in range(root_s.shape[0]):
+            lanes = slice(LANES * part, LANES * part + LANES)
+            value = own_ref[48:56, lanes] if d == 0 else msg_refs[d - 1][8:16, lanes]
+            root_s[part, pl.ds(start, 8), :] = root_s[part, pl.ds(start, 8), :] + value
+        if d > 0:
+            good = jnp.minimum(good, msg_refs[d - 1][24:32, LANES:256])
+    tile = 0
+    for start in range(0, 4 * blk_count, 8):
+        for part in range(root_s.shape[0]):
+            row = 48 + 8 * (tile // 2)
+            lanes = slice(LANES * (tile % 2), LANES * (tile % 2) + LANES)
+            out_ref[row : row + 8, lanes] = root_s[part, 4 + start : 12 + start]
+            tile += 1
+    row = 48 + 8 * root_tiles(sub_count, blk_count)
+    low = below(slice(24, 32), slice(0, LANES)) * z_low
+    high = above(slice(24, 32), slice(0, LANES)) * z_high
+    out_ref[row : row + 8, 0:LANES] = jnp.where(row8 == 0, low, turn(high, 1, 0))
+    out_ref[row : row + 8, LANES:256] = good
+    out_ref[row + 8 : row + 40, 0:LANES] = faces_ref[0:32]
+    out_ref[row + 8 : row + 40, LANES:256] = faces_ref[32:64]
+
+
+def owned_slots(sub_count, blk_count, slots, sub_here, blk_here, owner_ref, cell_ref):
+    parents = owner_ref.shape[1]
+    parent_len = parents // blk_count
+    side_y = parent_len // (sub_count // 2)
+    side_x = sub_count // 2
+    owners = owner_ref[0:1, :]
+    places = owner_ref[1:2, :]
+    number = lane_iota((1, parents))
+    shape = (parents, parents)
+    in_range = lax.div(number, parent_len) == blk_here
+    mine = in_range & (owners == sub_here)
+    column = cell_ref[:, 9:10]
+    row = row_iota((parents, 1))
+    column_mine = (column == sub_here) & (lax.div(row, parent_len) == blk_here)
+    rank = jnp.sum(
+        jnp.where(column_mine & (row_iota(shape) < lane_iota(shape)), 1.0, 0.0),
+        axis=0,
+        keepdims=True,
+    )
+    found = []
+    for k in range(slots):
+        chosen = jnp.where(mine & (rank == float(k)), 1.0, 0.0)
+        place = jnp.sum(chosen * places.astype(jnp.float32)).astype(jnp.int32)
+        found.append(
+            (lax.rem(lax.div(place, side_x), side_y), lax.rem(place, side_x), jnp.sum(chosen))
+        )
+    return found
+
+
+def solve_kernel(
+    sub_count, blk_count, slots, positions, owner_ref, cell_ref, all_ref, part_ref, *rest
+):
+    msg_refs = rest[: blk_count - 1]
+    leaf_ref, parent_ref = rest[blk_count - 1 : blk_count + 1]
+    placed, par_s, root_s, fine_s, push_s = rest[blk_count + 1 :]
+    blocks = part_ref.shape[0]
+    wide_y = blocks // 2
+    f = FACTOR
+    f2 = f * f
+    sub_here, blk_here, x_low, x_high, z_low, z_high = limits(sub_count, blk_count)
+    below, above = neighbour_pick(blk_here, blk_count, msg_refs)
+    owned = owned_slots(sub_count, blk_count, slots, sub_here, blk_here, owner_ref, cell_ref)
+    row8 = row_iota((8, LANES))
+    cell24 = lax.rem(lane_iota((24, LANES)), 8)
+    row24 = row_iota((24, LANES))
+    source = []
+    for c in range(sub_count):
+        halves = []
+        for half in range(2):
+            lanes = slice(LANES * half, LANES * half + LANES)
+            value = all_ref[c, 0:24, lanes]
+            if c + 1 < sub_count:
+                value = value + jnp.where(cell24 == 7, all_ref[c + 1, 24:48, lanes], 0.0)
+            if c > 0:
+                value = value + jnp.where(cell24 == 0, all_ref[c - 1, 24:48, lanes], 0.0)
+            halves.append(value)
+        source.append(halves)
+
+    root_lanes = 16 * sub_count
+    row_len = 2 * sub_count
+    root_rows = 4 * blk_count
+    parts = root_lanes // LANES
+    tile_rows = []
+    tile = 0
+    for _ in range(0, root_rows, 8):
+        pieces = []
+        for part in range(parts):
+            row = 48 + 8 * (tile // 2)
+            lanes = slice(LANES * (tile % 2), LANES * (tile % 2) + LANES)
+            total = all_ref[0, row : row + 8, lanes]
+            for c in range(1, sub_count):
+                total = total + all_ref[c, row : row + 8, lanes]
+            pieces.append(total)
+            tile += 1
+        tile_rows.append(jnp.concatenate(pieces, axis=1))
+    root_source = jnp.concatenate(tile_rows, axis=0)
+    root_source = root_source - jnp.sum(root_source) / (root_rows * root_lanes)
+    shape = root_source.shape
+    lane = lane_iota(shape)
+    row = row_iota(shape)
+    values = f * root_source
+    for _ in range(ROOT_SWEEPS - 1):
+        total = jnp.where(lane % row_len > 0, turn(values, 1, 1), 0.0)
+        total = total + jnp.where(lane % row_len < row_len - 1, turn(values, -1, 1), 0.0)
+        total = total + jnp.where(lane >= row_len, turn(values, row_len, 1), 0.0)
+        total = total + jnp.where(lane < root_lanes - row_len, turn(values, -row_len, 1), 0.0)
+        total = total + jnp.where(row > 0, turn(values, 1, 0), 0.0)
+        total = total + jnp.where(row < root_rows - 1, turn(values, -1, 0), 0.0)
+        values = SELF * values + f * (root_source + total)
+    root_s[...] = jnp.zeros(root_s.shape, jnp.float32)
+    for part in range(parts):
+        root_s[part, 4 : 4 + root_rows] = values[:, LANES * part : LANES * part + LANES]
+    mine = jnp.concatenate(
+        [root_s[part, pl.ds(4 * blk_here + 3, 8), :] for part in range(parts)], axis=1
+    )
+    left = jnp.concatenate([turn(mine, -2 * c, 1) for c in range(sub_count)], axis=0)
+    key = row_iota((root_lanes, 256))
+    col = lane_iota((root_lanes, 256))
+    wide = split_dot(left, zero_one(key == (col // 32) * row_len + col % 8 // 4))
+
+    valid = (
+        (row24 >= 2)
+        & (row24 < 22)
+        & ((row24 >= 4) | (z_low > 0.0))
+        & ((row24 < 20) | (z_high > 0.0))
+    )
+    near = coarse_beside(source)
+    three = []
+    for c in range(sub_count):
+        halves = []
+        for half in range(2):
+            lanes = slice(LANES * half, LANES * half + LANES)
+            wp = SELF * source[c][half] + f * near[c][half]
+            tiles = []
+            for t in range(3):
+                first = wide[8 * c + 2 * t : 8 * c + 2 * t + 1, lanes]
+                second = wide[8 * c + 2 * t + 1 : 8 * c + 2 * t + 2, lanes]
+                tiles.append(
+                    jnp.where(
+                        row8 < 4,
+                        jnp.broadcast_to(first, (8, LANES)),
+                        jnp.broadcast_to(second, (8, LANES)),
+                    )
+                )
+            value = f * (source[c][half] + wp) + jnp.concatenate(tiles, axis=0)
+            halves.append(jnp.where(valid, value, 0.0))
+        three.append(halves)
+    near = coarse_beside(three)
+    for c in range(sub_count):
+        for half in range(2):
+            value = SELF * three[c][half] + f * (near[c][half] + source[c][half])
+            par_s[c, half] = jnp.where(valid, value, 0.0)
+
+    pieces = []
+    for k in range(slots):
+        half, place_x, filled = owned[k]
+        pieces.append(
+            jnp.concatenate(
+                [par_s[2 * place_x, half, 4:20], par_s[2 * place_x + 1, half, 4:20]], axis=1
+            )
+            * filled
+        )
+    left = jnp.concatenate(pieces, axis=0)
+    key = row_iota((256, 256))
+    col = lane_iota((256, 256))
+    table = zero_one(key == (col % 16 // 8) * 128 + (col // 16) * 8 + col % 8)
+    moved = split_dot(left, table)
+    for k in range(slots):
+        parent_ref[k] = moved[16 * k : 16 * k + 16]
+
+    before = jnp.maximum(sub_here - 1, 0)
+    after = jnp.minimum(sub_here + 1, sub_count - 1)
+    columns = [
+        [par_s[before, half] * x_low for half in range(2)],
+        [par_s[sub_here, half] for half in range(2)],
+        [par_s[after, half] * x_high for half in range(2)],
+    ]
+    centre = columns[1]
+    in_y = y_pair(centre, 8)
+    lane16 = lane_iota((16, LANES))
+    left_rows = []
+    in_x = [coarse_x_pair(columns, 1, half) for half in range(2)]
+    blend = {}
+    for half in range(2):
+        for zp in range(2):
+            base = (SELF + 3.0 * f) * centre[half] + f * turn(centre[half], 1 - 2 * zp, 0)
+            for yp in range(2):
+                for xp in range(2):
+                    value = base + f * (in_y[yp][half] + in_x[half][xp])
+                    blend[half, zp, 2 * yp + xp] = value[4:20]
+    for yy in range(wide_y):
+        half = yy // 2
+        for zp in range(2):
+            pair = []
+            for v in (0, 2):
+                first = blend[half, zp, v]
+                second = blend[half, zp, v + 1]
+                if yy % 2 == 0:
+                    second = turn(second, 64, 1)
+                else:
+                    first = turn(first, 64, 1)
+                pair.append(jnp.where(lane16 < 64, first, second))
+            left_rows.append(jnp.concatenate(pair, axis=1))
+    left = jnp.concatenate(left_rows, axis=0)
+    key = row_iota((256, 256))
+    col = lane_iota((256, 256))
+    col_y = col // 16
+    col_x = col % 16
+    target = (col_y % 2 * 2 + col_x % 2) * 64 + col_y // 2 * 8 + col_x // 2
+    spread = split_dot(left, zero_one(key == target))
+    for yy in range(wide_y):
+        for zp in range(2):
+            line = 16 * (2 * yy + zp)
+            fine_s[2 * yy, pl.ds(zp, 16, stride=2), :] = spread[line : line + 16, 0:128]
+            fine_s[2 * yy + 1, pl.ds(zp, 16, stride=2), :] = spread[line : line + 16, 128:256]
+
+    line = 48 + 8 * root_tiles(sub_count, blk_count)
+    lane64 = lane_iota((32, LANES))
+    row32 = row_iota((32, LANES))
+    from_low = all_ref[before, line + 8 : line + 40, 0:LANES] * x_low
+    low_values = all_ref[before, line + 8 : line + 40, LANES:256] * x_low
+    from_high = all_ref[after, line + 8 : line + 40, 0:LANES] * x_high
+    high_values = all_ref[after, line + 8 : line + 40, LANES:256] * x_high
+    low_line = all_ref[before, line : line + 8, 0:LANES] * (2.0 * f2 * x_low)
+    high_line = all_ref[after, line : line + 8, 0:LANES] * (2.0 * f2 * x_high)
+    low_line = [jnp.broadcast_to(low_line[k : k + 1], (32, LANES)) for k in range(2)]
+    high_line = [jnp.broadcast_to(high_line[k : k + 1], (32, LANES)) for k in range(2)]
+    edge_low = (
+        from_low
+        + jnp.where(row32 == 0, low_line[0], 0.0)
+        + jnp.where(row32 == 31, low_line[1], 0.0)
+    )
+    edge_high = (
+        from_high
+        + jnp.where(row32 == 0, high_line[0], 0.0)
+        + jnp.where(row32 == 31, high_line[1], 0.0)
+    )
+    left = jnp.concatenate(
+        [
+            jnp.where(lane64 < 64, turn(edge_low, 64, 1), f2 * low_values),
+            jnp.where(lane64 < 64, edge_high, f2 * turn(high_values, 64, 1)),
+        ],
+        axis=1,
+    )
+    fine_lanes = 256 * wide_y
+    key = row_iota((256, fine_lanes))
+    col = lane_iota((256, fine_lanes))
+    kind = key // 64
+    kind_x = jnp.where(kind == 0, 0, jnp.where(kind == 1, 1, jnp.where(kind == 2, 15, 14)))
+    push = split_dot(left, zero_one((key % 64 == col // 16) & (col % 16 == kind_x)))
+    push_s[...] = push
+    own_low = below(slice(16, 24), slice(0, 256)) * z_low
+    own_high = above(slice(16, 24), slice(0, 256)) * z_high
+    for yy in range(wide_y):
+        lanes = slice(256 * yy, 256 * yy + 256)
+        push_s[0:1, lanes] = push_s[0:1, lanes] + own_low[yy : yy + 1]
+        push_s[1:2, lanes] = push_s[1:2, lanes] + f2 * own_low[wide_y + yy : wide_y + yy + 1]
+        push_s[31:32, lanes] = push_s[31:32, lanes] + own_high[yy : yy + 1]
+        push_s[30:31, lanes] = push_s[30:31, lanes] + f2 * own_high[wide_y + yy : wide_y + yy + 1]
+    for zz in range(2):
+        for yy in range(wide_y):
+            rows = slice(16 * zz, 16 * zz + 16)
+            lanes = slice(256 * yy, 256 * yy + 256)
+            index = zz * wide_y + yy
+            fine = jnp.concatenate([fine_s[2 * yy, rows], fine_s[2 * yy + 1, rows]], axis=1)
+            placed[index] = part_ref[index] + fine + f * push_s[rows, lanes]
+    for slot in range(blocks):
+        leaf_ref[slot] = placed[positions[slot]]
+
+
+def paired(count, step):
+    return [(i, i ^ step) for i in range(count)]
+
+
+def local(rhs, leaf_neighbors, parent_neighbors, children, owners, parent_places):
+    blk_count = lax.axis_size("blk")
+    sub_count = lax.axis_size("sub")
+    blocks = rhs.shape[0]
+    wide_y = blocks // 2
+    blk_bits = blk_count.bit_length() - 1
+    f32 = jnp.float32
+    vmem = pl.BlockSpec(memory_space=pltpu.VMEM)
+    smem = pl.BlockSpec(memory_space=pltpu.SMEM)
+    leaf_row = leaf_neighbors.T.reshape(1, -1)
+    parent_rows = jnp.stack([parent_neighbors.T.reshape(-1), jnp.tile(parent_places, 6)])
+    owner_rows = jnp.stack([owners, parent_places])
+    cells = jnp.concatenate([children, parent_places[:, None], owners[:, None]], axis=1)
+    outs = pl.pallas_call(
+        functools.partial(push_kernel, sub_count, blk_count, blk_bits),
+        name="push",
+        out_shape=[
+            jax.ShapeDtypeStruct((blocks,), jnp.int32),
+            jax.ShapeDtypeStruct((OWN_ROWS, 256), f32),
+            jax.ShapeDtypeStruct((blocks, 16, 256), f32),
+            jax.ShapeDtypeStruct((64, LANES), f32),
+        ]
+        + [jax.ShapeDtypeStruct((MSG_ROWS, 256), f32)] * blk_bits,
+        in_specs=[vmem] * 4,
+        out_specs=[smem] + [vmem] * (3 + blk_bits),
+        scratch_shapes=[
+            pltpu.VMEM((blocks, 16, 256), f32),
+            pltpu.VMEM((2 * wide_y, 32, LANES), f32),
+            pltpu.VMEM((2 * wide_y, 32, LANES), f32),
+            pltpu.VMEM((48 * wide_y, 256), f32),
+            pltpu.VMEM((64 * wide_y, 256), f32),
+            pltpu.VMEM((6, 32, LANES), f32),
+        ],
+    )(leaf_row, parent_rows, cells, rhs)
+    positions, own, own_part, faces = outs[:4]
+    messages = outs[4:]
+    received = [
+        lax.ppermute(messages[d.bit_length() - 1], "blk", paired(blk_count, d))
+        for d in range(1, blk_count)
+    ]
+    root_parts = 16 * sub_count // LANES
+    joined_rows = 48 + 8 * root_tiles(sub_count, blk_count) + 8 + 32
+    joined = pl.pallas_call(
+        functools.partial(join_kernel, sub_count, blk_count),
+        name="join",
+        out_shape=jax.ShapeDtypeStruct((joined_rows, 256), f32),
+        in_specs=[vmem] * (1 + blk_count),
+        out_specs=vmem,
+        scratch_shapes=[pltpu.VMEM((root_parts, 4 * blk_count + 8, LANES), f32)],
+    )(own, faces, *received)
+    gathered = lax.all_gather(joined, "sub", axis=0, tiled=False)
+    good = jnp.min(gathered[:, joined_rows - 40, LANES])
+
+    def fast():
+        return tuple(
+            pl.pallas_call(
+                functools.partial(solve_kernel, sub_count, blk_count, PMOST),
+                name="solve",
+                out_shape=[
+                    jax.ShapeDtypeStruct((blocks, 16, 256), f32),
+                    jax.ShapeDtypeStruct((PMOST, 16, 256), f32),
+                ],
+                in_specs=[smem] + [vmem] * (4 + blk_count - 1),
+                out_specs=[vmem] * 2,
+                scratch_shapes=[
+                    pltpu.VMEM((blocks, 16, 256), f32),
+                    pltpu.VMEM((sub_count, 2, 24, LANES), f32),
+                    pltpu.VMEM((root_parts, 4 * blk_count + 8, LANES), f32),
+                    pltpu.VMEM((2 * wide_y, 32, LANES), f32),
+                    pltpu.VMEM((32, 256 * wide_y), f32),
+                ],
+            )(positions, owner_rows, cells, gathered, own_part, *received)
+        )
+
+    def general():
+        return general_local(
+            rhs, leaf_neighbors, parent_neighbors, children, owners, parent_places
+        )
+
+    return lax.cond(good > 0.5, fast, general)
+
+
 def solution(mesh):
     in_specs = (P(("blk", "sub"), None, None), P(("blk", "sub"), None), P(), P(), P(), P())
     out_specs = (P(("blk", "sub"), None, None), P(("blk", "sub"), None, None))

time: 121 us -> 36.9 us (0.30)
  starting transfers between devices: 46.1 us -> 5.71 us
  local copies, waits for them, and re-layouts: 25.5 us -> 5.89 us
  blocking collectives: 28.6 us -> 10.7 us
  Pallas kernels: 0 us -> 7.62 us
  matrix products: 4.6 us -> 0 us
  waiting for transfers between devices: 7.32 us -> 3.66 us
  other arithmetic: 4.81 us -> 1.29 us
  between operations: 2.81 us -> 1.35 us
    ppermute x18 -> x3, starting transfers between devices: 46.1 us -> 5.71 us  [local(): lax.ppermute(messages[d.bit_length() - 1], 'blk', paired(blk_count, d))]
    all_gather x2 -> x1, blocking collectives: 28.6 us -> 10.7 us  [local(): gathered = lax.all_gather(joined, 'sub', axis=0, tiled=False)]
    pallas_call x0 -> x3, Pallas kernels: none -> 7.62 us  [the longest x1 3.07 us: fast(): pl.pallas_call(functools.partial(solve_kernel, sub_count, blk_count, PMOS...]
    gather x12 -> x0, local copies, waits for them, and re-layouts: 6.74 us -> none  [the longest x6 3.77 us: lookup(): jnp.take(face_table, rows_index.reshape(-1), axis=0).reshape(blocks, 6, 256)]
    slice x33 -> x0, local copies, waits for them, and re-layouts: 5.28 us -> none  [the longest x6 2.06 us: block_faces(): values[:, :, 15::16].reshape(blocks, 256)]
    dot_general x18 -> x0, matrix products: 4.6 us -> none  [exact_dot(): jnp.einsum('...k,kl->...l', left, table, precision=lax.Precision.HIGHEST)]
    ppermute x18 -> x3, waiting for transfers between devices: 7.32 us -> 3.66 us  [local(): lax.ppermute(messages[d.bit_length() - 1], 'blk', paired(blk_count, d))]
    another operation x65 -> x3, local copies, waits for them, and re-layouts: 5.09 us -> 1.5 us  [the longest x2 0.84 us: local(): jnp.stack([parent_neighbors.T.reshape(-1), jnp.tile(parent_places, 6)])]
  transfers between devices with their start and end apart: 18 -> 3, of which waited for: 4 -> 2; matrix products, arithmetic and copies ran while one was open for 7% -> 0% of each run, Pallas kernels for 0% -> 0%
where the time goes in v1:
time: 36.9 us; the launch traced here: 36.5 us
  blocking collectives  10.7 us (29%)
  Pallas kernels  7.62 us (21%)
  local copies, waits for them, and re-layouts  5.89 us (16%)
  starting transfers between devices  5.71 us (15%)
  waiting for transfers between devices  3.66 us (10%)
  between operations  1.35 us (4%)
  other arithmetic  1.29 us (3%)
    all_gather x1, blocking collectives, local(): gathered = lax.all_gather(joined, 'sub', axis=0, tiled=False)  10.7 us
    ppermute x3, starting transfers between devices, local(): lax.ppermute(messages[d.bit_length() - 1], 'blk', paired(blk_count, d))  5.71 us
    ppermute x3, waiting for transfers between devices, local(): lax.ppermute(messages[d.bit_length() - 1], 'blk', paired(blk_count, d))  3.66 us
    pallas_call x1, Pallas kernels, fast(): pl.pallas_call(functools.partial(solve_kernel, sub_count, blk_count, PMOS...  3.07 us
    pallas_call x1, Pallas kernels, local(): pl.pallas_call(functools.partial(push_kernel, sub_count, blk_count, blk_b...  3.03 us
    pallas_call x1, Pallas kernels, local(): pl.pallas_call(functools.partial(join_kernel, sub_count, blk_count), name...  1.52 us
    unnamed x13, local copies, waits for them, and re-layouts  1.48 us
    another operation x2, local copies, waits for them, and re-layouts, local(): jnp.stack([parent_neighbors.T.reshape(-1), jnp.tile(parent_places, 6)])  0.84 us
  transfers between devices with their start and end apart: 3, of which 2 were waited for; matrix products, arithmetic and copies ran while one was open for 0% of the time, Pallas kernels for 0%

profile of v1, /device:TPU:0, one launch (start us, length us, event | category | flops | bytes accessed | tf_op | source)
XLA Modules:
  0.0 36.5 jit_solution(1531491166759360479)
XLA Ops:
  0.6 0.8 %copy.73 = s32[32,8]{1,0:T(8,128)S(1)} copy(s32[32,8]{0,1:T(8,128)} %param.17) | data formatting | bytes 2048 | tf_op args[3]
  1.4 0.7 %copy.74 = s32[32,1]{1,0:T(8,128)S(1)} copy(s32[32,1]{0,1:T(1,128)} %bitcast.161) | data formatting | bytes 256 | tf_op jit(solution)/shard_map/broadcast_in_dim | solution.py:1055
  2.2 0.7 %copy.75 = s32[32,1]{1,0:T(8,128)S(1)} copy(s32[32,1]{0,1:T(1,128)} %bitcast.163) | data formatting | bytes 256 | tf_op jit(solution)/shard_map/broadcast_in_dim | solution.py:1055
  2.9 0.7 %tile.8 = s32[6,32]{1,0:T(8,128)S(1)} broadcast(s32[32]{0:T(128)} %param.19), dimensions={1} | broadcast | bytes 896 | tf_op jit(solution)/shard_map/tile | solution.py:1053
  3.6 0.1 stack_tile.3
  3.6 0.8 %stack_reshape.3 = s32[1,192]{1,0:T(1,128)S(1)} reshape(s32[6,32]{1,0:T(8,128)} %bitcast.159) | data formatting | bytes 1536 | tf_op jit(solution)/shard_map/stack;reshape | solution.py:1053
  4.4 0.8 %copy.72 = s32[6,8]{1,0:T(8,128)S(1)} copy(s32[6,8]{0,1:T(8,128)} %bitcast.160) | data formatting | bytes 384 | tf_op jit(solution)/shard_map/transpose | solution.py:1052
  5.2 0.7 %reshape.573.leaf_ref = s32[1,48]{1,0:T(1,128)} reshape(s32[6,8]{1,0:T(8,128)S(1)} %copy.72) | data formatting | bytes 384 | tf_op jit(solution)/shard_map/reshape | solution.py:1052
  5.8 0.6 %pad_add_fusion.1.parent_ref = s32[2,192]{1,0:T(2,128)} fusion(s32[1,192]{1,0:T(1,128)S(1)} %stack_tile.3, s32[1,192]{1,0:T(1,128)S(1)} %stack_reshape.3), kind=kLoop, calls=%fused_computation.476 | loop fusion | flops 384 | bytes 3072 | tf_op jit(solution)/shard_map/stack | solution.py:1053
  6.5 0.1 pad_add_fusion.cell_ref
  6.5 3.0 %push.1 = (s32[8]{0:T(128)S(1)}, f32[64,256]{1,0:T(8,128)}, f32[8,16,256]{2,1,0:T(8,128)S(1)}, f32[64,128]{1,0:T(8,128)}, f32[32,256]{1,0:T(8,128)}, /*index=5*/f32[32,256]{1,0:T(8,128)}) custom-call(s32[1,48]{1,0:T(1,128)} %reshape.573.leaf_ref, s32[2,192]{1,0:T(2,128)} %pad_add_fusion.1.parent_ref, s32[32,10]{1,0:T(8,128)S(1)} %pad_add_fusion.cell_ref, ...), custom_call_target="tpu_custom_call" | custom-call | tf_op jit(solution)/shard_map/push/pallas_call | solution.py:1056
  9.6 4.1 %collective-permute-start.19 = (f32[32,256]{1,0:T(8,128)}, f32[32,256]{1,0:T(8,128)S(1)}, u32[]{:S(2)}, u32[]{:S(2)}) collective-permute-start(f32[32,256]{1,0:T(8,128)} %get-tuple-element.61), channel_id=1, source_target_pairs={{0,16},{8,24},{16,0},{24,8},{1,17},{9,25},{17,1},{25,9},{2,18},{10... | collective-permute-start | bytes 98312 | tf_op jit(solution)/shard_map/ppermute | solution.py:1080
  13.7 1.3 %collective-permute-start.20 = (f32[32,256]{1,0:T(8,128)}, f32[32,256]{1,0:T(8,128)S(1)}, u32[]{:S(2)}, u32[]{:S(2)}) collective-permute-start(f32[32,256]{1,0:T(8,128)} %get-tuple-element.61), channel_id=1, source_target_pairs={{0,24},{8,16},{16,8},{24,0},{1,25},{9,17},{17,9},{25,1},{2,26},{10... | collective-permute-start | bytes 98312 | tf_op jit(solution)/shard_map/ppermute | solution.py:1080
  15.0 0.2 collective-permute-start.18
  15.3 0.7 %copy-done.4 = s32[32]{0:T(128)S(1)} copy-done((s32[32]{0:T(128)S(1)}, s32[32]{0:T(128)}, u32[]{:S(2)}) %copy-start.4) | copy-done | bytes 152
  15.9 0.0 copy-done.5
  16.0 0.2 collective-permute-done.19.rest_1_
  16.2 3.5 %collective-permute-done.20.rest_2_ = f32[32,256]{1,0:T(8,128)S(1)} collective-permute-done((f32[32,256]{1,0:T(8,128)}, f32[32,256]{1,0:T(8,128)S(1)}, u32[]{:S(2)}, u32[]{:S(2)}) %collective-permute-start.20) | collective-permute-done | bytes 32800 | tf_op jit(solution)/shard_map/ppermute | solution.py:1080
  19.6 0.0 collective-permute-done.18.rest_0_
  19.6 1.5 %join.1 = f32[96,256]{1,0:T(8,128)} custom-call(f32[64,256]{1,0:T(8,128)} %get-tuple-element.58.own_ref, f32[64,128]{1,0:T(8,128)} %get-tuple-element.59.faces_ref, f32[32,256]{1,0:T(8,128)S(1)} %collective-permute-done.18.rest_0_, f32[32,256]{1,0:T(8,128)S(1)} %collective-permute-done.19.rest_1_, f32[32,256]{1,0:T(8,128)S(1)} %collective-permute-done.20.rest_2_), custom_call_target="tpu_custom_call" | custom-call | tf_op jit(solution)/shard_map/join/pallas_call | solution.py:1085
  21.1 10.7 %all-gather = f32[768,256]{1,0:T(8,128)S(1)} all-gather(f32[96,256]{1,0:T(8,128)} %join.1), channel_id=2, replica_groups=mesh['blk'=4,'sub'=8] {'sub'}, dimensions={0}, use_global_device_ids=true | all-gather | bytes 884736 | tf_op jit(solution)/shard_map/all_gather | solution.py:1093
  31.9 0.6 %slice_reduce_fusion.24 = f32[]{:T(128)} fusion(f32[8,96,256]{2,1,0:T(8,128)S(1)} %bitcast.147), kind=kLoop, calls=%fused_computation.475 | loop fusion | flops 7 | bytes 36 | tf_op jit(solution)/shard_map/reduce_min | solution.py:1094
  33.2 3.3 %conditional.1 = ((f32[8,16,256]{2,1,0:T(8,128)}, f32[3,16,256]{2,1,0:T(8,128)})) conditional(s32[]{:T(128)} %convert_element_type.91, (f32[8,16,256]{2,1,0:T(8,128)S(1)}, s32[8,6]{1,0:T(8,128)S(1)}, (), s32[32,8]{0,1:T(8,128)S(1)}, s32[32,6]{0,1:T(8,128)S(1)}, /*index=5*/(), s32[32]{0:T(128)S(1)}, s32[32]{0:T(128)S(1)}) %tuple.107, ...), branch_computations={%region_1.12_spmd, %region_10.13_spmd} | conditional | flops 309503904 | bytes 22816608 | solution.py:1122
  33.4 3.1 %solve.1 = (f32[8,16,256]{2,1,0:T(8,128)}, f32[3,16,256]{2,1,0:T(8,128)}) custom-call(s32[8]{0:T(128)S(1)} %get-tuple-element.42.positions, s32[2,32]{1,0:T(2,128)S(1)} %get-tuple-element.43.owner_ref, s32[32,10]{1,0:T(8,128)S(1)} %get-tuple-element.44.cell_ref, f32[8,96,256]{2,1,0:T(8,128)S(1)} %get-tuple-element.45.all_ref, ...), custom_call_target="tpu_custom_call" | custom-call | tf_op jit(solution)/shard_map/cond/branch_1_fun/solve/pallas_call | solution.py:1098
  (11 shorter events, 0.0 us)
Async XLA Ops:
  0.6 5.9 %copy-start = (f32[8,16,256]{2,1,0:T(8,128)S(1)}, f32[8,16,256]{2,1,0:T(8,128)}, u32[]{:S(2)}) copy-start(f32[8,16,256]{2,1,0:T(8,128)} %rhs_ref.1) | copy-start | bytes 393220
  9.6 6.6 %collective-permute-start.19 = (f32[32,256]{1,0:T(8,128)}, f32[32,256]{1,0:T(8,128)S(1)}, u32[]{:S(2)}, u32[]{:S(2)}) collective-permute-start(f32[32,256]{1,0:T(8,128)} %get-tuple-element.61), channel_id=1, source_target_pairs={{0,16},{8,24},{16,0},{24,8},{1,17},{9,25},{17,1},{25,9},{2,18},{10... | collective-permute-start | bytes 98312 | tf_op jit(solution)/shard_map/ppermute | solution.py:1080
  13.7 5.9 %collective-permute-start.20 = (f32[32,256]{1,0:T(8,128)}, f32[32,256]{1,0:T(8,128)S(1)}, u32[]{:S(2)}, u32[]{:S(2)}) collective-permute-start(f32[32,256]{1,0:T(8,128)} %get-tuple-element.61), channel_id=1, source_target_pairs={{0,24},{8,16},{16,8},{24,0},{1,25},{9,17},{17,9},{25,1},{2,26},{10... | collective-permute-start | bytes 98312 | tf_op jit(solution)/shard_map/ppermute | solution.py:1080
  15.0 4.6 %collective-permute-start.18 = (f32[32,256]{1,0:T(8,128)}, f32[32,256]{1,0:T(8,128)S(1)}, u32[]{:S(2)}, u32[]{:S(2)}) collective-permute-start(f32[32,256]{1,0:T(8,128)} %get-tuple-element.60), channel_id=1, source_target_pairs={{0,8},{8,0},{16,24},{24,16},{1,9},{9,1},{17,25},{25,17},{2,10},{10... | collective-permute-start | bytes 98312 | tf_op jit(solution)/shard_map/ppermute | solution.py:1080
  15.3 0.7 %copy-start.4 = (s32[32]{0:T(128)S(1)}, s32[32]{0:T(128)}, u32[]{:S(2)}) copy-start(s32[32]{0:T(128)} %param.19) | copy-start | bytes 388
  15.3 0.7 %copy-start.5 = (s32[32]{0:T(128)S(1)}, s32[32]{0:T(128)}, u32[]{:S(2)}) copy-start(s32[32]{0:T(128)} %param.18) | copy-start | bytes 388
  31.9 1.3 %copy-start.2 = (s32[32,6]{0,1:T(8,128)S(1)}, s32[32,6]{0,1:T(8,128)}, u32[]{:S(2)}) copy-start(s32[32,6]{0,1:T(8,128)} %param.16) | copy-start | bytes 2308
  31.9 1.3 %copy-start.3 = (s32[8,6]{1,0:T(8,128)S(1)}, s32[8,6]{1,0:T(8,128)}, u32[]{:S(2)}) copy-start(s32[8,6]{1,0:T(8,128)} %param.15) | copy-start | bytes 580
  32.5 0.7 %copy-start.1 = (s32[32,8]{0,1:T(8,128)S(1)}, s32[32,8]{0,1:T(8,128)}, u32[]{:S(2)}) copy-start(s32[32,8]{0,1:T(8,128)} %param.17) | copy-start | bytes 3076

commit v2 on v1

--- a/solution.py
+++ b/solution.py
@@ -3,6 +3,7 @@
 import jax
 import jax.numpy as jnp
 from jax import lax
+import numpy as np
 from jax.experimental import pallas as pl
 from jax.experimental.pallas import tpu as pltpu
 from jax.sharding import PartitionSpec as P
@@ -351,6 +352,7 @@
 LANES = 128
 OWN_ROWS = 64
 MSG_ROWS = 32
+VMEM_LIMIT = 16 * 1024 * 1024
 
 
 def lane_iota(shape):
@@ -378,7 +380,66 @@
 
 
 def zero_one(condition, scale=1.0):
-    return jnp.where(condition, scale, 0.0).astype(jnp.bfloat16)
+    return np.where(condition, scale, 0.0).astype(jnp.bfloat16)
+
+
+def key_col(rows, columns):
+    return np.arange(rows)[:, None], np.arange(columns)[None, :]
+
+
+def octant_table():
+    key, col = key_col(256, LANES)
+    key_x = key % 16
+    col_x = col % 8
+    return zero_one(
+        (key // 32 == col % 64 // 8)
+        & (
+            ((col < 64) & (key_x // 2 == col_x))
+            | ((col >= 64) & (col_x == 7) & (key_x == 0))
+            | ((col >= 64) & (col_x == 0) & (key_x == 15))
+        ),
+        0.5,
+    )
+
+
+def face_table():
+    key, col = key_col(256, LANES)
+    return zero_one(
+        (key // 16 == col % 64)
+        & (((col < 64) & (key % 16 == 0)) | ((col >= 64) & (key % 16 == 15)))
+    )
+
+
+def root_table(sub_count):
+    key, col = key_col(4 * LANES, 16 * sub_count)
+    near_x = key % 8 // 4
+    row = (key // LANES) % 2 * 4 + key % LANES // 32
+    along = np.where(key < 256, near_x + 1, np.where(near_x == 0, 3, 0))
+    return zero_one(col == row * (2 * sub_count) + along, 0.25)
+
+
+def root_spread_table(sub_count):
+    key, col = key_col(16 * sub_count, 256)
+    return zero_one(key == (col // 32) * (2 * sub_count) + col % 8 // 4)
+
+
+def parent_table():
+    key, col = key_col(256, 256)
+    return zero_one(key == (col % 16 // 8) * LANES + (col // 16) * 8 + col % 8)
+
+
+def leaf_table_of_cells():
+    key, col = key_col(256, 256)
+    y = col // 16
+    x = col % 16
+    return zero_one(key == (y % 2 * 2 + x % 2) * 64 + y // 2 * 8 + x // 2)
+
+
+def push_table():
+    key, col = key_col(LANES, 256)
+    group = key // 16
+    cell = np.select([group == 0, group == 1, group == 4, group == 5], [0, 15, 1, 14], 16)
+    return zero_one((key % 16 == col // 16) & (col % 16 == cell))
 
 
 def beside_x(chunk, width):
@@ -422,111 +483,132 @@
     return in_x, in_y, in_z
 
 
-def coarse_x_pair(columns, index, half):
+def coarse_turns(columns):
+    return (
+        [[turn(chunk, 8, 1) for chunk in halves] for halves in columns],
+        [[turn(chunk, -8, 1) for chunk in halves] for halves in columns],
+    )
+
+
+def coarse_y_pair(up, down):
+    lane = lane_iota(up[0].shape)
+    zero = jnp.zeros_like(up[0])
+    lower = []
+    upper = []
+    for half in range(2):
+        lower.append(jnp.where(lane < 8, up[half - 1] if half > 0 else zero, up[half]))
+        upper.append(jnp.where(lane >= LANES - 8, down[half + 1] if half < 1 else zero, down[half]))
+    return lower, upper
+
+
+def coarse_x_pair(columns, up, down, index, half):
     chunk = columns[index][half]
     cell = lane_iota(chunk.shape) % 8
-    low = turn(chunk, 1, 1)
-    high = turn(chunk, -1, 1)
-    if index > 0:
-        low = jnp.where(cell == 0, turn(columns[index - 1][half], -7, 1), low)
-    else:
-        low = jnp.where(cell == 0, 0.0, low)
-    if index + 1 < len(columns):
-        high = jnp.where(cell == 7, turn(columns[index + 1][half], 7, 1), high)
-    else:
-        high = jnp.where(cell == 7, 0.0, high)
+    before = down[index - 1][half] if index > 0 else jnp.zeros_like(chunk)
+    after = up[index + 1][half] if index + 1 < len(columns) else jnp.zeros_like(chunk)
+    low = turn(jnp.where(cell == 7, before, chunk), 1, 1)
+    high = turn(jnp.where(cell == 0, after, chunk), -1, 1)
     return low, high
 
 
-def coarse_beside(columns):
-    result = []
-    for index in range(len(columns)):
-        lower, upper = y_pair(columns[index], 8)
+def coarse_sums(columns):
+    up, down = coarse_turns(columns)
+
+    def sums(index):
+        lower, upper = coarse_y_pair(up[index], down[index])
         halves = []
-        for half in range(len(columns[index])):
+        for half in range(2):
             chunk = columns[index][half]
-            low, high = coarse_x_pair(columns, index, half)
+            low, high = coarse_x_pair(columns, up, down, index, half)
             total = low + high + lower[half] + upper[half]
-            total = total + turn(chunk, 1, 0) + turn(chunk, -1, 0)
-            halves.append(total)
-        result.append(halves)
-    return result
-
-
-def count_true(condition):
-    return jnp.sum(jnp.where(condition, 1.0, 0.0))
-
-
-def list_check(sub_count, blk_count, blocks, leaf_ref, parent_ref, cell_ref, sub_here, blk_here):
+            halves.append(total + turn(chunk, 1, 0) + turn(chunk, -1, 0))
+        return halves
+
+    return sums
+
+
+def as_column(row):
+    count = row.shape[1]
+    shape = (count, count)
+    return jnp.sum(
+        jnp.where(row_iota(shape) == lane_iota(shape), row, 0.0), axis=1, keepdims=True
+    )
+
+
+def power_div(values, divisor):
+    return lax.shift_right_logical(values, jnp.full_like(values, divisor.bit_length() - 1))
+
+
+def power_rem(values, divisor):
+    return values & (divisor - 1)
+
+
+def grid_codes(sub_count, wide_y, child_ref, place_ref):
+    side_y = wide_y // 2
+    side_x = sub_count // 2
+    shape = child_ref.shape
+    octant = row_iota(shape)
+    place = jnp.broadcast_to(place_ref[...], shape)
+    cell_z = 2 * power_div(place, side_y * side_x) + power_div(octant, 4)
+    cell_y = 2 * power_rem(power_div(place, side_x), side_y) + power_rem(power_div(octant, 2), 2)
+    cell_x = 2 * power_rem(place, side_x) + power_rem(octant, 2)
+    return (cell_z * wide_y + cell_y) * sub_count + cell_x
+
+
+def own_codes(sub_count, blocks, child_ref, codes, sub_here, blk_here):
+    first = (blk_here * sub_count + sub_here) * blocks
+    codes = codes.astype(jnp.float32)
+    return [
+        jnp.sum(jnp.where(child_ref[...] == first + slot, codes, 0.0)).astype(jnp.int32)
+        for slot in range(blocks)
+    ]
+
+
+def lists_agree(sub_count, blk_count, leaf_ref, parent_ref, child_ref, place_ref, codes, own):
+    blocks = len(own)
     wide_y = blocks // 2
     side_y = wide_y // 2
     side_x = sub_count // 2
-    parents = cell_ref.shape[0]
-    side_yx = side_y * side_x
+    parents = child_ref.shape[1]
     layer = wide_y * sub_count
-    children = cell_ref[:, 0:8]
-    octant = lane_iota((parents, 8))
-    place = jnp.broadcast_to(cell_ref[:, 8:9], (parents, 8))
-    cell_z = 2 * lax.div(place, side_yx) + lax.div(octant, 4)
-    cell_y = 2 * lax.rem(lax.div(place, side_x), side_y) + lax.rem(lax.div(octant, 2), 2)
-    cell_x = 2 * lax.rem(place, side_x) + lax.rem(octant, 2)
-    code = (cell_z * wide_y + cell_y) * sub_count + cell_x
-    wrong = count_true(lax.div(children, blocks) != lax.div(cell_z, 2) * sub_count + cell_x)
-    width = 6 * blocks
-    listed = leaf_ref[...]
-    lane = lane_iota((1, width))
-    own = (blk_here * sub_count + sub_here) * blocks + lax.rem(lane, blocks)
-    found = jnp.zeros((parents, width), jnp.int32)
-    found_own = jnp.zeros((parents, width), jnp.int32)
-    for o in range(8):
-        child = children[:, o : o + 1]
-        value = code[:, o : o + 1]
-        found = jnp.where(child == listed, value, found)
-        found_own = jnp.where(child == own, value, found_own)
-    found = jnp.sum(found.astype(jnp.float32), axis=0, keepdims=True).astype(jnp.int32)
-    found_own = jnp.sum(found_own.astype(jnp.float32), axis=0, keepdims=True).astype(jnp.int32)
-    own_z = lax.div(found_own, layer)
-    own_y = lax.rem(lax.div(found_own, sub_count), wide_y)
-    own_x = lax.rem(found_own, sub_count)
-    face = lax.div(lane, blocks)
-
-    def by_axis(first, second, third):
-        return jnp.where(face < 2, first, jnp.where(face < 4, second, third))
-
-    sign = 2 * lax.rem(face, 2) - 1
-    goal = by_axis(own_x, own_y, own_z) + sign
-    exists = (goal >= 0) & (goal < by_axis(sub_count, wide_y, 2 * blk_count))
-    wanted = found_own + sign * by_axis(1, sub_count, layer)
-    wrong = wrong + jnp.sum(
-        jnp.where(
-            exists,
-            jnp.where((listed >= 0) & (found == wanted), 0.0, 1.0),
-            jnp.where(listed < 0, 0.0, 1.0),
-        )
-    )
-    position = lax.rem(own_z, 2) * wide_y + own_y
-    listed = parent_ref[0:1, :]
-    place = parent_ref[1:2, :]
-    shape = (parents, 6 * parents)
-    hit = row_iota(shape) == listed
-    found = jnp.sum(
-        jnp.where(hit, cell_ref[:, 8:9].astype(jnp.float32), 0.0), axis=0, keepdims=True
-    ).astype(jnp.int32)
-    face = lax.div(lane_iota((1, 6 * parents)), parents)
-    sign = 2 * lax.rem(face, 2) - 1
-    goal = sign + by_axis(
-        lax.rem(place, side_x), lax.rem(lax.div(place, side_x), side_y), lax.div(place, side_yx)
-    )
-    exists = (goal >= 0) & (goal < by_axis(side_x, side_y, blk_count))
-    wanted = place + sign * by_axis(1, side_x, side_yx)
-    wrong = wrong + jnp.sum(
-        jnp.where(
-            exists,
-            jnp.where((listed >= 0) & (found == wanted), 0.0, 1.0),
-            jnp.where(listed < 0, 0.0, 1.0),
-        )
-    )
-    return position, jnp.where(wrong == 0.0, 1.0, 0.0)
+    children = child_ref[...]
+    device = power_div(codes, 2 * layer) * sub_count + power_rem(codes, sub_count)
+    missed = jnp.where(power_div(children, blocks) != device, 1.0, 0.0)
+    faults = jnp.int32(0)
+    for slot in range(blocks):
+        for axis, (stride, length) in enumerate(
+            ((1, sub_count), (sub_count, wide_y), (layer, 2 * blk_count))
+        ):
+            along = lax.rem(lax.div(own[slot], stride), length)
+            for sign in (-1, 1):
+                listed = leaf_ref[slot, 2 * axis + (sign + 1) // 2]
+                exists = (along + sign >= 0) & (along + sign < length)
+                hit = (children == listed) & (codes == own[slot] + sign * stride)
+                missed = missed - jnp.where(hit, 1.0, 0.0)
+                faults = faults + jnp.where(
+                    exists, jnp.where(listed >= 0, 1, -100000), jnp.where(listed < 0, 0, -100000)
+                )
+    wrong = jnp.abs(jnp.sum(missed) + faults.astype(jnp.float32))
+    place_row = place_ref[...].astype(jnp.float32)
+    place_column = as_column(place_row)
+    number = row_iota((parents, parents))
+    place = place_ref[...]
+    missed = jnp.zeros((1, parents), jnp.float32)
+    for axis, (stride, length) in enumerate(((1, side_x), (side_x, side_y), (side_y * side_x, blk_count))):
+        along = power_rem(power_div(place, stride), length)
+        for sign in (-1, 1):
+            face = 2 * axis + (sign + 1) // 2
+            listed = parent_ref[face : face + 1, :]
+            found = jnp.sum(jnp.where(number == listed, place_column, 0.0), axis=0, keepdims=True)
+            exists = (along + sign >= 0) & (along + sign < length)
+            wanted = (place + sign * stride).astype(jnp.float32)
+            missed = missed + jnp.where(
+                exists,
+                jnp.where((listed >= 0) & (found == wanted), 0.0, 1.0),
+                jnp.where(listed < 0, 0.0, 1.0),
+            )
+    wrong = wrong + jnp.sum(missed)
+    return jnp.where(wrong == 0.0, 1.0, 0.0)
 
 
 def limits(sub_count, blk_count):
@@ -546,63 +628,67 @@
     )
 
 
+def placed_chunks(placed, wide_y):
+    chunks = []
+    for k in range(2 * wide_y):
+        lanes = slice(LANES * (k % 2), LANES * (k % 2) + LANES)
+        chunks.append(
+            jnp.concatenate([placed[k // 2, :, lanes], placed[wide_y + k // 2, :, lanes]], axis=0)
+        )
+    return chunks
+
+
+def return_gain(shape, x_low, x_high, z_low, z_high):
+    cell = lane_iota(shape) % 16
+    row = row_iota(shape)
+    return (
+        jnp.where(cell == 0, x_low, 0.0)
+        + jnp.where(cell == 15, x_high, 0.0)
+        + jnp.where(row == 0, z_low, 0.0)
+        + jnp.where(row == shape[0] - 1, z_high, 0.0)
+    ) * (FACTOR * FACTOR)
+
+
 def push_kernel(
-    sub_count, blk_count, blk_bits, leaf_ref, parent_ref, cell_ref, rhs_ref,
-    position_ref, own_ref, own_part_ref, faces_ref, *rest
+    sub_count, blk_count, blk_bits,
+    leaf_ref, parent_ref, child_ref, place_ref, rhs_ref, table_a_ref, table_r_ref,
+    position_ref, own_ref, *rest
 ):
     msg_refs = rest[:blk_bits]
-    placed, rows_s, rows_g, left_a, left_c, coarse_s = rest[blk_bits:]
+    placed, rows_s, rows_g, left_a, coarse_s = rest[blk_bits:]
     blocks = rhs_ref.shape[0]
     wide_y = blocks // 2
-    chunk_count = 2 * wide_y
     f = FACTOR
     f2 = f * f
     sub_here, blk_here, x_low, x_high, z_low, z_high = limits(sub_count, blk_count)
-    position, good = list_check(
-        sub_count, blk_count, blocks, leaf_ref, parent_ref, cell_ref, sub_here, blk_here
-    )
+    codes = grid_codes(sub_count, wide_y, child_ref, place_ref)
+    own_code = own_codes(sub_count, blocks, child_ref, codes, sub_here, blk_here)
+    layer = wide_y * sub_count
     for slot in range(blocks):
-        at = jnp.clip(position[0, slot], 0, blocks - 1)
-        position_ref[slot] = at
-        placed[at] = rhs_ref[slot]
-    s = []
-    for k in range(chunk_count):
-        lanes = slice(LANES * (k % 2), LANES * (k % 2) + LANES)
-        s.append(
-            jnp.concatenate([placed[k // 2, :, lanes], placed[wide_y + k // 2, :, lanes]], axis=0)
+        code = own_code[slot]
+        position = lax.rem(lax.div(code, layer), 2) * wide_y + lax.rem(
+            lax.div(code, sub_count), wide_y
         )
+        position_ref[slot] = position
+        placed[position] = rhs_ref[slot]
+    s = placed_chunks(placed, wide_y)
     shape = s[0].shape
-    cell = lane_iota(shape) % 16
-    row = row_iota(shape)
     top = shape[0] - 1
-    back = (
-        jnp.where(cell == 0, x_low, 0.0)
-        + jnp.where(cell == 15, x_high, 0.0)
-        + jnp.where(row == 0, z_low, 0.0)
-        + jnp.where(row == top, z_high, 0.0)
-    ) * f2
+    back = return_gain(shape, x_low, x_high, z_low, z_high)
     sx, sy, sz = fine_beside(s)
     w = [SELF * a + f * (x + y + z) for a, x, y, z in zip(s, sx, sy, sz)]
     wx, wy, wz = fine_beside(w)
-    for k in range(chunk_count):
+    for k in range(2 * wide_y):
         half = slice(LANES * (k % 2), LANES * (k % 2) + LANES)
-        r = SELF * w[k] + f * (wx[k] + wy[k] + wz[k]) + back * s[k]
-        part = f * (s[k] + w[k] + r)
-        own_part_ref[k // 2, :, half] = part[:16]
-        own_part_ref[wide_y + k // 2, :, half] = part[16:]
-        rows_s[k] = r
+        rows_s[k] = SELF * w[k] + f * (wx[k] + wy[k] + wz[k]) + back * s[k]
         base = (SELF * f + f2) * s[k] + f * w[k]
-        gx = base + f2 * (sy[k] + sz[k])
-        rows_g[k] = gx
+        rows_g[k] = base + f2 * (sy[k] + sz[k])
         gz = base + f2 * (sx[k] + sy[k])
         line = 48 * (k // 2)
         left_a[line + 16 : line + 17, half] = gz[0:1]
         left_a[line + 17 : line + 18, half] = gz[top : top + 1]
         left_a[line + 40 : line + 41, half] = (2.0 * f2) * s[k][0:1]
         left_a[line + 41 : line + 42, half] = (2.0 * f2) * s[k][top : top + 1]
-        line_c = 64 * (k // 2)
-        left_c[line_c : line_c + 32, half] = gx + (f - f2) * s[k]
-        left_c[line_c + 32 : line_c + 64, half] = s[k]
         edge = gz + (f - f2) * s[k]
         for bit in range(blk_bits):
             upward = (blk_here // (1 << bit)) % 2 == 0
@@ -612,7 +698,7 @@
             msg_refs[bit][16 + wide_y + k // 2 : 17 + wide_y + k // 2, half] = jnp.where(
                 upward, s[k][top : top + 1], s[k][0:1]
             )
-    for k in range(chunk_count):
+    for k in range(2 * wide_y):
         half = slice(LANES * (k % 2), LANES * (k % 2) + LANES)
         line = 48 * (k // 2)
         left_a[line : line + 16, half] = (
@@ -621,31 +707,10 @@
         left_a[line + 24 : line + 40, half] = (
             rows_g[k, pl.ds(0, 16, stride=2), :] + rows_g[k, pl.ds(1, 16, stride=2), :]
         )
-    key = row_iota((256, LANES))
-    col = lane_iota((256, LANES))
-    key_y = key // 16
-    key_x = key % 16
-    col_y = (col % 64) // 8
-    col_x = col % 8
-    same_y = key_y // 2 == col_y
-    table_a = zero_one(
-        same_y
-        & (
-            ((col < 64) & (key_x // 2 == col_x))
-            | ((col >= 64) & (col_x == 7) & (key_x == 0))
-            | ((col >= 64) & (col_x == 0) & (key_x == 15))
-        ),
-        0.5,
-    )
-    out_a = split_dot(left_a[...], table_a)
-    table_c = zero_one(
-        (key_y == col % 64) & (((col < 64) & (key_x == 0)) | ((col >= 64) & (key_x == 15)))
-    )
-    out_c = split_dot(left_c[...], table_c)
-    faces = out_c[0:64]
-    for yy in range(1, wide_y):
-        faces = faces + turn(out_c[64 * yy : 64 * yy + 64], 16 * yy, 1)
-    faces_ref[...] = faces
+    out_a = split_dot(left_a[...], table_a_ref[...])
+    good = lists_agree(
+        sub_count, blk_count, leaf_ref, parent_ref, child_ref, place_ref, codes, own_code
+    )
     lane24 = lane_iota((24, LANES))
     main = []
     side = []
@@ -656,14 +721,15 @@
         first = out_a[96 * half + 24 : 96 * half + 48]
         second = out_a[96 * half + 72 : 96 * half + 96]
         side.append(jnp.where(lane24 < 64, turn(first, 64, 1), second))
-    own_ref[...] = jnp.zeros(own_ref.shape, jnp.float32)
+    zero3 = jnp.zeros((3, LANES), jnp.float32)
     for half in range(2):
         lanes = slice(LANES * half, LANES * half + LANES)
         for base_row, piece in ((0, main[half]), (24, side[half])):
+            own_ref[base_row : base_row + 3, lanes] = zero3
+            own_ref[base_row + 3 : base_row + 4, lanes] = piece[16:17] * z_low
             own_ref[base_row + 4 : base_row + 20, lanes] = piece[0:16]
-            own_ref[base_row + 3 : base_row + 4, lanes] = piece[16:17] * z_low
             own_ref[base_row + 20 : base_row + 21, lanes] = piece[17:18] * z_high
-    own_ref[56:64, :] = jnp.zeros((8, 256), jnp.float32) + good
+            own_ref[base_row + 21 : base_row + 24, lanes] = zero3
     cell8 = lane24 % 8
     row24 = row_iota((24, LANES))
     inside_z = jnp.where(row24 < 4, z_low, jnp.where(row24 >= 20, z_high, 1.0))
@@ -675,16 +741,20 @@
         main24,
         [jnp.where(cell8 == 0, piece, 0.0) * x_high for piece in side24],
     ]
-    near = coarse_beside(columns)
-    wp = [
-        [gain[b] * (SELF * columns[b][h] + f * near[b][h]) for h in range(2)] for b in range(3)
-    ]
-    near = coarse_beside(wp)
+    sums = coarse_sums(columns)
+    wp = []
     for b in range(3):
+        near = sums(b)
+        wp.append([gain[b] * (SELF * columns[b][h] + f * near[h]) for h in range(2)])
+    sums = coarse_sums(wp)
+    zero8 = jnp.zeros((8, LANES), jnp.float32)
+    for b in range(3):
+        near = sums(b)
         for h in range(2):
-            coarse_s[2 * b + h, 0:24] = gain[b] * (SELF * wp[b][h] + f * near[b][h])
-            coarse_s[2 * b + h, 24:32] = jnp.zeros((8, LANES), jnp.float32)
+            coarse_s[2 * b + h, 0:24] = gain[b] * (SELF * wp[b][h] + f * near[h])
+            coarse_s[2 * b + h, 24:32] = zero8
     pieces = []
+    low_cells = lane_iota((8, LANES)) % 8 < 4
     for k in range(6):
         pieces.append(
             coarse_s[k, pl.ds(0, 8, stride=4), :]
@@ -692,27 +762,68 @@
             + coarse_s[k, pl.ds(2, 8, stride=4), :]
             + coarse_s[k, pl.ds(3, 8, stride=4), :]
         )
-    root_left = jnp.concatenate(pieces, axis=1)
+    outer = [jnp.where(low_cells, pieces[4 + h], pieces[h]) for h in range(2)]
+    root_left = jnp.concatenate([pieces[2], pieces[3]] + outer, axis=1)
     root_lanes = 16 * sub_count
-    key = row_iota((6 * LANES, root_lanes))
-    col = lane_iota((6 * LANES, root_lanes))
-    target = (
-        ((key // LANES) % 2 * 4 + key % LANES // 32) * (2 * sub_count)
-        + 2 * (sub_here + key // 256 - 1)
-        + key % 8 // 4
-    )
-    root_part = split_dot(root_left, zero_one(col == target, 0.25))
+    root_part = split_dot(root_left, table_r_ref[...])
+    root_part = pltpu.roll(root_part, 2 * sub_here + root_lanes - 1, 1)
+    root_part = jnp.where(row_iota(root_part.shape) < 6, root_part, 0.0)
     own_ref[48:56, 0:root_lanes] = root_part
+    if root_lanes < 256:
+        own_ref[48:56, root_lanes:256] = jnp.zeros((8, 256 - root_lanes), jnp.float32)
+    flag = jnp.zeros((8, LANES), jnp.float32) + good
+    for lanes in (slice(0, LANES), slice(LANES, 256)):
+        own_ref[56:64, lanes] = flag
     for bit in range(blk_bits):
         upward = (blk_here // (1 << bit)) % 2 == 0
         ref = msg_refs[bit]
         ref[8:16, :] = own_ref[48:56, :]
-        ref[24:32, :] = jnp.zeros((8, 256), jnp.float32) + good
-        ref[24:25, 0:LANES] = jnp.where(upward, faces[63:64], faces[32:33])
+        ref[24:32, 0:LANES] = zero8
+        ref[24:32, LANES:256] = flag
         for base_row, source in ((0, 0), (4, 24)):
             ref[base_row : base_row + 4, :] = jnp.where(
                 upward, own_ref[source + 17 : source + 21, :], own_ref[source + 3 : source + 7, :]
             )
+
+
+def side_kernel(
+    sub_count, blk_count, slots,
+    positions, owner_ref, place_ref, rhs_ref, table_ref,
+    slot_ref, part_ref, faces_ref,
+    placed, left_c
+):
+    blocks = rhs_ref.shape[0]
+    wide_y = blocks // 2
+    f = FACTOR
+    f2 = f * f
+    sub_here, blk_here, x_low, x_high, z_low, z_high = limits(sub_count, blk_count)
+    for slot in range(blocks):
+        placed[positions[slot]] = rhs_ref[slot]
+    s = placed_chunks(placed, wide_y)
+    back = return_gain(s[0].shape, x_low, x_high, z_low, z_high)
+    sx, sy, sz = fine_beside(s)
+    w = [SELF * a + f * (x + y + z) for a, x, y, z in zip(s, sx, sy, sz)]
+    wx, wy, wz = fine_beside(w)
+    for k in range(2 * wide_y):
+        half = slice(LANES * (k % 2), LANES * (k % 2) + LANES)
+        r = SELF * w[k] + f * (wx[k] + wy[k] + wz[k]) + back * s[k]
+        part = f * (s[k] + w[k] + r)
+        part_ref[k // 2, :, half] = part[:16]
+        part_ref[wide_y + k // 2, :, half] = part[16:]
+        line = 64 * (k // 2)
+        left_c[line : line + 32, half] = (
+            (SELF * f + f) * s[k] + f * w[k] + f2 * (sy[k] + sz[k])
+        )
+        left_c[line + 32 : line + 64, half] = s[k]
+    out_c = split_dot(left_c[...], table_ref[...])
+    faces = out_c[0:64]
+    for yy in range(1, wide_y):
+        faces = faces + turn(out_c[64 * yy : 64 * yy + 64], 16 * yy, 1)
+    faces_ref[...] = faces
+    owned = owned_slots(sub_count, blk_count, slots, sub_here, blk_here, owner_ref, place_ref)
+    for k in range(slots):
+        for j in range(3):
+            slot_ref[3 * k + j] = owned[k][j]
 
 
 def neighbour_pick(blk_here, blk_count, msg_refs):
@@ -742,12 +853,15 @@
 
 def join_kernel(sub_count, blk_count, own_ref, faces_ref, *rest):
     msg_refs = rest[: blk_count - 1]
-    out_ref, root_s = rest[blk_count - 1 :]
+    out_ref, lines_ref, root_s = rest[blk_count - 1 :]
     _, blk_here, _, _, z_low, z_high = limits(sub_count, blk_count)
     below, above = neighbour_pick(blk_here, blk_count, msg_refs)
     row8 = row_iota((8, LANES))
     low_rows = (row8 >= 1) & (row8 < 5)
     high_rows = (row8 >= 3) & (row8 < 7)
+    good = own_ref[56:64, 0:LANES]
+    for ref in msg_refs:
+        good = jnp.minimum(good, ref[24:32, LANES:256])
     for half in range(2):
         lanes = slice(LANES * half, LANES * half + LANES)
         low = below(slice(0, 8), lanes) * z_low
@@ -760,16 +874,14 @@
             out_ref[base + 16 : base + 24, lanes] = own_ref[
                 base + 16 : base + 24, lanes
             ] + jnp.where(high_rows, turn(high, high_turn, 0), 0.0)
+        out_ref[23:24, lanes] = good[0:1]
     root_s[...] = jnp.zeros(root_s.shape, jnp.float32)
-    good = own_ref[56:64, 0:LANES]
     for d in range(blk_count):
         start = 4 * (blk_here ^ d) + 3
         for part in range(root_s.shape[0]):
             lanes = slice(LANES * part, LANES * part + LANES)
             value = own_ref[48:56, lanes] if d == 0 else msg_refs[d - 1][8:16, lanes]
             root_s[part, pl.ds(start, 8), :] = root_s[part, pl.ds(start, 8), :] + value
-        if d > 0:
-            good = jnp.minimum(good, msg_refs[d - 1][24:32, LANES:256])
     tile = 0
     for start in range(0, 4 * blk_count, 8):
         for part in range(root_s.shape[0]):
@@ -778,59 +890,63 @@
             out_ref[row : row + 8, lanes] = root_s[part, 4 + start : 12 + start]
             tile += 1
     row = 48 + 8 * root_tiles(sub_count, blk_count)
-    low = below(slice(24, 32), slice(0, LANES)) * z_low
-    high = above(slice(24, 32), slice(0, LANES)) * z_high
-    out_ref[row : row + 8, 0:LANES] = jnp.where(row8 == 0, low, turn(high, 1, 0))
-    out_ref[row : row + 8, LANES:256] = good
+    count = lines_ref.shape[0] // 2
+    half = count // 2
+    low = below(slice(16, 16 + count), slice(0, 256)) * z_low
+    high = above(slice(16, 16 + count), slice(0, 256)) * z_high
+    lines_ref[0:count] = low
+    lines_ref[count : 2 * count] = high
+    out_ref[row : row + half, :] = low[half:count]
+    out_ref[row + half : row + count, :] = high[half:count]
     out_ref[row + 8 : row + 40, 0:LANES] = faces_ref[0:32]
     out_ref[row + 8 : row + 40, LANES:256] = faces_ref[32:64]
 
 
-def owned_slots(sub_count, blk_count, slots, sub_here, blk_here, owner_ref, cell_ref):
+def owned_slots(sub_count, blk_count, slots, sub_here, blk_here, owner_ref, place_ref):
     parents = owner_ref.shape[1]
     parent_len = parents // blk_count
-    side_y = parent_len // (sub_count // 2)
     side_x = sub_count // 2
-    owners = owner_ref[0:1, :]
-    places = owner_ref[1:2, :]
+    side_y = parent_len // side_x
     number = lane_iota((1, parents))
+    here = (owner_ref[...] == sub_here) & (lax.div(number, parent_len) == blk_here)
+    mine = jnp.where(here, 1.0, 0.0)
     shape = (parents, parents)
-    in_range = lax.div(number, parent_len) == blk_here
-    mine = in_range & (owners == sub_here)
-    column = cell_ref[:, 9:10]
-    row = row_iota((parents, 1))
-    column_mine = (column == sub_here) & (lax.div(row, parent_len) == blk_here)
     rank = jnp.sum(
-        jnp.where(column_mine & (row_iota(shape) < lane_iota(shape)), 1.0, 0.0),
-        axis=0,
-        keepdims=True,
-    )
+        jnp.where(row_iota(shape) < lane_iota(shape), as_column(mine), 0.0), axis=0, keepdims=True
+    )
+    places = place_ref[...].astype(jnp.float32)
     found = []
     for k in range(slots):
-        chosen = jnp.where(mine & (rank == float(k)), 1.0, 0.0)
-        place = jnp.sum(chosen * places.astype(jnp.float32)).astype(jnp.int32)
+        chosen = jnp.where(rank == float(k), mine, 0.0)
+        place = jnp.sum(chosen * places).astype(jnp.int32)
         found.append(
-            (lax.rem(lax.div(place, side_x), side_y), lax.rem(place, side_x), jnp.sum(chosen))
+            (
+                lax.rem(lax.div(place, side_x), side_y),
+                lax.rem(place, side_x),
+                jnp.sum(chosen).astype(jnp.int32),
+            )
         )
     return found
 
 
 def solve_kernel(
-    sub_count, blk_count, slots, positions, owner_ref, cell_ref, all_ref, part_ref, *rest
+    sub_count, blk_count, slots,
+    positions, owned, all_ref, part_ref, lines_ref, table_w_ref, table_p_ref, table_l_ref, table_x_ref,
+    leaf_ref, parent_ref, good_ref,
+    placed, par_s, root_s, fine_s, push_s
 ):
-    msg_refs = rest[: blk_count - 1]
-    leaf_ref, parent_ref = rest[blk_count - 1 : blk_count + 1]
-    placed, par_s, root_s, fine_s, push_s = rest[blk_count + 1 :]
     blocks = part_ref.shape[0]
     wide_y = blocks // 2
     f = FACTOR
     f2 = f * f
     sub_here, blk_here, x_low, x_high, z_low, z_high = limits(sub_count, blk_count)
-    below, above = neighbour_pick(blk_here, blk_count, msg_refs)
-    owned = owned_slots(sub_count, blk_count, slots, sub_here, blk_here, owner_ref, cell_ref)
     row8 = row_iota((8, LANES))
-    cell24 = lax.rem(lane_iota((24, LANES)), 8)
+    cell24 = lane_iota((24, LANES)) % 8
     row24 = row_iota((24, LANES))
+    good = all_ref[0, 16:24, 0:LANES]
+    for c in range(1, sub_count):
+        good = jnp.minimum(good, all_ref[c, 16:24, 0:LANES])
+    good_ref[0] = jnp.min(jnp.where(row8 == 7, good, 1.0)).astype(jnp.int32)
     source = []
     for c in range(sub_count):
         halves = []
@@ -866,15 +982,30 @@
     shape = root_source.shape
     lane = lane_iota(shape)
     row = row_iota(shape)
-    values = f * root_source
-    for _ in range(ROOT_SWEEPS - 1):
+
+    def root_sweep(values):
         total = jnp.where(lane % row_len > 0, turn(values, 1, 1), 0.0)
         total = total + jnp.where(lane % row_len < row_len - 1, turn(values, -1, 1), 0.0)
         total = total + jnp.where(lane >= row_len, turn(values, row_len, 1), 0.0)
         total = total + jnp.where(lane < root_lanes - row_len, turn(values, -row_len, 1), 0.0)
         total = total + jnp.where(row > 0, turn(values, 1, 0), 0.0)
         total = total + jnp.where(row < root_rows - 1, turn(values, -1, 0), 0.0)
-        values = SELF * values + f * (root_source + total)
+        return SELF * values + f * (root_source + total)
+
+    values = f * root_source
+    left_sweeps = ROOT_SWEEPS - 1
+    sums = coarse_sums(source)
+    two = []
+    for c in range(sub_count):
+        if left_sweeps > 0:
+            values = root_sweep(values)
+            left_sweeps -= 1
+        near = sums(c)
+        two.append(
+            [(f + f * SELF) * source[c][half] + f2 * near[half] for half in range(2)]
+        )
+    for _ in range(left_sweeps):
+        values = root_sweep(values)
     root_s[...] = jnp.zeros(root_s.shape, jnp.float32)
     for part in range(parts):
         root_s[part, 4 : 4 + root_rows] = values[:, LANES * part : LANES * part + LANES]
@@ -882,9 +1013,7 @@
         [root_s[part, pl.ds(4 * blk_here + 3, 8), :] for part in range(parts)], axis=1
     )
     left = jnp.concatenate([turn(mine, -2 * c, 1) for c in range(sub_count)], axis=0)
-    key = row_iota((root_lanes, 256))
-    col = lane_iota((root_lanes, 256))
-    wide = split_dot(left, zero_one(key == (col // 32) * row_len + col % 8 // 4))
+    wide = split_dot(left, table_w_ref[...])
 
     valid = (
         (row24 >= 2)
@@ -892,13 +1021,11 @@
         & ((row24 >= 4) | (z_low > 0.0))
         & ((row24 < 20) | (z_high > 0.0))
     )
-    near = coarse_beside(source)
     three = []
     for c in range(sub_count):
         halves = []
         for half in range(2):
             lanes = slice(LANES * half, LANES * half + LANES)
-            wp = SELF * source[c][half] + f * near[c][half]
             tiles = []
             for t in range(3):
                 first = wide[8 * c + 2 * t : 8 * c + 2 * t + 1, lanes]
@@ -910,18 +1037,21 @@
                         jnp.broadcast_to(second, (8, LANES)),
                     )
                 )
-            value = f * (source[c][half] + wp) + jnp.concatenate(tiles, axis=0)
+            value = two[c][half] + jnp.concatenate(tiles, axis=0)
             halves.append(jnp.where(valid, value, 0.0))
         three.append(halves)
-    near = coarse_beside(three)
+    sums = coarse_sums(three)
     for c in range(sub_count):
+        near = sums(c)
         for half in range(2):
-            value = SELF * three[c][half] + f * (near[c][half] + source[c][half])
+            value = SELF * three[c][half] + f * (near[half] + source[c][half])
             par_s[c, half] = jnp.where(valid, value, 0.0)
 
     pieces = []
     for k in range(slots):
-        half, place_x, filled = owned[k]
+        half = owned[3 * k]
+        place_x = owned[3 * k + 1]
+        filled = owned[3 * k + 2].astype(jnp.float32)
         pieces.append(
             jnp.concatenate(
                 [par_s[2 * place_x, half, 4:20], par_s[2 * place_x + 1, half, 4:20]], axis=1
@@ -929,10 +1059,7 @@
             * filled
         )
     left = jnp.concatenate(pieces, axis=0)
-    key = row_iota((256, 256))
-    col = lane_iota((256, 256))
-    table = zero_one(key == (col % 16 // 8) * 128 + (col // 16) * 8 + col % 8)
-    moved = split_dot(left, table)
+    moved = split_dot(left, table_p_ref[...])
     for k in range(slots):
         parent_ref[k] = moved[16 * k : 16 * k + 16]
 
@@ -944,10 +1071,11 @@
         [par_s[after, half] * x_high for half in range(2)],
     ]
     centre = columns[1]
-    in_y = y_pair(centre, 8)
+    up, down = coarse_turns(columns)
+    in_y = coarse_y_pair(up[1], down[1])
     lane16 = lane_iota((16, LANES))
     left_rows = []
-    in_x = [coarse_x_pair(columns, 1, half) for half in range(2)]
+    in_x = [coarse_x_pair(columns, up, down, 1, half) for half in range(2)]
     blend = {}
     for half in range(2):
         for zp in range(2):
@@ -970,61 +1098,60 @@
                 pair.append(jnp.where(lane16 < 64, first, second))
             left_rows.append(jnp.concatenate(pair, axis=1))
     left = jnp.concatenate(left_rows, axis=0)
-    key = row_iota((256, 256))
-    col = lane_iota((256, 256))
-    col_y = col // 16
-    col_x = col % 16
-    target = (col_y % 2 * 2 + col_x % 2) * 64 + col_y // 2 * 8 + col_x // 2
-    spread = split_dot(left, zero_one(key == target))
+    spread = split_dot(left, table_l_ref[...])
     for yy in range(wide_y):
         for zp in range(2):
-            line = 16 * (2 * yy + zp)
-            fine_s[2 * yy, pl.ds(zp, 16, stride=2), :] = spread[line : line + 16, 0:128]
-            fine_s[2 * yy + 1, pl.ds(zp, 16, stride=2), :] = spread[line : line + 16, 128:256]
+            top = 16 * (2 * yy + zp)
+            fine_s[2 * yy, pl.ds(zp, 16, stride=2), :] = spread[top : top + 16, 0:128]
+            fine_s[2 * yy + 1, pl.ds(zp, 16, stride=2), :] = spread[top : top + 16, 128:256]
 
     line = 48 + 8 * root_tiles(sub_count, blk_count)
     lane64 = lane_iota((32, LANES))
-    row32 = row_iota((32, LANES))
     from_low = all_ref[before, line + 8 : line + 40, 0:LANES] * x_low
     low_values = all_ref[before, line + 8 : line + 40, LANES:256] * x_low
     from_high = all_ref[after, line + 8 : line + 40, 0:LANES] * x_high
     high_values = all_ref[after, line + 8 : line + 40, LANES:256] * x_high
-    low_line = all_ref[before, line : line + 8, 0:LANES] * (2.0 * f2 * x_low)
-    high_line = all_ref[after, line : line + 8, 0:LANES] * (2.0 * f2 * x_high)
-    low_line = [jnp.broadcast_to(low_line[k : k + 1], (32, LANES)) for k in range(2)]
-    high_line = [jnp.broadcast_to(high_line[k : k + 1], (32, LANES)) for k in range(2)]
-    edge_low = (
-        from_low
-        + jnp.where(row32 == 0, low_line[0], 0.0)
-        + jnp.where(row32 == 31, low_line[1], 0.0)
-    )
-    edge_high = (
-        from_high
-        + jnp.where(row32 == 0, high_line[0], 0.0)
-        + jnp.where(row32 == 31, high_line[1], 0.0)
-    )
     left = jnp.concatenate(
         [
-            jnp.where(lane64 < 64, turn(edge_low, 64, 1), f2 * low_values),
-            jnp.where(lane64 < 64, edge_high, f2 * turn(high_values, 64, 1)),
+            jnp.where(lane64 < 64, turn(from_low, 64, 1), f2 * low_values),
+            jnp.where(lane64 < 64, from_high, f2 * turn(high_values, 64, 1)),
         ],
         axis=1,
     )
-    fine_lanes = 256 * wide_y
-    key = row_iota((256, fine_lanes))
-    col = lane_iota((256, fine_lanes))
-    kind = key // 64
-    kind_x = jnp.where(kind == 0, 0, jnp.where(kind == 1, 1, jnp.where(kind == 2, 15, 14)))
-    push = split_dot(left, zero_one((key % 64 == col // 16) & (col % 16 == kind_x)))
-    push_s[...] = push
-    own_low = below(slice(16, 24), slice(0, 256)) * z_low
-    own_high = above(slice(16, 24), slice(0, 256)) * z_high
+    lane128 = lane_iota((32, LANES))
+    rows = []
+    for yy in range(wide_y):
+        rows.append(
+            jnp.where(
+                lax.rem(lane128, 64) < 16,
+                turn(left[:, 0:LANES], -16 * yy, 1),
+                turn(left[:, LANES:256], 16 - 16 * yy, 1),
+            )
+        )
+    push = split_dot(jnp.concatenate(rows, axis=0), table_x_ref[...])
+    for yy in range(wide_y):
+        push_s[:, 256 * yy : 256 * yy + 256] = push[32 * yy : 32 * yy + 32]
+    cell = lane_iota((2 * wide_y, 256)) % 16
+    across = jnp.where(
+        cell == 0, turn(all_ref[before, line : line + 2 * wide_y, :], -15, 1) * x_low, 0.0
+    ) + jnp.where(
+        cell == 15, turn(all_ref[after, line : line + 2 * wide_y, :], 15, 1) * x_high, 0.0
+    )
+    across = (2.0 * f2) * across
+    count = 2 * wide_y
     for yy in range(wide_y):
         lanes = slice(256 * yy, 256 * yy + 256)
-        push_s[0:1, lanes] = push_s[0:1, lanes] + own_low[yy : yy + 1]
-        push_s[1:2, lanes] = push_s[1:2, lanes] + f2 * own_low[wide_y + yy : wide_y + yy + 1]
-        push_s[31:32, lanes] = push_s[31:32, lanes] + own_high[yy : yy + 1]
-        push_s[30:31, lanes] = push_s[30:31, lanes] + f2 * own_high[wide_y + yy : wide_y + yy + 1]
+        push_s[0:1, lanes] = push_s[0:1, lanes] + lines_ref[yy : yy + 1] + across[yy : yy + 1]
+        push_s[1:2, lanes] = push_s[1:2, lanes] + f2 * lines_ref[wide_y + yy : wide_y + yy + 1]
+        push_s[31:32, lanes] = (
+            push_s[31:32, lanes]
+            + lines_ref[count + yy : count + yy + 1]
+            + across[wide_y + yy : wide_y + yy + 1]
+        )
+        push_s[30:31, lanes] = (
+            push_s[30:31, lanes]
+            + f2 * lines_ref[count + wide_y + yy : count + wide_y + yy + 1]
+        )
     for zz in range(2):
         for yy in range(wide_y):
             rows = slice(16 * zz, 16 * zz + 16)
@@ -1040,86 +1167,116 @@
     return [(i, i ^ step) for i in range(count)]
 
 
+def is_power(number):
+    return number > 0 and number & (number - 1) == 0
+
+
 def local(rhs, leaf_neighbors, parent_neighbors, children, owners, parent_places):
     blk_count = lax.axis_size("blk")
     sub_count = lax.axis_size("sub")
     blocks = rhs.shape[0]
     wide_y = blocks // 2
+    lists = (leaf_neighbors, parent_neighbors, children, owners, parent_places)
+    fits = 32 * blocks == 2 * LANES and 16 * sub_count in (LANES, 2 * LANES)
+    if not (fits and blk_count > 1 and is_power(blk_count)):
+        return general_local(rhs, *lists)
     blk_bits = blk_count.bit_length() - 1
     f32 = jnp.float32
     vmem = pl.BlockSpec(memory_space=pltpu.VMEM)
     smem = pl.BlockSpec(memory_space=pltpu.SMEM)
-    leaf_row = leaf_neighbors.T.reshape(1, -1)
-    parent_rows = jnp.stack([parent_neighbors.T.reshape(-1), jnp.tile(parent_places, 6)])
-    owner_rows = jnp.stack([owners, parent_places])
-    cells = jnp.concatenate([children, parent_places[:, None], owners[:, None]], axis=1)
+    params = pltpu.CompilerParams(vmem_limit_bytes=VMEM_LIMIT)
+    owner_row = owners.reshape(1, -1)
+    place_row = parent_places.reshape(1, -1)
     outs = pl.pallas_call(
         functools.partial(push_kernel, sub_count, blk_count, blk_bits),
         name="push",
         out_shape=[
             jax.ShapeDtypeStruct((blocks,), jnp.int32),
             jax.ShapeDtypeStruct((OWN_ROWS, 256), f32),
-            jax.ShapeDtypeStruct((blocks, 16, 256), f32),
-            jax.ShapeDtypeStruct((64, LANES), f32),
         ]
         + [jax.ShapeDtypeStruct((MSG_ROWS, 256), f32)] * blk_bits,
-        in_specs=[vmem] * 4,
-        out_specs=[smem] + [vmem] * (3 + blk_bits),
+        in_specs=[smem] + [vmem] * 6,
+        out_specs=[smem] + [vmem] * (1 + blk_bits),
         scratch_shapes=[
             pltpu.VMEM((blocks, 16, 256), f32),
             pltpu.VMEM((2 * wide_y, 32, LANES), f32),
             pltpu.VMEM((2 * wide_y, 32, LANES), f32),
             pltpu.VMEM((48 * wide_y, 256), f32),
-            pltpu.VMEM((64 * wide_y, 256), f32),
             pltpu.VMEM((6, 32, LANES), f32),
         ],
-    )(leaf_row, parent_rows, cells, rhs)
-    positions, own, own_part, faces = outs[:4]
-    messages = outs[4:]
+        compiler_params=params,
+    )(
+        leaf_neighbors, parent_neighbors.T, children.T, place_row, rhs,
+        jnp.asarray(octant_table()), jnp.asarray(root_table(sub_count)),
+    )
+    positions, own = outs[:2]
+    messages = outs[2:]
     received = [
         lax.ppermute(messages[d.bit_length() - 1], "blk", paired(blk_count, d))
         for d in range(1, blk_count)
     ]
+    owned, own_part, faces = pl.pallas_call(
+        functools.partial(side_kernel, sub_count, blk_count, PMOST),
+        name="side",
+        out_shape=[
+            jax.ShapeDtypeStruct((3 * PMOST,), jnp.int32),
+            jax.ShapeDtypeStruct((blocks, 16, 256), f32),
+            jax.ShapeDtypeStruct((64, LANES), f32),
+        ],
+        in_specs=[smem] + [vmem] * 4,
+        out_specs=[smem] + [vmem] * 2,
+        scratch_shapes=[
+            pltpu.VMEM((blocks, 16, 256), f32),
+            pltpu.VMEM((64 * wide_y, 256), f32),
+        ],
+        compiler_params=params,
+    )(positions, owner_row, place_row, rhs, jnp.asarray(face_table()))
     root_parts = 16 * sub_count // LANES
     joined_rows = 48 + 8 * root_tiles(sub_count, blk_count) + 8 + 32
-    joined = pl.pallas_call(
+    joined, lines = pl.pallas_call(
         functools.partial(join_kernel, sub_count, blk_count),
         name="join",
-        out_shape=jax.ShapeDtypeStruct((joined_rows, 256), f32),
+        out_shape=[
+            jax.ShapeDtypeStruct((joined_rows, 256), f32),
+            jax.ShapeDtypeStruct((4 * wide_y, 256), f32),
+        ],
         in_specs=[vmem] * (1 + blk_count),
-        out_specs=vmem,
+        out_specs=[vmem] * 2,
         scratch_shapes=[pltpu.VMEM((root_parts, 4 * blk_count + 8, LANES), f32)],
+        compiler_params=params,
     )(own, faces, *received)
     gathered = lax.all_gather(joined, "sub", axis=0, tiled=False)
-    good = jnp.min(gathered[:, joined_rows - 40, LANES])
-
-    def fast():
-        return tuple(
-            pl.pallas_call(
-                functools.partial(solve_kernel, sub_count, blk_count, PMOST),
-                name="solve",
-                out_shape=[
-                    jax.ShapeDtypeStruct((blocks, 16, 256), f32),
-                    jax.ShapeDtypeStruct((PMOST, 16, 256), f32),
-                ],
-                in_specs=[smem] + [vmem] * (4 + blk_count - 1),
-                out_specs=[vmem] * 2,
-                scratch_shapes=[
-                    pltpu.VMEM((blocks, 16, 256), f32),
-                    pltpu.VMEM((sub_count, 2, 24, LANES), f32),
-                    pltpu.VMEM((root_parts, 4 * blk_count + 8, LANES), f32),
-                    pltpu.VMEM((2 * wide_y, 32, LANES), f32),
-                    pltpu.VMEM((32, 256 * wide_y), f32),
-                ],
-            )(positions, owner_rows, cells, gathered, own_part, *received)
-        )
-
-    def general():
-        return general_local(
-            rhs, leaf_neighbors, parent_neighbors, children, owners, parent_places
-        )
-
-    return lax.cond(good > 0.5, fast, general)
+    leaf_solution, parent_solution, good = pl.pallas_call(
+        functools.partial(solve_kernel, sub_count, blk_count, PMOST),
+        name="solve",
+        out_shape=[
+            jax.ShapeDtypeStruct((blocks, 16, 256), f32),
+            jax.ShapeDtypeStruct((PMOST, 16, 256), f32),
+            jax.ShapeDtypeStruct((1,), jnp.int32),
+        ],
+        in_specs=[smem] * 2 + [vmem] * 7,
+        out_specs=[vmem] * 2 + [smem],
+        scratch_shapes=[
+            pltpu.VMEM((blocks, 16, 256), f32),
+            pltpu.VMEM((sub_count, 2, 24, LANES), f32),
+            pltpu.VMEM((root_parts, 4 * blk_count + 8, LANES), f32),
+            pltpu.VMEM((2 * wide_y, 32, LANES), f32),
+            pltpu.VMEM((32, 256 * wide_y), f32),
+        ],
+        compiler_params=params,
+    )(
+        positions, owned, gathered, own_part, lines,
+        jnp.asarray(root_spread_table(sub_count)), jnp.asarray(parent_table()),
+        jnp.asarray(leaf_table_of_cells()), jnp.asarray(push_table()),
+    )
+
+    def general(state):
+        return (*general_local(rhs, *lists), jnp.ones_like(state[2]))
+
+    state = lax.while_loop(
+        lambda state: state[2][0] == 0, general, (leaf_solution, parent_solution, good)
+    )
+    return state[0], state[1]
 
 
 def solution(mesh):

time: 36.9 us -> 32.3 us (0.88)
  local copies, waits for them, and re-layouts: 5.89 us -> 3.78 us
  other arithmetic: 1.29 us -> 0 us
  waiting for transfers between devices: 3.66 us -> 2.74 us
  loops' own time: 0.24 us -> 0.78 us
  between operations: 1.35 us -> 0.92 us
    unnamed x13 -> x26, local copies, waits for them, and re-layouts: 1.48 us -> 3.78 us
    another operation x3 -> x0, local copies, waits for them, and re-layouts: 1.5 us -> none  [the longest x2 0.84 us: local(): jnp.stack([parent_neighbors.T.reshape(-1), jnp.tile(parent_places, 6)])]
    pallas_call x1 -> x2, Pallas kernels: 3.07 us -> 4.56 us  [the longest x1 2.92 us: local(): pl.pallas_call(functools.partial(solve_kernel, sub_count, blk_count, PMOS...]
    pallas_call x1, Pallas kernels: 1.52 us -> 0.04 us  [local(): pl.pallas_call(functools.partial(join_kernel, sub_count, blk_count), name...]
    broadcast_in_dim x2 -> x0, local copies, waits for them, and re-layouts: 1.47 us -> none  [the longest x1 0.74 us: local(): parent_places[:, None]]
    ppermute x3, waiting for transfers between devices: 3.66 us -> 2.74 us  [local(): lax.ppermute(messages[d.bit_length() - 1], 'blk', paired(blk_count, d))]
    transpose x1 -> x0, local copies, waits for them, and re-layouts: 0.77 us -> none  [local(): leaf_row = leaf_neighbors.T.reshape(1, -1)]
    reshape x1 -> x0, local copies, waits for them, and re-layouts: 0.67 us -> none  [local(): leaf_row = leaf_neighbors.T.reshape(1, -1)]
  transfers between devices with their start and end apart: 3 -> 3, of which waited for: 2 -> 2; matrix products, arithmetic and copies ran while one was open for 0% -> 0% of each run, Pallas kernels for 0% -> 5%
where the time goes in v2:
time: 32.3 us; the launch traced here: 32 us
  blocking collectives  10.5 us (33%)
  Pallas kernels  7.5 us (23%)
  starting transfers between devices  5.71 us (18%)
  local copies, waits for them, and re-layouts  3.78 us (12%)
  waiting for transfers between devices  2.74 us (8%)
  between operations  0.92 us (3%)
  loops' own time  0.78 us (2%)
    all_gather x1, blocking collectives, local(): gathered = lax.all_gather(joined, 'sub', axis=0, tiled=False)  10.5 us
    ppermute x3, starting transfers between devices, local(): lax.ppermute(messages[d.bit_length() - 1], 'blk', paired(blk_count, d))  5.71 us
    unnamed x26, local copies, waits for them, and re-layouts  3.78 us
    pallas_call x1, Pallas kernels, local(): pl.pallas_call(functools.partial(solve_kernel, sub_count, blk_count, PMOS...  2.92 us
    pallas_call x1, Pallas kernels, local(): pl.pallas_call(functools.partial(push_kernel, sub_count, blk_count, blk_b...  2.9 us
    ppermute x3, waiting for transfers between devices, local(): lax.ppermute(messages[d.bit_length() - 1], 'blk', paired(blk_count, d))  2.74 us
    pallas_call x1, Pallas kernels, local(): pl.pallas_call(functools.partial(side_kernel, sub_count, blk_count, PMOST...  1.64 us
    another operation x1, loops' own time, local(): lax.while_loop(lambda state: state[2][0] == 0, general, (leaf_solution, p...  0.78 us
  transfers between devices with their start and end apart: 3, of which 2 were waited for; matrix products, arithmetic and copies ran while one was open for 0% of the time, Pallas kernels for 5%

profile of v2, /device:TPU:0, one launch (start us, length us, event | category | flops | bytes accessed | tf_op | source)
XLA Modules:
  0.0 32.0 jit_solution(6210756788599394775)
XLA Ops:
  0.6 0.0 copy-start.8
  0.6 0.0 copy-start.13
  0.6 0.7 %copy-done.8 = s32[8,6]{1,0:T(8,128)S(1)} copy-done((s32[8,6]{1,0:T(8,128)S(1)}, s32[8,6]{1,0:T(8,128)}, u32[]{:S(2)}) %copy-start.8) | copy-done | bytes 216
  1.3 0.0 copy-done.13
  1.3 0.9 %copy-done.2 = bf16[512,128]{1,0:T(8,128)(2,1)S(1)} copy-done((bf16[512,128]{1,0:T(8,128)(2,1)S(1)}, bf16[512,128]{1,0:T(8,128)(2,1)}, u32[]{:S(2)}) %copy-start.2) | copy-done | bytes 131096
  2.2 0.8 %copy-done.6 = bf16[256,128]{1,0:T(8,128)(2,1)S(1)} copy-done((bf16[256,128]{1,0:T(8,128)(2,1)S(1)}, bf16[256,128]{1,0:T(8,128)(2,1)}, u32[]{:S(2)}) %copy-start.6) | copy-done | bytes 65560
  3.1 2.9 %push.1 = (s32[8]{0:T(128)S(1)}, f32[64,256]{1,0:T(8,128)S(1)}, f32[32,256]{1,0:T(8,128)S(1)}, f32[32,256]{1,0:T(8,128)S(1)}) custom-call(s32[8,6]{1,0:T(8,128)S(1)} %copy-done.8, s32[6,32]{1,0:T(8,128)} %bitcast.158, s32[8,32]{1,0:T(8,128)} %bitcast.159, s32[1,32]{1,0:T(1,128)S(1)} %bitcast.161, f32[8,16,256]{2,1,0:T(8,128)} %rhs_ref.3, ...), custom_call_target="tpu_custom_call" | custom-call | tf_op jit(solution)/shard_map/push/pallas_call | solution.py:1190
  6.0 3.1 %collective-permute-start.18 = (f32[32,256]{1,0:T(8,128)S(1)}, f32[32,256]{1,0:T(8,128)S(1)}, u32[]{:S(2)}, u32[]{:S(2)}) collective-permute-start(f32[32,256]{1,0:T(8,128)S(1)} %get-tuple-element.75), channel_id=1, source_target_pairs={{0,8},{8,0},{16,24},{24,16},{1,9},{9,1},{17,25},{25,17},{2,10},{10... | collective-permute-start | bytes 98312 | tf_op jit(solution)/shard_map/ppermute | solution.py:1215
  9.1 2.5 %collective-permute-start.20 = (f32[32,256]{1,0:T(8,128)S(1)}, f32[32,256]{1,0:T(8,128)S(1)}, u32[]{:S(2)}, u32[]{:S(2)}) collective-permute-start(f32[32,256]{1,0:T(8,128)S(1)} %get-tuple-element.76), channel_id=1, source_target_pairs={{0,24},{8,16},{16,8},{24,0},{1,25},{9,17},{17,9},{25,1},{2,26},{10... | collective-permute-start | bytes 98312 | tf_op jit(solution)/shard_map/ppermute | solution.py:1215
  11.6 0.1 collective-permute-start.19
  11.7 0.6 %copy-done.11 = s32[32]{0:T(128)S(1)} copy-done((s32[32]{0:T(128)S(1)}, s32[32]{0:T(128)}, u32[]{:S(2)}) %copy-start.11) | copy-done | bytes 152
  12.3 1.6 %side.1 = (s32[9]{0:T(128)S(1)}, f32[8,16,256]{2,1,0:T(8,128)S(1)}, f32[64,128]{1,0:T(8,128)S(1)}) custom-call(s32[8]{0:T(128)S(1)} %get-tuple-element.71.positions, s32[1,32]{1,0:T(1,128)S(1)} %bitcast.160, s32[1,32]{1,0:T(1,128)S(1)} %bitcast.162, f32[8,16,256]{2,1,0:T(8,128)S(1)} %copy-done.7, bf16[256,128]{1,0:T(8,128)(2,1)S(1)} %copy-done.5), custom_call_target="tpu_custom_call" | custom-call | tf_op jit(solution)/shard_map/side/pallas_call | solution.py:1218
  14.0 0.0 collective-permute-done.18.rest_0_
  14.0 1.3 %collective-permute-done.20.rest_2_ = f32[32,256]{1,0:T(8,128)S(1)} collective-permute-done((f32[32,256]{1,0:T(8,128)S(1)}, f32[32,256]{1,0:T(8,128)S(1)}, u32[]{:S(2)}, u32[]{:S(2)}) %collective-permute-start.20) | collective-permute-done | bytes 32800 | tf_op jit(solution)/shard_map/ppermute | solution.py:1215
  15.3 1.5 %collective-permute-done.19.rest_1_ = f32[32,256]{1,0:T(8,128)S(1)} collective-permute-done((f32[32,256]{1,0:T(8,128)S(1)}, f32[32,256]{1,0:T(8,128)S(1)}, u32[]{:S(2)}, u32[]{:S(2)}) %collective-permute-start.19) | collective-permute-done | bytes 32800 | tf_op jit(solution)/shard_map/ppermute | solution.py:1215
  16.8 0.0 copy-start.1
  16.8 0.0 copy-start.3
  16.8 0.0 copy-start.4
  16.8 10.5 %all-gather = f32[768,256]{1,0:T(8,128)S(1)} all-gather(f32[96,256]{1,0:T(8,128)S(1)} %get-tuple-element.77), channel_id=2, replica_groups=mesh['blk'=4,'sub'=8] {'sub'}, dimensions={0}, use_global_device_ids=true | all-gather | bytes 884736 | tf_op jit(solution)/shard_map/all_gather | solution.py:1248
  27.4 0.0 copy-start.10
  27.4 2.9 %solve.1 = (f32[8,16,256]{2,1,0:T(8,128)}, f32[3,16,256]{2,1,0:T(8,128)}, s32[1]{0:T(128)}) custom-call(s32[8]{0:T(128)S(1)} %get-tuple-element.71.positions, s32[9]{0:T(128)S(1)} %get-tuple-element.72.owned, f32[8,96,256]{2,1,0:T(8,128)S(1)} %bitcast.147, f32[8,16,256]{2,1,0:T(8,128)S(1)} %get-tuple-element.78.part_ref, ...), custom_call_target="tpu_custom_call" | custom-call | tf_op jit(solution)/shard_map/solve/pallas_call | solution.py:1249
  30.3 0.0 copy-start.9
  30.3 0.7 %copy-done.9 = s32[32,6]{0,1:T(8,128)S(1)} copy-done((s32[32,6]{0,1:T(8,128)S(1)}, s32[32,6]{0,1:T(8,128)}, u32[]{:S(2)}) %copy-start.9) | copy-done | bytes 792
  31.0 0.8 %while.13 = (f32[8,16,256]{2,1,0:T(8,128)}, f32[3,16,256]{2,1,0:T(8,128)}, s32[1]{0:T(128)}, f32[8,16,256]{2,1,0:T(8,128)S(1)}, s32[8,6]{1,0:T(8,128)S(1)}, /*in...) while((f32[8,16,256]{2,1,0:T(8,128)}, ...), condition=%region_9.12_spmd.clone.clone, body=%region_0.11_spmd.sunk.clone.clone | while | flops 309503840 | bytes 22816824 | solution.py:1276
  (14 shorter events, 0.1 us)
Async XLA Ops:
  0.6 0.7 %copy-start.8 = (s32[8,6]{1,0:T(8,128)S(1)}, s32[8,6]{1,0:T(8,128)}, u32[]{:S(2)}) copy-start(s32[8,6]{1,0:T(8,128)} %leaf_ref.1) | copy-start | bytes 580
  0.6 0.7 %copy-start.13 = (s32[32]{0:T(128)S(1)}, s32[32]{0:T(128)}, u32[]{:S(2)}) copy-start(s32[32]{0:T(128)} %param.26) | copy-start | bytes 388
  1.3 0.9 %copy-start.2 = (bf16[512,128]{1,0:T(8,128)(2,1)S(1)}, bf16[512,128]{1,0:T(8,128)(2,1)}, u32[]{:S(2)}) copy-start(bf16[512,128]{1,0:T(8,128)(2,1)} %constant.456.clone.table_r_ref) | copy-start | bytes 393220
  2.2 0.8 %copy-start.6 = (bf16[256,128]{1,0:T(8,128)(2,1)S(1)}, bf16[256,128]{1,0:T(8,128)(2,1)}, u32[]{:S(2)}) copy-start(bf16[256,128]{1,0:T(8,128)(2,1)} %constant.455.clone.table_a_ref) | copy-start | bytes 196612
  3.1 8.6 %copy-start.5 = (bf16[256,128]{1,0:T(8,128)(2,1)S(1)}, bf16[256,128]{1,0:T(8,128)(2,1)}, u32[]{:S(2)}) copy-start(bf16[256,128]{1,0:T(8,128)(2,1)} %constant.457.clone.table_ref) | copy-start | bytes 196612
  3.1 8.6 %copy-start.7 = (f32[8,16,256]{2,1,0:T(8,128)S(1)}, f32[8,16,256]{2,1,0:T(8,128)}, u32[]{:S(2)}) copy-start(f32[8,16,256]{2,1,0:T(8,128)} %rhs_ref.3) | copy-start | bytes 393220
  6.0 8.0 %collective-permute-start.18 = (f32[32,256]{1,0:T(8,128)S(1)}, f32[32,256]{1,0:T(8,128)S(1)}, u32[]{:S(2)}, u32[]{:S(2)}) collective-permute-start(f32[32,256]{1,0:T(8,128)S(1)} %get-tuple-element.75), channel_id=1, source_target_pairs={{0,8},{8,0},{16,24},{24,16},{1,9},{9,1},{17,25},{25,17},{2,10},{10... | collective-permute-start | bytes 98312 | tf_op jit(solution)/shard_map/ppermute | solution.py:1215
  9.1 6.2 %collective-permute-start.20 = (f32[32,256]{1,0:T(8,128)S(1)}, f32[32,256]{1,0:T(8,128)S(1)}, u32[]{:S(2)}, u32[]{:S(2)}) collective-permute-start(f32[32,256]{1,0:T(8,128)S(1)} %get-tuple-element.76), channel_id=1, source_target_pairs={{0,24},{8,16},{16,8},{24,0},{1,25},{9,17},{17,9},{25,1},{2,26},{10... | collective-permute-start | bytes 98312 | tf_op jit(solution)/shard_map/ppermute | solution.py:1215
  11.6 5.2 %collective-permute-start.19 = (f32[32,256]{1,0:T(8,128)S(1)}, f32[32,256]{1,0:T(8,128)S(1)}, u32[]{:S(2)}, u32[]{:S(2)}) collective-permute-start(f32[32,256]{1,0:T(8,128)S(1)} %get-tuple-element.76), channel_id=1, source_target_pairs={{0,16},{8,24},{16,0},{24,8},{1,17},{9,25},{17,1},{25,9},{2,18},{10... | collective-permute-start | bytes 98312 | tf_op jit(solution)/shard_map/ppermute | solution.py:1215
  11.7 0.7 %copy-start.11 = (s32[32]{0:T(128)S(1)}, s32[32]{0:T(128)}, u32[]{:S(2)}) copy-start(s32[32]{0:T(128)} %param.25) | copy-start | bytes 388
  16.8 10.6 %copy-start = (bf16[256,256]{1,0:T(8,128)(2,1)S(1)}, bf16[256,256]{1,0:T(8,128)(2,1)}, u32[]{:S(2)}) copy-start(bf16[256,256]{1,0:T(8,128)(2,1)} %constant.460.clone.table_l_ref) | copy-start | bytes 393220
  16.8 10.6 %copy-start.1 = (bf16[256,256]{1,0:T(8,128)(2,1)S(1)}, bf16[256,256]{1,0:T(8,128)(2,1)}, u32[]{:S(2)}) copy-start(bf16[256,256]{1,0:T(8,128)(2,1)} %constant.459.clone.table_p_ref) | copy-start | bytes 393220
  16.8 10.6 %copy-start.3 = (bf16[128,256]{1,0:T(8,128)(2,1)S(1)}, bf16[128,256]{1,0:T(8,128)(2,1)}, u32[]{:S(2)}) copy-start(bf16[128,256]{1,0:T(8,128)(2,1)} %constant.461.clone.table_x_ref) | copy-start | bytes 196612
  16.8 10.6 %copy-start.4 = (bf16[128,256]{1,0:T(8,128)(2,1)S(1)}, bf16[128,256]{1,0:T(8,128)(2,1)}, u32[]{:S(2)}) copy-start(bf16[128,256]{1,0:T(8,128)(2,1)} %constant.458.clone.table_w_ref) | copy-start | bytes 196612
  27.4 3.0 %copy-start.10 = (s32[32,8]{0,1:T(8,128)S(1)}, s32[32,8]{0,1:T(8,128)}, u32[]{:S(2)}) copy-start(s32[32,8]{0,1:T(8,128)} %param.24) | copy-start | bytes 3076
  30.3 0.7 %copy-start.9 = (s32[32,6]{0,1:T(8,128)S(1)}, s32[32,6]{0,1:T(8,128)}, u32[]{:S(2)}) copy-start(s32[32,6]{0,1:T(8,128)} %param.23) | copy-start | bytes 2308

commit v3 on v2

--- a/solution.py
+++ b/solution.py
@@ -387,35 +387,12 @@
     return np.arange(rows)[:, None], np.arange(columns)[None, :]
 
 
-def octant_table():
-    key, col = key_col(256, LANES)
-    key_x = key % 16
-    col_x = col % 8
-    return zero_one(
-        (key // 32 == col % 64 // 8)
-        & (
-            ((col < 64) & (key_x // 2 == col_x))
-            | ((col >= 64) & (col_x == 7) & (key_x == 0))
-            | ((col >= 64) & (col_x == 0) & (key_x == 15))
-        ),
-        0.5,
-    )
-
-
 def face_table():
     key, col = key_col(256, LANES)
     return zero_one(
         (key // 16 == col % 64)
         & (((col < 64) & (key % 16 == 0)) | ((col >= 64) & (key % 16 == 15)))
     )
-
-
-def root_table(sub_count):
-    key, col = key_col(4 * LANES, 16 * sub_count)
-    near_x = key % 8 // 4
-    row = (key // LANES) % 2 * 4 + key % LANES // 32
-    along = np.where(key < 256, near_x + 1, np.where(near_x == 0, 3, 0))
-    return zero_one(col == row * (2 * sub_count) + along, 0.25)
 
 
 def root_spread_table(sub_count):
@@ -527,20 +504,41 @@
     return sums
 
 
+def power_div(values, divisor):
+    return lax.shift_right_logical(values, jnp.full_like(values, divisor.bit_length() - 1))
+
+
+def power_rem(values, divisor):
+    return values & (divisor - 1)
+
+
+def octant_table():
+    key = row_iota((256, LANES))
+    col = lane_iota((256, LANES))
+    key_x = power_rem(key, 16)
+    col_x = power_rem(col, 8)
+    side_x = jnp.where(col_x == 7, 0, jnp.where(col_x == 0, 15, 16))
+    right_x = jnp.where(col < 64, power_div(key_x, 2) - col_x, key_x - side_x)
+    right_y = power_div(key, 32) - power_div(power_rem(col, 64), 8)
+    return jnp.where((right_x | right_y) == 0, 0.5, 0.0).astype(jnp.bfloat16)
+
+
+def root_table(sub_count):
+    shape = (4 * LANES, 16 * sub_count)
+    key = row_iota(shape)
+    near_x = power_div(power_rem(key, 8), 4)
+    row = power_div(power_rem(key, 256), 32)
+    along = jnp.where(key < 256, near_x + 1, 3 - 3 * near_x)
+    target = row * (2 * sub_count) + along
+    return jnp.where(lane_iota(shape) == target, 0.25, 0.0).astype(jnp.bfloat16)
+
+
 def as_column(row):
     count = row.shape[1]
     shape = (count, count)
     return jnp.sum(
         jnp.where(row_iota(shape) == lane_iota(shape), row, 0.0), axis=1, keepdims=True
     )
-
-
-def power_div(values, divisor):
-    return lax.shift_right_logical(values, jnp.full_like(values, divisor.bit_length() - 1))
-
-
-def power_rem(values, divisor):
-    return values & (divisor - 1)
 
 
 def grid_codes(sub_count, wide_y, child_ref, place_ref):
@@ -562,6 +560,12 @@
         jnp.sum(jnp.where(child_ref[...] == first + slot, codes, 0.0)).astype(jnp.int32)
         for slot in range(blocks)
     ]
+
+
+def own_position(sub_count, wide_y, code):
+    return lax.rem(lax.div(code, wide_y * sub_count), 2) * wide_y + lax.rem(
+        lax.div(code, sub_count), wide_y
+    )
 
 
 def lists_agree(sub_count, blk_count, leaf_ref, parent_ref, child_ref, place_ref, codes, own):
@@ -651,26 +655,41 @@
 
 def push_kernel(
     sub_count, blk_count, blk_bits,
-    leaf_ref, parent_ref, child_ref, place_ref, rhs_ref, table_a_ref, table_r_ref,
-    position_ref, own_ref, *rest
+    leaf_hbm, parent_hbm, child_hbm, place_hbm, owner_hbm, rhs_hbm,
+    placed, own_ref, leaf_out, parent_ref, child_ref, place_ref, owner_out, *rest
 ):
     msg_refs = rest[:blk_bits]
-    placed, rows_s, rows_g, left_a, coarse_s = rest[blk_bits:]
+    leaf_ref, rhs_ref, rows_s, rows_g, left_a, coarse_s, sems = rest[blk_bits:]
+    copies = [
+        pltpu.make_async_copy(source, target, sems.at[k])
+        for k, (source, target) in enumerate(
+            (
+                (child_hbm, child_ref),
+                (place_hbm, place_ref),
+                (rhs_hbm, rhs_ref),
+                (leaf_hbm, leaf_ref),
+                (parent_hbm, parent_ref),
+                (leaf_hbm, leaf_out),
+                (owner_hbm, owner_out),
+            )
+        )
+    ]
+    for copy in copies:
+        copy.start()
+    table_a = octant_table()
+    table_r = root_table(sub_count)
     blocks = rhs_ref.shape[0]
     wide_y = blocks // 2
     f = FACTOR
     f2 = f * f
     sub_here, blk_here, x_low, x_high, z_low, z_high = limits(sub_count, blk_count)
+    copies[0].wait()
+    copies[1].wait()
     codes = grid_codes(sub_count, wide_y, child_ref, place_ref)
     own_code = own_codes(sub_count, blocks, child_ref, codes, sub_here, blk_here)
-    layer = wide_y * sub_count
+    copies[2].wait()
     for slot in range(blocks):
-        code = own_code[slot]
-        position = lax.rem(lax.div(code, layer), 2) * wide_y + lax.rem(
-            lax.div(code, sub_count), wide_y
-        )
-        position_ref[slot] = position
-        placed[position] = rhs_ref[slot]
+        placed[own_position(sub_count, wide_y, own_code[slot])] = rhs_ref[slot]
     s = placed_chunks(placed, wide_y)
     shape = s[0].shape
     top = shape[0] - 1
@@ -707,7 +726,9 @@
         left_a[line + 24 : line + 40, half] = (
             rows_g[k, pl.ds(0, 16, stride=2), :] + rows_g[k, pl.ds(1, 16, stride=2), :]
         )
-    out_a = split_dot(left_a[...], table_a_ref[...])
+    for copy in copies[3:]:
+        copy.wait()
+    out_a = split_dot(left_a[...], table_a)
     good = lists_agree(
         sub_count, blk_count, leaf_ref, parent_ref, child_ref, place_ref, codes, own_code
     )
@@ -765,7 +786,7 @@
     outer = [jnp.where(low_cells, pieces[4 + h], pieces[h]) for h in range(2)]
     root_left = jnp.concatenate([pieces[2], pieces[3]] + outer, axis=1)
     root_lanes = 16 * sub_count
-    root_part = split_dot(root_left, table_r_ref[...])
+    root_part = split_dot(root_left, table_r)
     root_part = pltpu.roll(root_part, 2 * sub_here + root_lanes - 1, 1)
     root_part = jnp.where(row_iota(root_part.shape) < 6, root_part, 0.0)
     own_ref[48:56, 0:root_lanes] = root_part
@@ -788,17 +809,19 @@
 
 def side_kernel(
     sub_count, blk_count, slots,
-    positions, owner_ref, place_ref, rhs_ref, table_ref,
-    slot_ref, part_ref, faces_ref,
-    placed, left_c
+    child_ref, owner_ref, place_ref, placed, table_ref,
+    position_ref, slot_ref, part_ref, faces_ref,
+    left_c
 ):
-    blocks = rhs_ref.shape[0]
+    blocks = placed.shape[0]
     wide_y = blocks // 2
     f = FACTOR
     f2 = f * f
     sub_here, blk_here, x_low, x_high, z_low, z_high = limits(sub_count, blk_count)
+    codes = grid_codes(sub_count, wide_y, child_ref, place_ref)
+    own_code = own_codes(sub_count, blocks, child_ref, codes, sub_here, blk_here)
     for slot in range(blocks):
-        placed[positions[slot]] = rhs_ref[slot]
+        position_ref[slot] = own_position(sub_count, wide_y, own_code[slot])
     s = placed_chunks(placed, wide_y)
     back = return_gain(s[0].shape, x_low, x_high, z_low, z_high)
     sx, sy, sz = fine_beside(s)
@@ -1187,50 +1210,62 @@
     params = pltpu.CompilerParams(vmem_limit_bytes=VMEM_LIMIT)
     owner_row = owners.reshape(1, -1)
     place_row = parent_places.reshape(1, -1)
+    child_rows = children.T
+    parent_rows = parent_neighbors.T
+    grid_shape = (blocks, 16, 256)
     outs = pl.pallas_call(
         functools.partial(push_kernel, sub_count, blk_count, blk_bits),
         name="push",
         out_shape=[
-            jax.ShapeDtypeStruct((blocks,), jnp.int32),
+            jax.ShapeDtypeStruct(grid_shape, f32),
             jax.ShapeDtypeStruct((OWN_ROWS, 256), f32),
         ]
+        + [
+            jax.ShapeDtypeStruct(array.shape, jnp.int32)
+            for array in (leaf_neighbors, parent_rows, child_rows, place_row, owner_row)
+        ]
         + [jax.ShapeDtypeStruct((MSG_ROWS, 256), f32)] * blk_bits,
-        in_specs=[smem] + [vmem] * 6,
-        out_specs=[smem] + [vmem] * (1 + blk_bits),
+        in_specs=[pl.BlockSpec(memory_space=pltpu.HBM)] * 6,
+        out_specs=[vmem] * (7 + blk_bits),
         scratch_shapes=[
-            pltpu.VMEM((blocks, 16, 256), f32),
+            pltpu.SMEM(leaf_neighbors.shape, jnp.int32),
+            pltpu.VMEM(grid_shape, f32),
             pltpu.VMEM((2 * wide_y, 32, LANES), f32),
             pltpu.VMEM((2 * wide_y, 32, LANES), f32),
             pltpu.VMEM((48 * wide_y, 256), f32),
             pltpu.VMEM((6, 32, LANES), f32),
+            pltpu.SemaphoreType.DMA((7,)),
         ],
         compiler_params=params,
     )(
-        leaf_neighbors, parent_neighbors.T, children.T, place_row, rhs,
-        jnp.asarray(octant_table()), jnp.asarray(root_table(sub_count)),
-    )
-    positions, own = outs[:2]
-    messages = outs[2:]
+        *(
+            pltpu.with_memory_space_constraint(array, pltpu.HBM)
+            for array in (leaf_neighbors, parent_rows, child_rows, place_row, owner_row, rhs)
+        )
+    )
+    placed, own, leaf_neighbors, parent_rows, child_rows, place_row, owner_row = outs[:7]
+    messages = outs[7:]
+    lists = (
+        leaf_neighbors, parent_rows.T, child_rows.T, owner_row.reshape(-1), place_row.reshape(-1),
+    )
     received = [
         lax.ppermute(messages[d.bit_length() - 1], "blk", paired(blk_count, d))
         for d in range(1, blk_count)
     ]
-    owned, own_part, faces = pl.pallas_call(
+    positions, owned, own_part, faces = pl.pallas_call(
         functools.partial(side_kernel, sub_count, blk_count, PMOST),
         name="side",
         out_shape=[
+            jax.ShapeDtypeStruct((blocks,), jnp.int32),
             jax.ShapeDtypeStruct((3 * PMOST,), jnp.int32),
-            jax.ShapeDtypeStruct((blocks, 16, 256), f32),
+            jax.ShapeDtypeStruct(grid_shape, f32),
             jax.ShapeDtypeStruct((64, LANES), f32),
         ],
-        in_specs=[smem] + [vmem] * 4,
-        out_specs=[smem] + [vmem] * 2,
-        scratch_shapes=[
-            pltpu.VMEM((blocks, 16, 256), f32),
-            pltpu.VMEM((64 * wide_y, 256), f32),
-        ],
+        in_specs=[vmem] * 5,
+        out_specs=[smem] * 2 + [vmem] * 2,
+        scratch_shapes=[pltpu.VMEM((64 * wide_y, 256), f32)],
         compiler_params=params,
-    )(positions, owner_row, place_row, rhs, jnp.asarray(face_table()))
+    )(child_rows, owner_row, place_row, placed, jnp.asarray(face_table()))
     root_parts = 16 * sub_count // LANES
     joined_rows = 48 + 8 * root_tiles(sub_count, blk_count) + 8 + 32
     joined, lines = pl.pallas_call(

time: 32.3 us -> 28.5 us (0.88)
  local copies, waits for them, and re-layouts: 3.78 us -> 0.04 us
  waiting for transfers between devices: 2.74 us -> 3.9 us
  Pallas kernels: 7.5 us -> 6.5 us
    unnamed x26 -> x12, local copies, waits for them, and re-layouts: 3.78 us -> 0.04 us
    ppermute x3, waiting for transfers between devices: 2.74 us -> 3.9 us  [local(): lax.ppermute(messages[d.bit_length() - 1], 'blk', paired(blk_count, d))]
    pallas_call x1, Pallas kernels: 1.64 us -> 1.13 us  [local(): pl.pallas_call(functools.partial(side_kernel, sub_count, blk_count, PMOST...]
    pallas_call x1, Pallas kernels: 2.9 us -> 2.4 us  [local(): pl.pallas_call(functools.partial(push_kernel, sub_count, blk_count, blk_b...]
  transfers between devices with their start and end apart: 3 -> 3, of which waited for: 2 -> 2; matrix products, arithmetic and copies ran while one was open for 0% -> 0% of each run, Pallas kernels for 5% -> 4%
where the time goes in v3:
time: 28.5 us; the launch traced here: 28.4 us
  blocking collectives  10.5 us (37%)
  Pallas kernels  6.5 us (23%)
  starting transfers between devices  5.71 us (20%)
  waiting for transfers between devices  3.9 us (14%)
  between operations  0.9 us (3%)
  loops' own time  0.79 us (3%)
    all_gather x1, blocking collectives, local(): gathered = lax.all_gather(joined, 'sub', axis=0, tiled=False)  10.5 us
    ppermute x3, starting transfers between devices, local(): lax.ppermute(messages[d.bit_length() - 1], 'blk', paired(blk_count, d))  5.71 us
    ppermute x3, waiting for transfers between devices, local(): lax.ppermute(messages[d.bit_length() - 1], 'blk', paired(blk_count, d))  3.9 us
    pallas_call x1, Pallas kernels, local(): pl.pallas_call(functools.partial(solve_kernel, sub_count, blk_count, PMOS...  2.92 us
    pallas_call x1, Pallas kernels, local(): pl.pallas_call(functools.partial(push_kernel, sub_count, blk_count, blk_b...  2.4 us
    pallas_call x1, Pallas kernels, local(): pl.pallas_call(functools.partial(side_kernel, sub_count, blk_count, PMOST...  1.13 us
    another operation x1, loops' own time, local(): lax.while_loop(lambda state: state[2][0] == 0, general, (leaf_solution, p...  0.79 us
  transfers between devices with their start and end apart: 3, of which 2 were waited for; matrix products, arithmetic and copies ran while one was open for 0% of the time, Pallas kernels for 4%

profile of v3, /device:TPU:0, one launch (start us, length us, event | category | flops | bytes accessed | tf_op | source)
XLA Modules:
  0.0 28.4 jit_solution(2958811248106595539)
XLA Ops:
  0.6 0.0 copy-start.4
  0.6 2.4 %push.1 = (f32[8,16,256]{2,1,0:T(8,128)S(1)}, f32[64,256]{1,0:T(8,128)S(1)}, s32[8,6]{1,0:T(8,128)S(1)}, s32[6,32]{1,0:T(8,128)S(1)}, s32[8,32]{1,0:T(8,128)S(1)...) custom-call(s32[8,6]{1,0:T(8,128)} %leaf_hbm.1, ...), custom_call_target="tpu_custom_call" | custom-call | tf_op jit(solution)/shard_map/push/pallas_call | solution.py:1216
  3.1 3.1 %collective-permute-start.18 = (f32[32,256]{1,0:T(8,128)S(1)}, f32[32,256]{1,0:T(8,128)S(1)}, u32[]{:S(2)}, u32[]{:S(2)}) collective-permute-start(f32[32,256]{1,0:T(8,128)S(1)} %get-tuple-element.90), channel_id=1, source_target_pairs={{0,8},{8,0},{16,24},{24,16},{1,9},{9,1},{17,25},{25,17},{2,10},{10... | collective-permute-start | bytes 98312 | tf_op jit(solution)/shard_map/ppermute | solution.py:1252
  6.2 2.5 %collective-permute-start.20 = (f32[32,256]{1,0:T(8,128)S(1)}, f32[32,256]{1,0:T(8,128)S(1)}, u32[]{:S(2)}, u32[]{:S(2)}) collective-permute-start(f32[32,256]{1,0:T(8,128)S(1)} %get-tuple-element.91), channel_id=1, source_target_pairs={{0,24},{8,16},{16,8},{24,0},{1,25},{9,17},{17,9},{25,1},{2,26},{10... | collective-permute-start | bytes 98312 | tf_op jit(solution)/shard_map/ppermute | solution.py:1252
  8.6 0.1 collective-permute-start.19
  8.8 0.0 copy-done.4
  8.8 1.1 %side.1 = (s32[8]{0:T(128)S(1)}, s32[9]{0:T(128)S(1)}, f32[8,16,256]{2,1,0:T(8,128)S(1)}, f32[64,128]{1,0:T(8,128)S(1)}) custom-call(s32[8,32]{1,0:T(8,128)S(1)} %get-tuple-element.82.child_ref, s32[1,32]{1,0:T(1,128)S(1)} %get-tuple-element.344.owner_ref, s32[1,32]{1,0:T(1,128)S(1)} %get-tuple-element.84.place_ref, ...), custom_call_target="tpu_custom_call" | custom-call | tf_op jit(solution)/shard_map/side/pallas_call | solution.py:1255
  9.9 0.0 collective-permute-done.18.rest_0_
  9.9 2.4 %collective-permute-done.20.rest_2_ = f32[32,256]{1,0:T(8,128)S(1)} collective-permute-done((f32[32,256]{1,0:T(8,128)S(1)}, f32[32,256]{1,0:T(8,128)S(1)}, u32[]{:S(2)}, u32[]{:S(2)}) %collective-permute-start.20) | collective-permute-done | bytes 32800 | tf_op jit(solution)/shard_map/ppermute | solution.py:1252
  12.3 1.5 %collective-permute-done.19.rest_1_ = f32[32,256]{1,0:T(8,128)S(1)} collective-permute-done((f32[32,256]{1,0:T(8,128)S(1)}, f32[32,256]{1,0:T(8,128)S(1)}, u32[]{:S(2)}, u32[]{:S(2)}) %collective-permute-start.19) | collective-permute-done | bytes 32800 | tf_op jit(solution)/shard_map/ppermute | solution.py:1252
  13.9 0.0 copy-start
  13.9 0.0 copy-start.1
  13.9 0.0 copy-start.2
  13.9 0.0 copy-start.3
  13.9 10.5 %all-gather = f32[768,256]{1,0:T(8,128)S(1)} all-gather(f32[96,256]{1,0:T(8,128)S(1)} %get-tuple-element.92), channel_id=2, replica_groups=mesh['blk'=4,'sub'=8] {'sub'}, dimensions={0}, use_global_device_ids=true | all-gather | bytes 884736 | tf_op jit(solution)/shard_map/all_gather | solution.py:1283
  24.4 0.0 copy-done
  24.4 0.0 copy-done.1
  24.4 0.0 copy-done.2
  24.4 0.0 copy-done.3
  24.4 0.0 copy-start.5
  24.5 2.9 %solve.1 = (f32[8,16,256]{2,1,0:T(8,128)}, f32[3,16,256]{2,1,0:T(8,128)}, s32[1]{0:T(128)}) custom-call(s32[8]{0:T(128)S(1)} %get-tuple-element.86.positions, s32[9]{0:T(128)S(1)} %get-tuple-element.87.owned, f32[8,96,256]{2,1,0:T(8,128)S(1)} %bitcast.151, f32[8,16,256]{2,1,0:T(8,128)S(1)} %get-tuple-element.93.part_ref, ...), custom_call_target="tpu_custom_call" | custom-call | tf_op jit(solution)/shard_map/solve/pallas_call | solution.py:1284
  27.4 0.0 copy-done.5
  27.4 0.8 %while.13 = (f32[8,16,256]{2,1,0:T(8,128)}, f32[3,16,256]{2,1,0:T(8,128)}, s32[1]{0:T(128)}, f32[8,16,256]{2,1,0:T(8,128)S(1)}, s32[8,6]{1,0:T(8,128)S(1)}, /*in...) while((f32[8,16,256]{2,1,0:T(8,128)}, ...), condition=%region_9.12_spmd.clone.clone, body=%region_0.11_spmd.sunk.clone.clone | while | flops 309503840 | bytes 22817100 | solution.py:1311
  (1 shorter events, 0.0 us)
Async XLA Ops:
  0.6 8.1 %copy-start.4 = (bf16[256,128]{1,0:T(8,128)(2,1)S(1)}, bf16[256,128]{1,0:T(8,128)(2,1)}, u32[]{:S(2)}) copy-start(bf16[256,128]{1,0:T(8,128)(2,1)} %constant.451.clone.table_ref) | copy-start | bytes 196612
  3.1 6.9 %collective-permute-start.18 = (f32[32,256]{1,0:T(8,128)S(1)}, f32[32,256]{1,0:T(8,128)S(1)}, u32[]{:S(2)}, u32[]{:S(2)}) collective-permute-start(f32[32,256]{1,0:T(8,128)S(1)} %get-tuple-element.90), channel_id=1, source_target_pairs={{0,8},{8,0},{16,24},{24,16},{1,9},{9,1},{17,25},{25,17},{2,10},{10... | collective-permute-start | bytes 98312 | tf_op jit(solution)/shard_map/ppermute | solution.py:1252
  6.2 6.2 %collective-permute-start.20 = (f32[32,256]{1,0:T(8,128)S(1)}, f32[32,256]{1,0:T(8,128)S(1)}, u32[]{:S(2)}, u32[]{:S(2)}) collective-permute-start(f32[32,256]{1,0:T(8,128)S(1)} %get-tuple-element.91), channel_id=1, source_target_pairs={{0,24},{8,16},{16,8},{24,0},{1,25},{9,17},{17,9},{25,1},{2,26},{10... | collective-permute-start | bytes 98312 | tf_op jit(solution)/shard_map/ppermute | solution.py:1252
  8.6 5.2 %collective-permute-start.19 = (f32[32,256]{1,0:T(8,128)S(1)}, f32[32,256]{1,0:T(8,128)S(1)}, u32[]{:S(2)}, u32[]{:S(2)}) collective-permute-start(f32[32,256]{1,0:T(8,128)S(1)} %get-tuple-element.91), channel_id=1, source_target_pairs={{0,16},{8,24},{16,0},{24,8},{1,17},{9,25},{17,1},{25,9},{2,18},{10... | collective-permute-start | bytes 98312 | tf_op jit(solution)/shard_map/ppermute | solution.py:1252
  13.9 10.6 %copy-start = (bf16[256,256]{1,0:T(8,128)(2,1)S(1)}, bf16[256,256]{1,0:T(8,128)(2,1)}, u32[]{:S(2)}) copy-start(bf16[256,256]{1,0:T(8,128)(2,1)} %constant.454.clone.table_l_ref) | copy-start | bytes 393220
  13.9 10.6 %copy-start.1 = (bf16[256,256]{1,0:T(8,128)(2,1)S(1)}, bf16[256,256]{1,0:T(8,128)(2,1)}, u32[]{:S(2)}) copy-start(bf16[256,256]{1,0:T(8,128)(2,1)} %constant.453.clone.table_p_ref) | copy-start | bytes 393220
  13.9 10.6 %copy-start.2 = (bf16[128,256]{1,0:T(8,128)(2,1)S(1)}, bf16[128,256]{1,0:T(8,128)(2,1)}, u32[]{:S(2)}) copy-start(bf16[128,256]{1,0:T(8,128)(2,1)} %constant.455.clone.table_x_ref) | copy-start | bytes 196612
  13.9 10.6 %copy-start.3 = (bf16[128,256]{1,0:T(8,128)(2,1)S(1)}, bf16[128,256]{1,0:T(8,128)(2,1)}, u32[]{:S(2)}) copy-start(bf16[128,256]{1,0:T(8,128)(2,1)} %constant.452.clone.table_w_ref) | copy-start | bytes 196612
  24.4 2.9 %copy-start.5 = (f32[8,16,256]{2,1,0:T(8,128)S(1)}, f32[8,16,256]{2,1,0:T(8,128)}, u32[]{:S(2)}) copy-start(f32[8,16,256]{2,1,0:T(8,128)} %rhs_hbm.1) | copy-start | bytes 393220

commit v4 on v3

--- a/solution.py
+++ b/solution.py
@@ -63,7 +63,7 @@
 
 def apply_operator(values, ghosts):
     blocks = values.shape[0]
-    lane_y, lane_x = lane_parts()
+    _, lane_x = lane_parts()
     ghost_x_low = ghosts[:, 0].reshape(blocks, 16, 16)
     ghost_x_high = ghosts[:, 1].reshape(blocks, 16, 16)
     ghost_y_low = ghosts[:, 2].reshape(blocks, 16, 16)
@@ -329,7 +329,7 @@
     )
     root_source = root_source - jnp.mean(root_source)
     root_values = jnp.zeros_like(root_source)
-    for repeat in range(ROOT_SWEEPS):
+    for _ in range(ROOT_SWEEPS):
         root_values = root_relax(root_values, root_source, 4 * side_x)
     root_back = (
         root_values.reshape(blk_count, 4, side_y, 4, side_x, 4)
@@ -351,6 +351,7 @@
 SELF = 1.0 - 6.0 * FACTOR
 LANES = 128
 OWN_ROWS = 64
+ROOT_ROW = 32
 MSG_ROWS = 32
 VMEM_LIMIT = 16 * 1024 * 1024
 
@@ -547,28 +548,25 @@
     shape = child_ref.shape
     octant = row_iota(shape)
     place = jnp.broadcast_to(place_ref[...], shape)
-    cell_z = 2 * power_div(place, side_y * side_x) + power_div(octant, 4)
+    half_z = power_div(octant, 4)
+    cell_z = 2 * power_div(place, side_y * side_x) + half_z
     cell_y = 2 * power_rem(power_div(place, side_x), side_y) + power_rem(power_div(octant, 2), 2)
     cell_x = 2 * power_rem(place, side_x) + power_rem(octant, 2)
-    return (cell_z * wide_y + cell_y) * sub_count + cell_x
-
-
-def own_codes(sub_count, blocks, child_ref, codes, sub_here, blk_here):
+    return (cell_z * wide_y + cell_y) * sub_count + cell_x, half_z * wide_y + cell_y
+
+
+def of_own(child_ref, values, blocks, sub_count, sub_here, blk_here):
     first = (blk_here * sub_count + sub_here) * blocks
-    codes = codes.astype(jnp.float32)
+    values = values.astype(jnp.float32)
     return [
-        jnp.sum(jnp.where(child_ref[...] == first + slot, codes, 0.0)).astype(jnp.int32)
+        jnp.sum(jnp.where(child_ref[...] == first + slot, values, 0.0)).astype(jnp.int32)
         for slot in range(blocks)
     ]
 
 
-def own_position(sub_count, wide_y, code):
-    return lax.rem(lax.div(code, wide_y * sub_count), 2) * wide_y + lax.rem(
-        lax.div(code, sub_count), wide_y
-    )
-
-
-def lists_agree(sub_count, blk_count, leaf_ref, parent_ref, child_ref, place_ref, codes, own):
+def lists_agree(
+    sub_count, blk_count, leaf_ref, leaf_vector, parent_ref, child_ref, place_ref, codes, own
+):
     blocks = len(own)
     wide_y = blocks // 2
     side_y = wide_y // 2
@@ -578,21 +576,36 @@
     children = child_ref[...]
     device = power_div(codes, 2 * layer) * sub_count + power_rem(codes, sub_count)
     missed = jnp.where(power_div(children, blocks) != device, 1.0, 0.0)
-    faults = jnp.int32(0)
+    shape = (blocks, 6)
+    row = row_iota(shape)
+    own_code = jnp.zeros(shape, jnp.int32)
     for slot in range(blocks):
-        for axis, (stride, length) in enumerate(
-            ((1, sub_count), (sub_count, wide_y), (layer, 2 * blk_count))
-        ):
-            along = lax.rem(lax.div(own[slot], stride), length)
-            for sign in (-1, 1):
-                listed = leaf_ref[slot, 2 * axis + (sign + 1) // 2]
-                exists = (along + sign >= 0) & (along + sign < length)
-                hit = (children == listed) & (codes == own[slot] + sign * stride)
-                missed = missed - jnp.where(hit, 1.0, 0.0)
-                faults = faults + jnp.where(
-                    exists, jnp.where(listed >= 0, 1, -100000), jnp.where(listed < 0, 0, -100000)
-                )
-    wrong = jnp.abs(jnp.sum(missed) + faults.astype(jnp.float32))
+        own_code = jnp.where(row == slot, own[slot], own_code)
+        for face, stride in enumerate((-1, 1, -sub_count, sub_count, -layer, layer)):
+            hit = (children == leaf_ref[slot, face]) & (codes == own[slot] + stride)
+            missed = missed - jnp.where(hit, 1.0, 0.0)
+    face = lane_iota(shape)
+    along = jnp.where(
+        face < 2,
+        power_rem(own_code, sub_count),
+        jnp.where(
+            face < 4,
+            power_rem(power_div(own_code, sub_count), wide_y),
+            power_div(own_code, layer),
+        ),
+    )
+    length = jnp.where(face < 2, sub_count, jnp.where(face < 4, wide_y, 2 * blk_count))
+    goal = along + 2 * power_rem(face, 2) - 1
+    exists = (goal >= 0) & (goal < length)
+    listed = leaf_vector[...]
+    faults = jnp.sum(
+        jnp.where(
+            exists,
+            jnp.where(listed >= 0, 1.0, -100000.0),
+            jnp.where(listed < 0, 0.0, -100000.0),
+        )
+    )
+    wrong = jnp.abs(jnp.sum(missed) + faults)
     place_row = place_ref[...].astype(jnp.float32)
     place_column = as_column(place_row)
     number = row_iota((parents, parents))
@@ -685,11 +698,11 @@
     sub_here, blk_here, x_low, x_high, z_low, z_high = limits(sub_count, blk_count)
     copies[0].wait()
     copies[1].wait()
-    codes = grid_codes(sub_count, wide_y, child_ref, place_ref)
-    own_code = own_codes(sub_count, blocks, child_ref, codes, sub_here, blk_here)
+    codes, positions = grid_codes(sub_count, wide_y, child_ref, place_ref)
+    positions = of_own(child_ref, positions, blocks, sub_count, sub_here, blk_here)
     copies[2].wait()
     for slot in range(blocks):
-        placed[own_position(sub_count, wide_y, own_code[slot])] = rhs_ref[slot]
+        placed[positions[slot]] = rhs_ref[slot]
     s = placed_chunks(placed, wide_y)
     shape = s[0].shape
     top = shape[0] - 1
@@ -729,8 +742,9 @@
     for copy in copies[3:]:
         copy.wait()
     out_a = split_dot(left_a[...], table_a)
+    own_code = of_own(child_ref, codes, blocks, sub_count, sub_here, blk_here)
     good = lists_agree(
-        sub_count, blk_count, leaf_ref, parent_ref, child_ref, place_ref, codes, own_code
+        sub_count, blk_count, leaf_ref, leaf_out, parent_ref, child_ref, place_ref, codes, own_code
     )
     lane24 = lane_iota((24, LANES))
     main = []
@@ -810,7 +824,7 @@
 def side_kernel(
     sub_count, blk_count, slots,
     child_ref, owner_ref, place_ref, placed, table_ref,
-    position_ref, slot_ref, part_ref, faces_ref,
+    position_ref, slot_ref, part_ref, cross_ref, pair_ref,
     left_c
 ):
     blocks = placed.shape[0]
@@ -818,10 +832,10 @@
     f = FACTOR
     f2 = f * f
     sub_here, blk_here, x_low, x_high, z_low, z_high = limits(sub_count, blk_count)
-    codes = grid_codes(sub_count, wide_y, child_ref, place_ref)
-    own_code = own_codes(sub_count, blocks, child_ref, codes, sub_here, blk_here)
+    _, positions = grid_codes(sub_count, wide_y, child_ref, place_ref)
+    positions = of_own(child_ref, positions, blocks, sub_count, sub_here, blk_here)
     for slot in range(blocks):
-        position_ref[slot] = own_position(sub_count, wide_y, own_code[slot])
+        position_ref[slot] = positions[slot]
     s = placed_chunks(placed, wide_y)
     back = return_gain(s[0].shape, x_low, x_high, z_low, z_high)
     sx, sy, sz = fine_beside(s)
@@ -842,7 +856,12 @@
     faces = out_c[0:64]
     for yy in range(1, wide_y):
         faces = faces + turn(out_c[64 * yy : 64 * yy + 64], 16 * yy, 1)
-    faces_ref[...] = faces
+    lane = lane_iota((32, LANES))
+    low = jnp.where(lane < 64, faces[0:32], turn(faces[32:64], 64, 1))
+    high = jnp.where(lane < 64, turn(faces[0:32], 64, 1), faces[32:64])
+    even = sub_here % 2 == 0
+    cross_ref[...] = jnp.where(even, low, high)
+    pair_ref[...] = jnp.where(even, high, low)
     owned = owned_slots(sub_count, blk_count, slots, sub_here, blk_here, owner_ref, place_ref)
     for k in range(slots):
         for j in range(3):
@@ -874,12 +893,13 @@
     return (sub_count * blk_count // 16 + 1) // 2
 
 
-def join_kernel(sub_count, blk_count, own_ref, faces_ref, *rest):
+def join_kernel(sub_count, blk_count, own_ref, cross_ref, *rest):
     msg_refs = rest[: blk_count - 1]
     out_ref, lines_ref, root_s = rest[blk_count - 1 :]
     _, blk_here, _, _, z_low, z_high = limits(sub_count, blk_count)
     below, above = neighbour_pick(blk_here, blk_count, msg_refs)
     row8 = row_iota((8, LANES))
+    cell8 = lane_iota((8, LANES)) % 8
     low_rows = (row8 >= 1) & (row8 < 5)
     high_rows = (row8 >= 3) & (row8 < 7)
     good = own_ref[56:64, 0:LANES]
@@ -889,14 +909,24 @@
         lanes = slice(LANES * half, LANES * half + LANES)
         low = below(slice(0, 8), lanes) * z_low
         high = above(slice(0, 8), lanes) * z_high
+        tiles = []
         for base, low_turn, high_turn in ((0, 1, 3), (24, 5, 7)):
-            out_ref[base : base + 8, lanes] = own_ref[base : base + 8, lanes] + jnp.where(
-                low_rows, turn(low, low_turn, 0), 0.0
+            tiles.append(
+                (
+                    own_ref[base : base + 8, lanes]
+                    + jnp.where(low_rows, turn(low, low_turn, 0), 0.0),
+                    own_ref[base + 8 : base + 16, lanes],
+                    own_ref[base + 16 : base + 24, lanes]
+                    + jnp.where(high_rows, turn(high, high_turn, 0), 0.0),
+                )
             )
-            out_ref[base + 8 : base + 16, lanes] = own_ref[base + 8 : base + 16, lanes]
-            out_ref[base + 16 : base + 24, lanes] = own_ref[
-                base + 16 : base + 24, lanes
-            ] + jnp.where(high_rows, turn(high, high_turn, 0), 0.0)
+        packed = tiles[1][0]
+        for g in range(3):
+            out_ref[8 * g : 8 * g + 8, lanes] = tiles[0][g]
+            if g > 0:
+                packed = packed + turn(jnp.where(cell8 == 0, tiles[1][g], 0.0), g, 1)
+                packed = packed + turn(jnp.where(cell8 == 7, tiles[1][g], 0.0), -g, 1)
+        out_ref[24:32, lanes] = packed
         out_ref[23:24, lanes] = good[0:1]
     root_s[...] = jnp.zeros(root_s.shape, jnp.float32)
     for d in range(blk_count):
@@ -908,11 +938,11 @@
     tile = 0
     for start in range(0, 4 * blk_count, 8):
         for part in range(root_s.shape[0]):
-            row = 48 + 8 * (tile // 2)
+            row = ROOT_ROW + 8 * (tile // 2)
             lanes = slice(LANES * (tile % 2), LANES * (tile % 2) + LANES)
             out_ref[row : row + 8, lanes] = root_s[part, 4 + start : 12 + start]
             tile += 1
-    row = 48 + 8 * root_tiles(sub_count, blk_count)
+    row = ROOT_ROW + 8 * root_tiles(sub_count, blk_count)
     count = lines_ref.shape[0] // 2
     half = count // 2
     low = below(slice(16, 16 + count), slice(0, 256)) * z_low
@@ -921,8 +951,8 @@
     lines_ref[count : 2 * count] = high
     out_ref[row : row + half, :] = low[half:count]
     out_ref[row + half : row + count, :] = high[half:count]
-    out_ref[row + 8 : row + 40, 0:LANES] = faces_ref[0:32]
-    out_ref[row + 8 : row + 40, LANES:256] = faces_ref[32:64]
+    out_ref[row + 8 : row + 24, 0:LANES] = cross_ref[0:16]
+    out_ref[row + 8 : row + 24, LANES:256] = cross_ref[16:32]
 
 
 def owned_slots(sub_count, blk_count, slots, sub_here, blk_here, owner_ref, place_ref):
@@ -952,9 +982,13 @@
     return found
 
 
+def exchange_slot(sub_count, distance):
+    return lax.shift_right_logical(distance, 1) + (distance & 1) * (sub_count // 2)
+
+
 def solve_kernel(
     sub_count, blk_count, slots,
-    positions, owned, all_ref, part_ref, lines_ref, table_w_ref, table_p_ref, table_l_ref, table_x_ref,
+    positions, owned, all_ref, pair_ref, part_ref, lines_ref, table_w_ref, table_p_ref, table_l_ref, table_x_ref,
     leaf_ref, parent_ref, good_ref,
     placed, par_s, root_s, fine_s, push_s
 ):
@@ -963,6 +997,7 @@
     f = FACTOR
     f2 = f * f
     sub_here, blk_here, x_low, x_high, z_low, z_high = limits(sub_count, blk_count)
+    slot_of = [exchange_slot(sub_count, sub_here ^ c) for c in range(sub_count)]
     row8 = row_iota((8, LANES))
     cell24 = lane_iota((24, LANES)) % 8
     row24 = row_iota((24, LANES))
@@ -970,16 +1005,32 @@
     for c in range(1, sub_count):
         good = jnp.minimum(good, all_ref[c, 16:24, 0:LANES])
     good_ref[0] = jnp.min(jnp.where(row8 == 7, good, 1.0)).astype(jnp.int32)
+    cell8 = lane_iota((8, LANES)) % 8
+    sides = []
+    for c in range(sub_count):
+        halves = []
+        for half in range(2):
+            packed = all_ref[slot_of[c], 24:32, LANES * half : LANES * half + LANES]
+            halves.append(
+                (
+                    jnp.concatenate(
+                        [jnp.where(cell8 == 7, turn(packed, g, 1), 0.0) for g in range(3)], axis=0
+                    ),
+                    jnp.concatenate(
+                        [jnp.where(cell8 == 0, turn(packed, -g, 1), 0.0) for g in range(3)], axis=0
+                    ),
+                )
+            )
+        sides.append(halves)
     source = []
     for c in range(sub_count):
         halves = []
         for half in range(2):
-            lanes = slice(LANES * half, LANES * half + LANES)
-            value = all_ref[c, 0:24, lanes]
+            value = all_ref[slot_of[c], 0:24, LANES * half : LANES * half + LANES]
             if c + 1 < sub_count:
-                value = value + jnp.where(cell24 == 7, all_ref[c + 1, 24:48, lanes], 0.0)
+                value = value + sides[c + 1][half][0]
             if c > 0:
-                value = value + jnp.where(cell24 == 0, all_ref[c - 1, 24:48, lanes], 0.0)
+                value = value + sides[c - 1][half][1]
             halves.append(value)
         source.append(halves)
 
@@ -991,8 +1042,8 @@
     tile = 0
     for _ in range(0, root_rows, 8):
         pieces = []
-        for part in range(parts):
-            row = 48 + 8 * (tile // 2)
+        for _ in range(parts):
+            row = ROOT_ROW + 8 * (tile // 2)
             lanes = slice(LANES * (tile % 2), LANES * (tile % 2) + LANES)
             total = all_ref[0, row : row + 8, lanes]
             for c in range(1, sub_count):
@@ -1128,27 +1179,28 @@
             fine_s[2 * yy, pl.ds(zp, 16, stride=2), :] = spread[top : top + 16, 0:128]
             fine_s[2 * yy + 1, pl.ds(zp, 16, stride=2), :] = spread[top : top + 16, 128:256]
 
-    line = 48 + 8 * root_tiles(sub_count, blk_count)
-    lane64 = lane_iota((32, LANES))
-    from_low = all_ref[before, line + 8 : line + 40, 0:LANES] * x_low
-    low_values = all_ref[before, line + 8 : line + 40, LANES:256] * x_low
-    from_high = all_ref[after, line + 8 : line + 40, 0:LANES] * x_high
-    high_values = all_ref[after, line + 8 : line + 40, LANES:256] * x_high
-    left = jnp.concatenate(
-        [
-            jnp.where(lane64 < 64, turn(from_low, 64, 1), f2 * low_values),
-            jnp.where(lane64 < 64, from_high, f2 * turn(high_values, 64, 1)),
-        ],
-        axis=1,
-    )
+    slot_before = exchange_slot(sub_count, sub_here ^ before)
+    slot_after = exchange_slot(sub_count, sub_here ^ after)
+    line = ROOT_ROW + 8 * root_tiles(sub_count, blk_count)
+    even = sub_here % 2 == 0
+
+    def crossed(slot):
+        rows = all_ref[slot, line + 8 : line + 24, :]
+        return jnp.concatenate([rows[:, 0:LANES], rows[:, LANES:256]], axis=0)
+
+    pair = pair_ref[...]
+    from_low = jnp.where(even, crossed(slot_before), pair) * x_low
+    from_high = jnp.where(even, pair, crossed(slot_after)) * x_high
+    behind = jnp.where(lane_iota((32, LANES)) < 64, 1.0, f2)
+    left = [from_low * behind, from_high * behind]
     lane128 = lane_iota((32, LANES))
     rows = []
     for yy in range(wide_y):
         rows.append(
             jnp.where(
                 lax.rem(lane128, 64) < 16,
-                turn(left[:, 0:LANES], -16 * yy, 1),
-                turn(left[:, LANES:256], 16 - 16 * yy, 1),
+                turn(left[0], -16 * yy, 1),
+                turn(left[1], 16 - 16 * yy, 1),
             )
         )
     push = split_dot(jnp.concatenate(rows, axis=0), table_x_ref[...])
@@ -1156,9 +1208,9 @@
         push_s[:, 256 * yy : 256 * yy + 256] = push[32 * yy : 32 * yy + 32]
     cell = lane_iota((2 * wide_y, 256)) % 16
     across = jnp.where(
-        cell == 0, turn(all_ref[before, line : line + 2 * wide_y, :], -15, 1) * x_low, 0.0
+        cell == 0, turn(all_ref[slot_before, line : line + 2 * wide_y, :], -15, 1) * x_low, 0.0
     ) + jnp.where(
-        cell == 15, turn(all_ref[after, line : line + 2 * wide_y, :], 15, 1) * x_high, 0.0
+        cell == 15, turn(all_ref[slot_after, line : line + 2 * wide_y, :], 15, 1) * x_high, 0.0
     )
     across = (2.0 * f2) * across
     count = 2 * wide_y
@@ -1248,26 +1300,28 @@
     lists = (
         leaf_neighbors, parent_rows.T, child_rows.T, owner_row.reshape(-1), place_row.reshape(-1),
     )
-    received = [
-        lax.ppermute(messages[d.bit_length() - 1], "blk", paired(blk_count, d))
-        for d in range(1, blk_count)
-    ]
-    positions, owned, own_part, faces = pl.pallas_call(
+    received = []
+    for d in range(1, blk_count):
+        received.append(
+            lax.ppermute(messages[d.bit_length() - 1], "blk", paired(blk_count, d))
+        )
+    positions, owned, own_part, cross_faces, pair_faces = pl.pallas_call(
         functools.partial(side_kernel, sub_count, blk_count, PMOST),
         name="side",
         out_shape=[
             jax.ShapeDtypeStruct((blocks,), jnp.int32),
             jax.ShapeDtypeStruct((3 * PMOST,), jnp.int32),
             jax.ShapeDtypeStruct(grid_shape, f32),
-            jax.ShapeDtypeStruct((64, LANES), f32),
-        ],
+        ]
+        + [jax.ShapeDtypeStruct((32, LANES), f32)] * 2,
         in_specs=[vmem] * 5,
-        out_specs=[smem] * 2 + [vmem] * 2,
+        out_specs=[smem] * 2 + [vmem] * 3,
         scratch_shapes=[pltpu.VMEM((64 * wide_y, 256), f32)],
         compiler_params=params,
     )(child_rows, owner_row, place_row, placed, jnp.asarray(face_table()))
+    pair_faces = lax.ppermute(pair_faces, "sub", paired(sub_count, 1))
     root_parts = 16 * sub_count // LANES
-    joined_rows = 48 + 8 * root_tiles(sub_count, blk_count) + 8 + 32
+    joined_rows = ROOT_ROW + 8 * root_tiles(sub_count, blk_count) + 8 + 16
     joined, lines = pl.pallas_call(
         functools.partial(join_kernel, sub_count, blk_count),
         name="join",
@@ -1279,8 +1333,13 @@
         out_specs=[vmem] * 2,
         scratch_shapes=[pltpu.VMEM((root_parts, 4 * blk_count + 8, LANES), f32)],
         compiler_params=params,
-    )(own, faces, *received)
-    gathered = lax.all_gather(joined, "sub", axis=0, tiled=False)
+    )(own, cross_faces, *received)
+    block = [joined]
+    for d in range(2, sub_count, 2):
+        block.append(lax.ppermute(joined, "sub", paired(sub_count, d)))
+    block = jnp.stack(block)
+    other = lax.ppermute(block, "sub", paired(sub_count, 1))
+    gathered = jnp.concatenate([block, other], axis=0)
     leaf_solution, parent_solution, good = pl.pallas_call(
         functools.partial(solve_kernel, sub_count, blk_count, PMOST),
         name="solve",
@@ -1289,7 +1348,7 @@
             jax.ShapeDtypeStruct((PMOST, 16, 256), f32),
             jax.ShapeDtypeStruct((1,), jnp.int32),
         ],
-        in_specs=[smem] * 2 + [vmem] * 7,
+        in_specs=[smem] * 2 + [vmem] * 8,
         out_specs=[vmem] * 2 + [smem],
         scratch_shapes=[
             pltpu.VMEM((blocks, 16, 256), f32),
@@ -1300,7 +1359,7 @@
         ],
         compiler_params=params,
     )(
-        positions, owned, gathered, own_part, lines,
+        positions, owned, gathered, pair_faces, own_part, lines,
         jnp.asarray(root_spread_table(sub_count)), jnp.asarray(parent_table()),
         jnp.asarray(leaf_table_of_cells()), jnp.asarray(push_table()),
     )

time: 28.5 us -> 28.5 us (level)
  blocking collectives: 10.5 us -> 0 us
  waiting for transfers between devices: 3.9 us -> 10.6 us
  starting transfers between devices: 5.71 us -> 9.35 us
    all_gather x1 -> x0, blocking collectives: 10.5 us -> none  [local(): gathered = lax.all_gather(joined, 'sub', axis=0, tiled=False)]
    ppermute x0 -> x5, waiting for transfers between devices: none -> 6.11 us  [the longest x3 4.68 us: local(): block.append(lax.ppermute(joined, 'sub', paired(sub_count, d)))]
    ppermute x0 -> x5, starting transfers between devices: none -> 3.64 us  [the longest x3 3.5 us: local(): block.append(lax.ppermute(joined, 'sub', paired(sub_count, d)))]
    ppermute x3, waiting for transfers between devices: 3.9 us -> 4.46 us  [local(): lax.ppermute(messages[d.bit_length() - 1], 'blk', paired(blk_count, d))]
  transfers between devices with their start and end apart: 3 -> 8, of which waited for: 2 -> 6; matrix products, arithmetic and copies ran while one was open for 0% -> 0% of each run, Pallas kernels for 4% -> 4%
where the time goes in v4:
time: 28.5 us; the launch traced here: 28.3 us
  waiting for transfers between devices  10.6 us (37%)
  starting transfers between devices  9.35 us (33%)
  Pallas kernels  6.53 us (23%)
  between operations  0.99 us (3%)
  loops' own time  0.79 us (3%)
    ppermute x3, starting transfers between devices, local(): lax.ppermute(messages[d.bit_length() - 1], 'blk', paired(blk_count, d))  5.71 us
    ppermute x3, waiting for transfers between devices, local(): block.append(lax.ppermute(joined, 'sub', paired(sub_count, d)))  4.68 us
    ppermute x3, waiting for transfers between devices, local(): lax.ppermute(messages[d.bit_length() - 1], 'blk', paired(blk_count, d))  4.46 us
    ppermute x3, starting transfers between devices, local(): block.append(lax.ppermute(joined, 'sub', paired(sub_count, d)))  3.5 us
    pallas_call x1, Pallas kernels, local(): pl.pallas_call(functools.partial(solve_kernel, sub_count, blk_count, PMOS...  2.92 us
    pallas_call x1, Pallas kernels, local(): pl.pallas_call(functools.partial(push_kernel, sub_count, blk_count, blk_b...  2.37 us
    ppermute x1, waiting for transfers between devices, local(): other = lax.ppermute(block, 'sub', paired(sub_count, 1))  1.43 us
    pallas_call x1, Pallas kernels, local(): pl.pallas_call(functools.partial(side_kernel, sub_count, blk_count, PMOST...  1.15 us
  transfers between devices with their start and end apart: 8, of which 6 were waited for; matrix products, arithmetic and copies ran while one was open for 0% of the time, Pallas kernels for 4%

profile of v4, /device:TPU:0, one launch (start us, length us, event | category | flops | bytes accessed | tf_op | source)
XLA Modules:
  0.0 28.3 jit_solution(8694055265902973999)
XLA Ops:
  0.6 0.0 copy-start.4
  0.6 2.4 %push.1 = (f32[8,16,256]{2,1,0:T(8,128)S(1)}, f32[64,256]{1,0:T(8,128)S(1)}, s32[8,6]{1,0:T(8,128)S(1)}, s32[6,32]{1,0:T(8,128)S(1)}, s32[8,32]{1,0:T(8,128)S(1)...) custom-call(s32[8,6]{1,0:T(8,128)} %leaf_hbm.1, ...), custom_call_target="tpu_custom_call" | custom-call | tf_op jit(solution)/shard_map/push/pallas_call | solution.py:1268
  3.0 3.1 %collective-permute-start.18 = (f32[32,256]{1,0:T(8,128)S(1)}, f32[32,256]{1,0:T(8,128)S(1)}, u32[]{:S(2)}, u32[]{:S(2)}) collective-permute-start(f32[32,256]{1,0:T(8,128)S(1)} %get-tuple-element.91), channel_id=1, source_target_pairs={{0,8},{8,0},{16,24},{24,16},{1,9},{9,1},{17,25},{25,17},{2,10},{10... | collective-permute-start | bytes 98312 | tf_op jit(solution)/shard_map/ppermute | solution.py:1306
  6.1 2.6 %collective-permute-start.19 = (f32[32,256]{1,0:T(8,128)S(1)}, f32[32,256]{1,0:T(8,128)S(1)}, u32[]{:S(2)}, u32[]{:S(2)}) collective-permute-start(f32[32,256]{1,0:T(8,128)S(1)} %get-tuple-element.92), channel_id=1, source_target_pairs={{0,16},{8,24},{16,0},{24,8},{1,17},{9,25},{17,1},{25,9},{2,18},{10... | collective-permute-start | bytes 98312 | tf_op jit(solution)/shard_map/ppermute | solution.py:1306
  8.7 1.1 %side.1 = (s32[8]{0:T(128)S(1)}, s32[9]{0:T(128)S(1)}, f32[8,16,256]{2,1,0:T(8,128)S(1)}, f32[32,128]{1,0:T(8,128)S(1)}, f32[32,128]{1,0:T(8,128)S(1)}) custom-call(s32[8,32]{1,0:T(8,128)S(1)} %get-tuple-element.83.child_ref, s32[1,32]{1,0:T(1,128)S(1)} %get-tuple-element.346.owner_ref, s32[1,32]{1,0:T(1,128)S(1)} %get-tuple-element.85.place_ref, ...), custom_call_target="tpu_custom_call" | custom-call | tf_op jit(solution)/shard_map/side/pallas_call | solution.py:1308
  9.9 0.1 collective-permute-start.25
  10.0 1.6 %collective-permute-done.19.rest_1_ = f32[32,256]{1,0:T(8,128)S(1)} collective-permute-done((f32[32,256]{1,0:T(8,128)S(1)}, f32[32,256]{1,0:T(8,128)S(1)}, u32[]{:S(2)}, u32[]{:S(2)}) %collective-permute-start.19) | collective-permute-done | bytes 32800 | tf_op jit(solution)/shard_map/ppermute | solution.py:1306
  11.5 2.9 %collective-permute-done.20.rest_2_ = f32[32,256]{1,0:T(8,128)S(1)} collective-permute-done((f32[32,256]{1,0:T(8,128)S(1)}, f32[32,256]{1,0:T(8,128)S(1)}, u32[]{:S(2)}, u32[]{:S(2)}) %collective-permute-start.20) | collective-permute-done | bytes 32800 | tf_op jit(solution)/shard_map/ppermute | solution.py:1306
  14.4 0.1 join.1
  14.5 1.5 %collective-permute-start.21 = (f32[64,256]{1,0:T(8,128)S(1)}, f32[64,256]{1,0:T(8,128)S(1)}, u32[]{:S(2)}, u32[]{:S(2)}) collective-permute-start(f32[64,256]{1,0:T(8,128)S(1)} %get-tuple-element.93), channel_id=1, source_target_pairs={{0,2},{1,3},{2,0},{3,1},{4,6},{5,7},{6,4},{7,5},{8,10},{9,11},{10,... | collective-permute-start | bytes 196616 | tf_op jit(solution)/shard_map/ppermute | solution.py:1339
  16.0 1.5 %collective-permute-start.22 = (f32[64,256]{1,0:T(8,128)S(1)}, f32[64,256]{1,0:T(8,128)S(1)}, u32[]{:S(2)}, u32[]{:S(2)}) collective-permute-start(f32[64,256]{1,0:T(8,128)S(1)} %get-tuple-element.93), channel_id=1, source_target_pairs={{0,4},{1,5},{2,6},{3,7},{4,0},{5,1},{6,2},{7,3},{8,12},{9,13},{10,... | collective-permute-start | bytes 196616 | tf_op jit(solution)/shard_map/ppermute | solution.py:1339
  17.6 0.5 %collective-permute-start.23 = (f32[64,256]{1,0:T(8,128)S(1)}, f32[64,256]{1,0:T(8,128)S(1)}, u32[]{:S(2)}, u32[]{:S(2)}) collective-permute-start(f32[64,256]{1,0:T(8,128)S(1)} %get-tuple-element.93), channel_id=1, source_target_pairs={{0,6},{1,7},{2,4},{3,5},{4,2},{5,3},{6,0},{7,1},{8,14},{9,15},{10,... | collective-permute-start | bytes 196616 | tf_op jit(solution)/shard_map/ppermute | solution.py:1339
  18.0 1.1 %collective-permute-done.21 = f32[64,256]{1,0:T(8,128)S(1)} collective-permute-done((f32[64,256]{1,0:T(8,128)S(1)}, f32[64,256]{1,0:T(8,128)S(1)}, u32[]{:S(2)}, u32[]{:S(2)}) %collective-permute-start.21) | collective-permute-done | bytes 65568 | tf_op jit(solution)/shard_map/ppermute | solution.py:1339
  19.2 1.2 %collective-permute-done.22 = f32[64,256]{1,0:T(8,128)S(1)} collective-permute-done((f32[64,256]{1,0:T(8,128)S(1)}, f32[64,256]{1,0:T(8,128)S(1)}, u32[]{:S(2)}, u32[]{:S(2)}) %collective-permute-start.22) | collective-permute-done | bytes 65568 | tf_op jit(solution)/shard_map/ppermute | solution.py:1339
  20.4 2.3 %collective-permute-done.23 = f32[64,256]{1,0:T(8,128)S(1)} collective-permute-done((f32[64,256]{1,0:T(8,128)S(1)}, f32[64,256]{1,0:T(8,128)S(1)}, u32[]{:S(2)}, u32[]{:S(2)}) %collective-permute-start.23) | collective-permute-done | bytes 65568 | tf_op jit(solution)/shard_map/ppermute | solution.py:1339
  22.7 0.1 collective-permute-start.24
  22.9 0.0 copy-start
  22.9 0.0 copy-start.1
  22.9 0.0 copy-start.2
  22.9 0.0 copy-start.3
  22.9 1.4 %collective-permute-done.24 = f32[4,64,256]{2,1,0:T(8,128)S(1)} collective-permute-done((f32[4,64,256]{2,1,0:T(8,128)S(1)}, f32[4,64,256]{2,1,0:T(8,128)S(1)}, u32[]{:S(2)}, u32[]{:S(2)}) %collective-permute-start.24) | collective-permute-done | bytes 262176 | tf_op jit(solution)/shard_map/ppermute | solution.py:1341
  24.4 0.0 copy-start.5
  24.4 2.9 %solve.1 = (f32[8,16,256]{2,1,0:T(8,128)}, f32[3,16,256]{2,1,0:T(8,128)}, s32[1]{0:T(128)}) custom-call(s32[8]{0:T(128)S(1)} %get-tuple-element.87.positions, s32[9]{0:T(128)S(1)} %get-tuple-element.88.owned, f32[8,64,256]{2,1,0:T(8,128)S(1)} %constant_dynamic-update-slice_fusion.15.all_ref, f32[32,128]{1,0:T(8,128)S(1)} %collective-permute-done.25.pair_ref, ...), custom_call_target="tpu_custom_call" | custom-call | tf_op jit(solution)/shard_map/solve/pallas_call | solution.py:1343
  27.4 0.8 %while.13 = (f32[8,16,256]{2,1,0:T(8,128)}, f32[3,16,256]{2,1,0:T(8,128)}, s32[1]{0:T(128)}, f32[8,16,256]{2,1,0:T(8,128)S(1)}, s32[8,6]{1,0:T(8,128)S(1)}, /*in...) while((f32[8,16,256]{2,1,0:T(8,128)}, ...), condition=%region_9.12_spmd.clone.clone, body=%region_0.11_spmd.sunk.clone.clone | while | flops 309503840 | bytes 22817100 | solution.py:1370
  (15 shorter events, 0.1 us)
Async XLA Ops:
  0.6 8.1 %copy-start.4 = (bf16[256,128]{1,0:T(8,128)(2,1)S(1)}, bf16[256,128]{1,0:T(8,128)(2,1)}, u32[]{:S(2)}) copy-start(bf16[256,128]{1,0:T(8,128)(2,1)} %constant.451.clone.table_ref) | copy-start | bytes 196612
  3.0 7.0 %collective-permute-start.18 = (f32[32,256]{1,0:T(8,128)S(1)}, f32[32,256]{1,0:T(8,128)S(1)}, u32[]{:S(2)}, u32[]{:S(2)}) collective-permute-start(f32[32,256]{1,0:T(8,128)S(1)} %get-tuple-element.91), channel_id=1, source_target_pairs={{0,8},{8,0},{16,24},{24,16},{1,9},{9,1},{17,25},{25,17},{2,10},{10... | collective-permute-start | bytes 98312 | tf_op jit(solution)/shard_map/ppermute | solution.py:1306
  6.1 5.4 %collective-permute-start.19 = (f32[32,256]{1,0:T(8,128)S(1)}, f32[32,256]{1,0:T(8,128)S(1)}, u32[]{:S(2)}, u32[]{:S(2)}) collective-permute-start(f32[32,256]{1,0:T(8,128)S(1)} %get-tuple-element.92), channel_id=1, source_target_pairs={{0,16},{8,24},{16,0},{24,8},{1,17},{9,25},{17,1},{25,9},{2,18},{10... | collective-permute-start | bytes 98312 | tf_op jit(solution)/shard_map/ppermute | solution.py:1306
  8.7 5.7 %collective-permute-start.20 = (f32[32,256]{1,0:T(8,128)S(1)}, f32[32,256]{1,0:T(8,128)S(1)}, u32[]{:S(2)}, u32[]{:S(2)}) collective-permute-start(f32[32,256]{1,0:T(8,128)S(1)} %get-tuple-element.92), channel_id=1, source_target_pairs={{0,24},{8,16},{16,8},{24,0},{1,25},{9,17},{17,9},{25,1},{2,26},{10... | collective-permute-start | bytes 98312 | tf_op jit(solution)/shard_map/ppermute | solution.py:1306
  9.9 14.5 %collective-permute-start.25 = (f32[32,128]{1,0:T(8,128)S(1)}, f32[32,128]{1,0:T(8,128)S(1)}, u32[]{:S(2)}, u32[]{:S(2)}) collective-permute-start(f32[32,128]{1,0:T(8,128)S(1)} %get-tuple-element.94), channel_id=1, source_target_pairs={{0,1},{1,0},{2,3},{3,2},{4,5},{5,4},{6,7},{7,6},{8,9},{9,8},{10,11... | collective-permute-start | bytes 49160 | tf_op jit(solution)/shard_map/ppermute | solution.py:1322
  14.5 4.6 %collective-permute-start.21 = (f32[64,256]{1,0:T(8,128)S(1)}, f32[64,256]{1,0:T(8,128)S(1)}, u32[]{:S(2)}, u32[]{:S(2)}) collective-permute-start(f32[64,256]{1,0:T(8,128)S(1)} %get-tuple-element.93), channel_id=1, source_target_pairs={{0,2},{1,3},{2,0},{3,1},{4,6},{5,7},{6,4},{7,5},{8,10},{9,11},{10,... | collective-permute-start | bytes 196616 | tf_op jit(solution)/shard_map/ppermute | solution.py:1339
  16.0 4.4 %collective-permute-start.22 = (f32[64,256]{1,0:T(8,128)S(1)}, f32[64,256]{1,0:T(8,128)S(1)}, u32[]{:S(2)}, u32[]{:S(2)}) collective-permute-start(f32[64,256]{1,0:T(8,128)S(1)} %get-tuple-element.93), channel_id=1, source_target_pairs={{0,4},{1,5},{2,6},{3,7},{4,0},{5,1},{6,2},{7,3},{8,12},{9,13},{10,... | collective-permute-start | bytes 196616 | tf_op jit(solution)/shard_map/ppermute | solution.py:1339
  17.6 5.2 %collective-permute-start.23 = (f32[64,256]{1,0:T(8,128)S(1)}, f32[64,256]{1,0:T(8,128)S(1)}, u32[]{:S(2)}, u32[]{:S(2)}) collective-permute-start(f32[64,256]{1,0:T(8,128)S(1)} %get-tuple-element.93), channel_id=1, source_target_pairs={{0,6},{1,7},{2,4},{3,5},{4,2},{5,3},{6,0},{7,1},{8,14},{9,15},{10,... | collective-permute-start | bytes 196616 | tf_op jit(solution)/shard_map/ppermute | solution.py:1339
  22.7 1.6 %collective-permute-start.24 = (f32[4,64,256]{2,1,0:T(8,128)S(1)}, f32[4,64,256]{2,1,0:T(8,128)S(1)}, u32[]{:S(2)}, u32[]{:S(2)}) collective-permute-start(f32[4,64,256]{2,1,0:T(8,128)S(1)} %pad_maximum_fusion.3), channel_id=1, source_target_pairs={{0,1},{1,0},{2,3},{3,2},{4,5},{5,4},{6,7},{7,6},{8,9},{9,8},{10,11... | collective-permute-start | bytes 786440 | tf_op jit(solution)/shard_map/ppermute | solution.py:1341
  22.9 1.5 %copy-start = (bf16[256,256]{1,0:T(8,128)(2,1)S(1)}, bf16[256,256]{1,0:T(8,128)(2,1)}, u32[]{:S(2)}) copy-start(bf16[256,256]{1,0:T(8,128)(2,1)} %constant.453.clone.table_p_ref) | copy-start | bytes 393220
  22.9 1.5 %copy-start.1 = (bf16[256,256]{1,0:T(8,128)(2,1)S(1)}, bf16[256,256]{1,0:T(8,128)(2,1)}, u32[]{:S(2)}) copy-start(bf16[256,256]{1,0:T(8,128)(2,1)} %constant.454.clone.table_l_ref) | copy-start | bytes 393220
  22.9 1.5 %copy-start.2 = (bf16[128,256]{1,0:T(8,128)(2,1)S(1)}, bf16[128,256]{1,0:T(8,128)(2,1)}, u32[]{:S(2)}) copy-start(bf16[128,256]{1,0:T(8,128)(2,1)} %constant.452.clone.table_w_ref) | copy-start | bytes 196612
  22.9 1.5 %copy-start.3 = (bf16[128,256]{1,0:T(8,128)(2,1)S(1)}, bf16[128,256]{1,0:T(8,128)(2,1)}, u32[]{:S(2)}) copy-start(bf16[128,256]{1,0:T(8,128)(2,1)} %constant.455.clone.table_x_ref) | copy-start | bytes 196612
  24.4 2.9 %copy-start.5 = (f32[8,16,256]{2,1,0:T(8,128)S(1)}, f32[8,16,256]{2,1,0:T(8,128)}, u32[]{:S(2)}) copy-start(f32[8,16,256]{2,1,0:T(8,128)} %rhs_hbm.1) | copy-start | bytes 393220

commit v5 on v4

--- a/solution.py
+++ b/solution.py
@@ -350,9 +350,9 @@
 FACTOR = relax_weight / 6.0
 SELF = 1.0 - 6.0 * FACTOR
 LANES = 128
-OWN_ROWS = 64
+OWN_ROWS = 56
 ROOT_ROW = 32
-MSG_ROWS = 32
+MSG_ROWS = 24
 VMEM_LIMIT = 16 * 1024 * 1024
 
 
@@ -479,17 +479,19 @@
     return lower, upper
 
 
-def coarse_x_pair(columns, up, down, index, half):
+def coarse_x_pair(columns, up, down, index, half, ring=False):
     chunk = columns[index][half]
     cell = lane_iota(chunk.shape) % 8
-    before = down[index - 1][half] if index > 0 else jnp.zeros_like(chunk)
-    after = up[index + 1][half] if index + 1 < len(columns) else jnp.zeros_like(chunk)
+    count = len(columns)
+    zero = jnp.zeros_like(chunk)
+    before = down[(index - 1) % count][half] if ring or index > 0 else zero
+    after = up[(index + 1) % count][half] if ring or index + 1 < count else zero
     low = turn(jnp.where(cell == 7, before, chunk), 1, 1)
     high = turn(jnp.where(cell == 0, after, chunk), -1, 1)
     return low, high
 
 
-def coarse_sums(columns):
+def coarse_sums(columns, ring=False):
     up, down = coarse_turns(columns)
 
     def sums(index):
@@ -497,7 +499,7 @@
         halves = []
         for half in range(2):
             chunk = columns[index][half]
-            low, high = coarse_x_pair(columns, up, down, index, half)
+            low, high = coarse_x_pair(columns, up, down, index, half, ring)
             total = low + high + lower[half] + upper[half]
             halves.append(total + turn(chunk, 1, 0) + turn(chunk, -1, 0))
         return halves
@@ -669,7 +671,7 @@
 def push_kernel(
     sub_count, blk_count, blk_bits,
     leaf_hbm, parent_hbm, child_hbm, place_hbm, owner_hbm, rhs_hbm,
-    placed, own_ref, leaf_out, parent_ref, child_ref, place_ref, owner_out, *rest
+    placed, own_ref, root_ref, leaf_out, parent_ref, child_ref, place_ref, owner_out, *rest
 ):
     msg_refs = rest[:blk_bits]
     leaf_ref, rhs_ref, rows_s, rows_g, left_a, coarse_s, sems = rest[blk_bits:]
@@ -742,10 +744,6 @@
     for copy in copies[3:]:
         copy.wait()
     out_a = split_dot(left_a[...], table_a)
-    own_code = of_own(child_ref, codes, blocks, sub_count, sub_here, blk_here)
-    good = lists_agree(
-        sub_count, blk_count, leaf_ref, leaf_out, parent_ref, child_ref, place_ref, codes, own_code
-    )
     lane24 = lane_iota((24, LANES))
     main = []
     side = []
@@ -768,53 +766,50 @@
     cell8 = lane24 % 8
     row24 = row_iota((24, LANES))
     inside_z = jnp.where(row24 < 4, z_low, jnp.where(row24 >= 20, z_high, 1.0))
-    gain = [inside_z * x_low, inside_z, inside_z * x_high]
     main24 = [own_ref[0:24, 0:LANES], own_ref[0:24, LANES:256]]
     side24 = [own_ref[24:48, 0:LANES], own_ref[24:48, LANES:256]]
-    columns = [
-        [jnp.where(cell8 == 7, piece, 0.0) * x_low for piece in side24],
-        main24,
-        [jnp.where(cell8 == 0, piece, 0.0) * x_high for piece in side24],
-    ]
-    sums = coarse_sums(columns)
+    gain = [inside_z, inside_z * jnp.where(cell8 < 4, x_high, x_low)]
+    columns = [main24, [gain[1] * piece for piece in side24]]
+    sums = coarse_sums(columns, ring=True)
     wp = []
-    for b in range(3):
+    for b in range(2):
         near = sums(b)
         wp.append([gain[b] * (SELF * columns[b][h] + f * near[h]) for h in range(2)])
-    sums = coarse_sums(wp)
+    sums = coarse_sums(wp, ring=True)
     zero8 = jnp.zeros((8, LANES), jnp.float32)
-    for b in range(3):
+    pieces = []
+    for b in range(2):
         near = sums(b)
         for h in range(2):
-            coarse_s[2 * b + h, 0:24] = gain[b] * (SELF * wp[b][h] + f * near[h])
-            coarse_s[2 * b + h, 24:32] = zero8
-    pieces = []
-    low_cells = lane_iota((8, LANES)) % 8 < 4
-    for k in range(6):
+            k = 2 * b + h
+            coarse_s[k, 0:24] = gain[b] * (SELF * wp[b][h] + f * near[h])
+            coarse_s[k, 24:32] = zero8
+    for k in range(4):
         pieces.append(
             coarse_s[k, pl.ds(0, 8, stride=4), :]
             + coarse_s[k, pl.ds(1, 8, stride=4), :]
             + coarse_s[k, pl.ds(2, 8, stride=4), :]
             + coarse_s[k, pl.ds(3, 8, stride=4), :]
         )
-    outer = [jnp.where(low_cells, pieces[4 + h], pieces[h]) for h in range(2)]
-    root_left = jnp.concatenate([pieces[2], pieces[3]] + outer, axis=1)
+    root_left = jnp.concatenate(pieces, axis=1)
     root_lanes = 16 * sub_count
     root_part = split_dot(root_left, table_r)
     root_part = pltpu.roll(root_part, 2 * sub_here + root_lanes - 1, 1)
-    root_part = jnp.where(row_iota(root_part.shape) < 6, root_part, 0.0)
-    own_ref[48:56, 0:root_lanes] = root_part
+    own_code = of_own(child_ref, codes, blocks, sub_count, sub_here, blk_here)
+    good = lists_agree(
+        sub_count, blk_count, leaf_ref, leaf_out, parent_ref, child_ref, place_ref, codes, own_code
+    )
     if root_lanes < 256:
-        own_ref[48:56, root_lanes:256] = jnp.zeros((8, 256 - root_lanes), jnp.float32)
-    flag = jnp.zeros((8, LANES), jnp.float32) + good
-    for lanes in (slice(0, LANES), slice(LANES, 256)):
-        own_ref[56:64, lanes] = flag
+        root_part = jnp.concatenate(
+            [root_part, jnp.zeros((8, 256 - root_lanes), jnp.float32)], axis=1
+        )
+    root_part = jnp.where(row_iota(root_part.shape) < 6, root_part, good)
+    own_ref[48:56, :] = root_part
+    root_ref[...] = root_part
     for bit in range(blk_bits):
         upward = (blk_here // (1 << bit)) % 2 == 0
         ref = msg_refs[bit]
-        ref[8:16, :] = own_ref[48:56, :]
-        ref[24:32, 0:LANES] = zero8
-        ref[24:32, LANES:256] = flag
+        ref[8:16, :] = root_part
         for base_row, source in ((0, 0), (4, 24)):
             ref[base_row : base_row + 4, :] = jnp.where(
                 upward, own_ref[source + 17 : source + 21, :], own_ref[source + 3 : source + 7, :]
@@ -902,9 +897,16 @@
     cell8 = lane_iota((8, LANES)) % 8
     low_rows = (row8 >= 1) & (row8 < 5)
     high_rows = (row8 >= 3) & (row8 < 7)
-    good = own_ref[56:64, 0:LANES]
-    for ref in msg_refs:
-        good = jnp.minimum(good, ref[24:32, LANES:256])
+
+    def root_rows(d, lanes):
+        if d == 0:
+            return own_ref[48:56, lanes]
+        ref = msg_refs[d - 1]
+        return ref[0:8, lanes] if ref.shape[0] == 8 else ref[8:16, lanes]
+
+    good = root_rows(0, slice(0, LANES))
+    for d in range(1, blk_count):
+        good = jnp.minimum(good, root_rows(d, slice(0, LANES)))
     for half in range(2):
         lanes = slice(LANES * half, LANES * half + LANES)
         low = below(slice(0, 8), lanes) * z_low
@@ -927,13 +929,13 @@
                 packed = packed + turn(jnp.where(cell8 == 0, tiles[1][g], 0.0), g, 1)
                 packed = packed + turn(jnp.where(cell8 == 7, tiles[1][g], 0.0), -g, 1)
         out_ref[24:32, lanes] = packed
-        out_ref[23:24, lanes] = good[0:1]
+        out_ref[23:24, lanes] = good[7:8]
     root_s[...] = jnp.zeros(root_s.shape, jnp.float32)
     for d in range(blk_count):
         start = 4 * (blk_here ^ d) + 3
         for part in range(root_s.shape[0]):
             lanes = slice(LANES * part, LANES * part + LANES)
-            value = own_ref[48:56, lanes] if d == 0 else msg_refs[d - 1][8:16, lanes]
+            value = jnp.where(row8 < 6, root_rows(d, lanes), 0.0)
             root_s[part, pl.ds(start, 8), :] = root_s[part, pl.ds(start, 8), :] + value
     tile = 0
     for start in range(0, 4 * blk_count, 8):
@@ -988,10 +990,14 @@
 
 def solve_kernel(
     sub_count, blk_count, slots,
-    positions, owned, all_ref, pair_ref, part_ref, lines_ref, table_w_ref, table_p_ref, table_l_ref, table_x_ref,
+    positions_in, owned_in, all_ref, pair_ref, part_ref, lines_ref, table_w_ref, table_p_ref, table_l_ref, table_x_ref,
     leaf_ref, parent_ref, good_ref,
-    placed, par_s, root_s, fine_s, push_s
+    placed, par_s, root_s, fine_s, push_s, positions, owned, sems
 ):
+    position_copy = pltpu.make_async_copy(positions_in, positions, sems.at[0])
+    owned_copy = pltpu.make_async_copy(owned_in, owned, sems.at[1])
+    position_copy.start()
+    owned_copy.start()
     blocks = part_ref.shape[0]
     wide_y = blocks // 2
     f = FACTOR
@@ -1066,6 +1072,56 @@
         total = total + jnp.where(row < root_rows - 1, turn(values, -1, 0), 0.0)
         return SELF * values + f * (root_source + total)
 
+    before = jnp.maximum(sub_here - 1, 0)
+    after = jnp.minimum(sub_here + 1, sub_count - 1)
+    slot_before = exchange_slot(sub_count, sub_here ^ before)
+    slot_after = exchange_slot(sub_count, sub_here ^ after)
+    line = ROOT_ROW + 8 * root_tiles(sub_count, blk_count)
+    even = sub_here % 2 == 0
+
+    def crossed(slot):
+        rows = all_ref[slot, line + 8 : line + 24, :]
+        return jnp.concatenate([rows[:, 0:LANES], rows[:, LANES:256]], axis=0)
+
+    pair = pair_ref[...]
+    from_low = jnp.where(even, crossed(slot_before), pair) * x_low
+    from_high = jnp.where(even, pair, crossed(slot_after)) * x_high
+    behind = jnp.where(lane_iota((32, LANES)) < 64, 1.0, f2)
+    left = [from_low * behind, from_high * behind]
+    lane128 = lane_iota((32, LANES))
+    rows = []
+    for yy in range(wide_y):
+        rows.append(
+            jnp.where(
+                lax.rem(lane128, 64) < 16,
+                turn(left[0], -16 * yy, 1),
+                turn(left[1], 16 - 16 * yy, 1),
+            )
+        )
+    push = split_dot(jnp.concatenate(rows, axis=0), table_x_ref[...])
+    for yy in range(wide_y):
+        push_s[:, 256 * yy : 256 * yy + 256] = push[32 * yy : 32 * yy + 32]
+    cell = lane_iota((2 * wide_y, 256)) % 16
+    across = jnp.where(
+        cell == 0, turn(all_ref[slot_before, line : line + 2 * wide_y, :], -15, 1) * x_low, 0.0
+    ) + jnp.where(
+        cell == 15, turn(all_ref[slot_after, line : line + 2 * wide_y, :], 15, 1) * x_high, 0.0
+    )
+    across = (2.0 * f2) * across
+    count = 2 * wide_y
+    for yy in range(wide_y):
+        lanes = slice(256 * yy, 256 * yy + 256)
+        push_s[0:1, lanes] = push_s[0:1, lanes] + lines_ref[yy : yy + 1] + across[yy : yy + 1]
+        push_s[1:2, lanes] = push_s[1:2, lanes] + f2 * lines_ref[wide_y + yy : wide_y + yy + 1]
+        push_s[31:32, lanes] = (
+            push_s[31:32, lanes]
+            + lines_ref[count + yy : count + yy + 1]
+            + across[wide_y + yy : wide_y + yy + 1]
+        )
+        push_s[30:31, lanes] = (
+            push_s[30:31, lanes]
+            + f2 * lines_ref[count + wide_y + yy : count + wide_y + yy + 1]
+        )
     values = f * root_source
     left_sweeps = ROOT_SWEEPS - 1
     sums = coarse_sums(source)
@@ -1121,6 +1177,7 @@
             value = SELF * three[c][half] + f * (near[half] + source[c][half])
             par_s[c, half] = jnp.where(valid, value, 0.0)
 
+    owned_copy.wait()
     pieces = []
     for k in range(slots):
         half = owned[3 * k]
@@ -1137,8 +1194,6 @@
     for k in range(slots):
         parent_ref[k] = moved[16 * k : 16 * k + 16]
 
-    before = jnp.maximum(sub_here - 1, 0)
-    after = jnp.minimum(sub_here + 1, sub_count - 1)
     columns = [
         [par_s[before, half] * x_low for half in range(2)],
         [par_s[sub_here, half] for half in range(2)],
@@ -1179,54 +1234,6 @@
             fine_s[2 * yy, pl.ds(zp, 16, stride=2), :] = spread[top : top + 16, 0:128]
             fine_s[2 * yy + 1, pl.ds(zp, 16, stride=2), :] = spread[top : top + 16, 128:256]
 
-    slot_before = exchange_slot(sub_count, sub_here ^ before)
-    slot_after = exchange_slot(sub_count, sub_here ^ after)
-    line = ROOT_ROW + 8 * root_tiles(sub_count, blk_count)
-    even = sub_here % 2 == 0
-
-    def crossed(slot):
-        rows = all_ref[slot, line + 8 : line + 24, :]
-        return jnp.concatenate([rows[:, 0:LANES], rows[:, LANES:256]], axis=0)
-
-    pair = pair_ref[...]
-    from_low = jnp.where(even, crossed(slot_before), pair) * x_low
-    from_high = jnp.where(even, pair, crossed(slot_after)) * x_high
-    behind = jnp.where(lane_iota((32, LANES)) < 64, 1.0, f2)
-    left = [from_low * behind, from_high * behind]
-    lane128 = lane_iota((32, LANES))
-    rows = []
-    for yy in range(wide_y):
-        rows.append(
-            jnp.where(
-                lax.rem(lane128, 64) < 16,
-                turn(left[0], -16 * yy, 1),
-                turn(left[1], 16 - 16 * yy, 1),
-            )
-        )
-    push = split_dot(jnp.concatenate(rows, axis=0), table_x_ref[...])
-    for yy in range(wide_y):
-        push_s[:, 256 * yy : 256 * yy + 256] = push[32 * yy : 32 * yy + 32]
-    cell = lane_iota((2 * wide_y, 256)) % 16
-    across = jnp.where(
-        cell == 0, turn(all_ref[slot_before, line : line + 2 * wide_y, :], -15, 1) * x_low, 0.0
-    ) + jnp.where(
-        cell == 15, turn(all_ref[slot_after, line : line + 2 * wide_y, :], 15, 1) * x_high, 0.0
-    )
-    across = (2.0 * f2) * across
-    count = 2 * wide_y
-    for yy in range(wide_y):
-        lanes = slice(256 * yy, 256 * yy + 256)
-        push_s[0:1, lanes] = push_s[0:1, lanes] + lines_ref[yy : yy + 1] + across[yy : yy + 1]
-        push_s[1:2, lanes] = push_s[1:2, lanes] + f2 * lines_ref[wide_y + yy : wide_y + yy + 1]
-        push_s[31:32, lanes] = (
-            push_s[31:32, lanes]
-            + lines_ref[count + yy : count + yy + 1]
-            + across[wide_y + yy : wide_y + yy + 1]
-        )
-        push_s[30:31, lanes] = (
-            push_s[30:31, lanes]
-            + f2 * lines_ref[count + wide_y + yy : count + wide_y + yy + 1]
-        )
     for zz in range(2):
         for yy in range(wide_y):
             rows = slice(16 * zz, 16 * zz + 16)
@@ -1234,6 +1241,7 @@
             index = zz * wide_y + yy
             fine = jnp.concatenate([fine_s[2 * yy, rows], fine_s[2 * yy + 1, rows]], axis=1)
             placed[index] = part_ref[index] + fine + f * push_s[rows, lanes]
+    position_copy.wait()
     for slot in range(blocks):
         leaf_ref[slot] = placed[positions[slot]]
 
@@ -1271,6 +1279,7 @@
         out_shape=[
             jax.ShapeDtypeStruct(grid_shape, f32),
             jax.ShapeDtypeStruct((OWN_ROWS, 256), f32),
+            jax.ShapeDtypeStruct((8, 256), f32),
         ]
         + [
             jax.ShapeDtypeStruct(array.shape, jnp.int32)
@@ -1278,14 +1287,14 @@
         ]
         + [jax.ShapeDtypeStruct((MSG_ROWS, 256), f32)] * blk_bits,
         in_specs=[pl.BlockSpec(memory_space=pltpu.HBM)] * 6,
-        out_specs=[vmem] * (7 + blk_bits),
+        out_specs=[vmem] * (8 + blk_bits),
         scratch_shapes=[
             pltpu.SMEM(leaf_neighbors.shape, jnp.int32),
             pltpu.VMEM(grid_shape, f32),
             pltpu.VMEM((2 * wide_y, 32, LANES), f32),
             pltpu.VMEM((2 * wide_y, 32, LANES), f32),
             pltpu.VMEM((48 * wide_y, 256), f32),
-            pltpu.VMEM((6, 32, LANES), f32),
+            pltpu.VMEM((4, 32, LANES), f32),
             pltpu.SemaphoreType.DMA((7,)),
         ],
         compiler_params=params,
@@ -1295,16 +1304,15 @@
             for array in (leaf_neighbors, parent_rows, child_rows, place_row, owner_row, rhs)
         )
     )
-    placed, own, leaf_neighbors, parent_rows, child_rows, place_row, owner_row = outs[:7]
-    messages = outs[7:]
+    placed, own, root_tile, leaf_neighbors, parent_rows, child_rows, place_row, owner_row = outs[:8]
+    messages = outs[8:]
     lists = (
         leaf_neighbors, parent_rows.T, child_rows.T, owner_row.reshape(-1), place_row.reshape(-1),
     )
     received = []
     for d in range(1, blk_count):
-        received.append(
-            lax.ppermute(messages[d.bit_length() - 1], "blk", paired(blk_count, d))
-        )
+        message = messages[d.bit_length() - 1] if is_power(d + 1) else root_tile
+        received.append(lax.ppermute(message, "blk", paired(blk_count, d)))
     positions, owned, own_part, cross_faces, pair_faces = pl.pallas_call(
         functools.partial(side_kernel, sub_count, blk_count, PMOST),
         name="side",
@@ -1348,7 +1356,7 @@
             jax.ShapeDtypeStruct((PMOST, 16, 256), f32),
             jax.ShapeDtypeStruct((1,), jnp.int32),
         ],
-        in_specs=[smem] * 2 + [vmem] * 8,
+        in_specs=[pl.BlockSpec(memory_space=pl.ANY)] * 2 + [vmem] * 8,
         out_specs=[vmem] * 2 + [smem],
         scratch_shapes=[
             pltpu.VMEM((blocks, 16, 256), f32),
@@ -1356,6 +1364,9 @@
             pltpu.VMEM((root_parts, 4 * blk_count + 8, LANES), f32),
             pltpu.VMEM((2 * wide_y, 32, LANES), f32),
             pltpu.VMEM((32, 256 * wide_y), f32),
+            pltpu.SMEM((blocks,), jnp.int32),
+            pltpu.SMEM((3 * PMOST,), jnp.int32),
+            pltpu.SemaphoreType.DMA((2,)),
         ],
         compiler_params=params,
     )(

time: 28.5 us -> 26.7 us (0.937)
  waiting for transfers between devices: 10.6 us -> 9.31 us
  Pallas kernels: 6.53 us -> 6 us
    ppermute x3, waiting for transfers between devices: 4.46 us -> 3.2 us  [local(): received.append(lax.ppermute(message, 'blk', paired(blk_count, d)))]
    pallas_call x1, Pallas kernels: 2.92 us -> 2.39 us  [local(): pl.pallas_call(functools.partial(solve_kernel, sub_count, blk_count, PMOS...]
  transfers between devices with their start and end apart: 8 -> 8, of which waited for: 6 -> 5; matrix products, arithmetic and copies ran while one was open for 0% -> 0% of each run, Pallas kernels for 4% -> 5%
where the time goes in v5:
time: 26.7 us; the launch traced here: 26.5 us
  starting transfers between devices  9.35 us (35%)
  waiting for transfers between devices  9.31 us (35%)
  Pallas kernels  6 us (22%)
  between operations  0.98 us (4%)
  loops' own time  0.79 us (3%)
    ppermute x3, starting transfers between devices, local(): received.append(lax.ppermute(message, 'blk', paired(blk_count, d)))  5.71 us
    ppermute x3, waiting for transfers between devices, local(): block.append(lax.ppermute(joined, 'sub', paired(sub_count, d)))  4.68 us
    ppermute x3, starting transfers between devices, local(): block.append(lax.ppermute(joined, 'sub', paired(sub_count, d)))  3.51 us
    ppermute x3, waiting for transfers between devices, local(): received.append(lax.ppermute(message, 'blk', paired(blk_count, d)))  3.2 us
    pallas_call x1, Pallas kernels, local(): pl.pallas_call(functools.partial(solve_kernel, sub_count, blk_count, PMOS...  2.39 us
    pallas_call x1, Pallas kernels, local(): pl.pallas_call(functools.partial(push_kernel, sub_count, blk_count, blk_b...  2.37 us
    ppermute x1, waiting for transfers between devices, local(): other = lax.ppermute(block, 'sub', paired(sub_count, 1))  1.43 us
    pallas_call x1, Pallas kernels, local(): pl.pallas_call(functools.partial(side_kernel, sub_count, blk_count, PMOST...  1.15 us
  transfers between devices with their start and end apart: 8, of which 5 were waited for; matrix products, arithmetic and copies ran while one was open for 0% of the time, Pallas kernels for 5%

profile of v5, /device:TPU:0, one launch (start us, length us, event | category | flops | bytes accessed | tf_op | source)
XLA Modules:
  0.0 26.5 jit_solution(17236160457579975920)
XLA Ops:
  0.6 0.0 copy-start.4
  0.6 2.4 %push.1 = (f32[8,16,256]{2,1,0:T(8,128)S(1)}, f32[56,256]{1,0:T(8,128)S(1)}, f32[8,256]{1,0:T(8,128)S(1)}, s32[8,6]{1,0:T(8,128)S(1)}, s32[6,32]{1,0:T(8,128)S(1...) custom-call(s32[8,6]{1,0:T(8,128)} %leaf_hbm.1, ...), custom_call_target="tpu_custom_call" | custom-call | tf_op jit(solution)/shard_map/push/pallas_call | solution.py:1276
  3.0 3.1 %collective-permute-start.18 = (f32[24,256]{1,0:T(8,128)S(1)}, f32[24,256]{1,0:T(8,128)S(1)}, u32[]{:S(2)}, u32[]{:S(2)}) collective-permute-start(f32[24,256]{1,0:T(8,128)S(1)} %get-tuple-element.92), channel_id=1, source_target_pairs={{0,8},{8,0},{16,24},{24,16},{1,9},{9,1},{17,25},{25,17},{2,10},{10... | collective-permute-start | bytes 73736 | tf_op jit(solution)/shard_map/ppermute | solution.py:1315
  6.1 2.5 %collective-permute-start.20 = (f32[24,256]{1,0:T(8,128)S(1)}, f32[24,256]{1,0:T(8,128)S(1)}, u32[]{:S(2)}, u32[]{:S(2)}) collective-permute-start(f32[24,256]{1,0:T(8,128)S(1)} %get-tuple-element.94), channel_id=1, source_target_pairs={{0,24},{8,16},{16,8},{24,0},{1,25},{9,17},{17,9},{25,1},{2,26},{10... | collective-permute-start | bytes 73736 | tf_op jit(solution)/shard_map/ppermute | solution.py:1315
  8.6 0.1 collective-permute-start.19
  8.7 1.1 %side.1 = (s32[8]{0:T(128)S(1)}, s32[9]{0:T(128)S(1)}, f32[8,16,256]{2,1,0:T(8,128)S(1)}, f32[32,128]{1,0:T(8,128)S(1)}, f32[32,128]{1,0:T(8,128)S(1)}) custom-call(s32[8,32]{1,0:T(8,128)S(1)} %get-tuple-element.84.child_ref, s32[1,32]{1,0:T(1,128)S(1)} %get-tuple-element.348.owner_ref, s32[1,32]{1,0:T(1,128)S(1)} %get-tuple-element.86.place_ref, ...), custom_call_target="tpu_custom_call" | custom-call | tf_op jit(solution)/shard_map/side/pallas_call | solution.py:1316
  9.9 0.1 collective-permute-start.25
  10.0 3.2 %collective-permute-done.19.rest_1_ = f32[8,256]{1,0:T(8,128)S(1)} collective-permute-done((f32[8,256]{1,0:T(8,128)S(1)}, f32[8,256]{1,0:T(8,128)S(1)}, u32[]{:S(2)}, u32[]{:S(2)}) %collective-permute-start.19) | collective-permute-done | bytes 8224 | tf_op jit(solution)/shard_map/ppermute | solution.py:1315
  13.2 0.1 join.1
  13.3 1.5 %collective-permute-start.21 = (f32[64,256]{1,0:T(8,128)S(1)}, f32[64,256]{1,0:T(8,128)S(1)}, u32[]{:S(2)}, u32[]{:S(2)}) collective-permute-start(f32[64,256]{1,0:T(8,128)S(1)} %get-tuple-element.95), channel_id=1, source_target_pairs={{0,2},{1,3},{2,0},{3,1},{4,6},{5,7},{6,4},{7,5},{8,10},{9,11},{10,... | collective-permute-start | bytes 196616 | tf_op jit(solution)/shard_map/ppermute | solution.py:1347
  14.8 1.5 %collective-permute-start.22 = (f32[64,256]{1,0:T(8,128)S(1)}, f32[64,256]{1,0:T(8,128)S(1)}, u32[]{:S(2)}, u32[]{:S(2)}) collective-permute-start(f32[64,256]{1,0:T(8,128)S(1)} %get-tuple-element.95), channel_id=1, source_target_pairs={{0,4},{1,5},{2,6},{3,7},{4,0},{5,1},{6,2},{7,3},{8,12},{9,13},{10,... | collective-permute-start | bytes 196616 | tf_op jit(solution)/shard_map/ppermute | solution.py:1347
  16.3 0.5 %collective-permute-start.23 = (f32[64,256]{1,0:T(8,128)S(1)}, f32[64,256]{1,0:T(8,128)S(1)}, u32[]{:S(2)}, u32[]{:S(2)}) collective-permute-start(f32[64,256]{1,0:T(8,128)S(1)} %get-tuple-element.95), channel_id=1, source_target_pairs={{0,6},{1,7},{2,4},{3,5},{4,2},{5,3},{6,0},{7,1},{8,14},{9,15},{10,... | collective-permute-start | bytes 196616 | tf_op jit(solution)/shard_map/ppermute | solution.py:1347
  16.8 1.3 %collective-permute-done.21 = f32[64,256]{1,0:T(8,128)S(1)} collective-permute-done((f32[64,256]{1,0:T(8,128)S(1)}, f32[64,256]{1,0:T(8,128)S(1)}, u32[]{:S(2)}, u32[]{:S(2)}) %collective-permute-start.21) | collective-permute-done | bytes 65568 | tf_op jit(solution)/shard_map/ppermute | solution.py:1347
  18.1 1.2 %collective-permute-done.22 = f32[64,256]{1,0:T(8,128)S(1)} collective-permute-done((f32[64,256]{1,0:T(8,128)S(1)}, f32[64,256]{1,0:T(8,128)S(1)}, u32[]{:S(2)}, u32[]{:S(2)}) %collective-permute-start.22) | collective-permute-done | bytes 65568 | tf_op jit(solution)/shard_map/ppermute | solution.py:1347
  19.3 2.1 %collective-permute-done.23 = f32[64,256]{1,0:T(8,128)S(1)} collective-permute-done((f32[64,256]{1,0:T(8,128)S(1)}, f32[64,256]{1,0:T(8,128)S(1)}, u32[]{:S(2)}, u32[]{:S(2)}) %collective-permute-start.23) | collective-permute-done | bytes 65568 | tf_op jit(solution)/shard_map/ppermute | solution.py:1347
  21.5 0.1 collective-permute-start.24
  21.6 0.0 copy-start
  21.6 0.0 copy-start.1
  21.6 0.0 copy-start.2
  21.6 0.0 copy-start.3
  21.7 1.4 %collective-permute-done.24 = f32[4,64,256]{2,1,0:T(8,128)S(1)} collective-permute-done((f32[4,64,256]{2,1,0:T(8,128)S(1)}, f32[4,64,256]{2,1,0:T(8,128)S(1)}, u32[]{:S(2)}, u32[]{:S(2)}) %collective-permute-start.24) | collective-permute-done | bytes 262176 | tf_op jit(solution)/shard_map/ppermute | solution.py:1349
  23.2 0.0 copy-start.5
  23.2 2.4 %solve.1 = (f32[8,16,256]{2,1,0:T(8,128)}, f32[3,16,256]{2,1,0:T(8,128)}, s32[1]{0:T(128)}) custom-call(s32[8]{0:T(128)S(1)} %get-tuple-element.88.positions_in, s32[9]{0:T(128)S(1)} %get-tuple-element.89.owned_in, f32[8,64,256]{2,1,0:T(8,128)S(1)} %constant_dynamic-update-slice_fusion.15.all_ref, f32[32,128]{1,0:T(8,128)S(1)} %collective-permute-done.25.pair_ref, ...), custom_call_target="tpu_custom_call" | custom-call | tf_op jit(solution)/shard_map/solve/pallas_call | solution.py:1351
  25.6 0.8 %while.13 = (f32[8,16,256]{2,1,0:T(8,128)}, f32[3,16,256]{2,1,0:T(8,128)}, s32[1]{0:T(128)}, f32[8,16,256]{2,1,0:T(8,128)S(1)}, s32[8,6]{1,0:T(8,128)S(1)}, /*in...) while((f32[8,16,256]{2,1,0:T(8,128)}, ...), condition=%region_9.12_spmd.clone.clone, body=%region_0.11_spmd.sunk.clone.clone | while | flops 309503840 | bytes 22817100 | solution.py:1381
  (15 shorter events, 0.1 us)
Async XLA Ops:
  0.6 8.1 %copy-start.4 = (bf16[256,128]{1,0:T(8,128)(2,1)S(1)}, bf16[256,128]{1,0:T(8,128)(2,1)}, u32[]{:S(2)}) copy-start(bf16[256,128]{1,0:T(8,128)(2,1)} %constant.451.clone.table_ref) | copy-start | bytes 196612
  3.0 10.1 %collective-permute-start.18 = (f32[24,256]{1,0:T(8,128)S(1)}, f32[24,256]{1,0:T(8,128)S(1)}, u32[]{:S(2)}, u32[]{:S(2)}) collective-permute-start(f32[24,256]{1,0:T(8,128)S(1)} %get-tuple-element.92), channel_id=1, source_target_pairs={{0,8},{8,0},{16,24},{24,16},{1,9},{9,1},{17,25},{25,17},{2,10},{10... | collective-permute-start | bytes 73736 | tf_op jit(solution)/shard_map/ppermute | solution.py:1315
  6.1 7.0 %collective-permute-start.20 = (f32[24,256]{1,0:T(8,128)S(1)}, f32[24,256]{1,0:T(8,128)S(1)}, u32[]{:S(2)}, u32[]{:S(2)}) collective-permute-start(f32[24,256]{1,0:T(8,128)S(1)} %get-tuple-element.94), channel_id=1, source_target_pairs={{0,24},{8,16},{16,8},{24,0},{1,25},{9,17},{17,9},{25,1},{2,26},{10... | collective-permute-start | bytes 73736 | tf_op jit(solution)/shard_map/ppermute | solution.py:1315
  8.6 4.5 %collective-permute-start.19 = (f32[8,256]{1,0:T(8,128)S(1)}, f32[8,256]{1,0:T(8,128)S(1)}, u32[]{:S(2)}, u32[]{:S(2)}) collective-permute-start(f32[8,256]{1,0:T(8,128)S(1)} %get-tuple-element.93), channel_id=1, source_target_pairs={{0,16},{8,24},{16,0},{24,8},{1,17},{9,25},{17,1},{25,9},{2,18},{10... | collective-permute-start | bytes 24584 | tf_op jit(solution)/shard_map/ppermute | solution.py:1315
  9.9 13.2 %collective-permute-start.25 = (f32[32,128]{1,0:T(8,128)S(1)}, f32[32,128]{1,0:T(8,128)S(1)}, u32[]{:S(2)}, u32[]{:S(2)}) collective-permute-start(f32[32,128]{1,0:T(8,128)S(1)} %get-tuple-element.96), channel_id=1, source_target_pairs={{0,1},{1,0},{2,3},{3,2},{4,5},{5,4},{6,7},{7,6},{8,9},{9,8},{10,11... | collective-permute-start | bytes 49160 | tf_op jit(solution)/shard_map/ppermute | solution.py:1330
  13.3 4.8 %collective-permute-start.21 = (f32[64,256]{1,0:T(8,128)S(1)}, f32[64,256]{1,0:T(8,128)S(1)}, u32[]{:S(2)}, u32[]{:S(2)}) collective-permute-start(f32[64,256]{1,0:T(8,128)S(1)} %get-tuple-element.95), channel_id=1, source_target_pairs={{0,2},{1,3},{2,0},{3,1},{4,6},{5,7},{6,4},{7,5},{8,10},{9,11},{10,... | collective-permute-start | bytes 196616 | tf_op jit(solution)/shard_map/ppermute | solution.py:1347
  14.8 4.5 %collective-permute-start.22 = (f32[64,256]{1,0:T(8,128)S(1)}, f32[64,256]{1,0:T(8,128)S(1)}, u32[]{:S(2)}, u32[]{:S(2)}) collective-permute-start(f32[64,256]{1,0:T(8,128)S(1)} %get-tuple-element.95), channel_id=1, source_target_pairs={{0,4},{1,5},{2,6},{3,7},{4,0},{5,1},{6,2},{7,3},{8,12},{9,13},{10,... | collective-permute-start | bytes 196616 | tf_op jit(solution)/shard_map/ppermute | solution.py:1347
  16.3 5.2 %collective-permute-start.23 = (f32[64,256]{1,0:T(8,128)S(1)}, f32[64,256]{1,0:T(8,128)S(1)}, u32[]{:S(2)}, u32[]{:S(2)}) collective-permute-start(f32[64,256]{1,0:T(8,128)S(1)} %get-tuple-element.95), channel_id=1, source_target_pairs={{0,6},{1,7},{2,4},{3,5},{4,2},{5,3},{6,0},{7,1},{8,14},{9,15},{10,... | collective-permute-start | bytes 196616 | tf_op jit(solution)/shard_map/ppermute | solution.py:1347
  21.5 1.6 %collective-permute-start.24 = (f32[4,64,256]{2,1,0:T(8,128)S(1)}, f32[4,64,256]{2,1,0:T(8,128)S(1)}, u32[]{:S(2)}, u32[]{:S(2)}) collective-permute-start(f32[4,64,256]{2,1,0:T(8,128)S(1)} %pad_maximum_fusion.3), channel_id=1, source_target_pairs={{0,1},{1,0},{2,3},{3,2},{4,5},{5,4},{6,7},{7,6},{8,9},{9,8},{10,11... | collective-permute-start | bytes 786440 | tf_op jit(solution)/shard_map/ppermute | solution.py:1349
  21.6 1.5 %copy-start = (bf16[256,256]{1,0:T(8,128)(2,1)S(1)}, bf16[256,256]{1,0:T(8,128)(2,1)}, u32[]{:S(2)}) copy-start(bf16[256,256]{1,0:T(8,128)(2,1)} %constant.453.clone.table_p_ref) | copy-start | bytes 393220
  21.6 1.5 %copy-start.1 = (bf16[256,256]{1,0:T(8,128)(2,1)S(1)}, bf16[256,256]{1,0:T(8,128)(2,1)}, u32[]{:S(2)}) copy-start(bf16[256,256]{1,0:T(8,128)(2,1)} %constant.454.clone.table_l_ref) | copy-start | bytes 393220
  21.6 1.5 %copy-start.2 = (bf16[128,256]{1,0:T(8,128)(2,1)S(1)}, bf16[128,256]{1,0:T(8,128)(2,1)}, u32[]{:S(2)}) copy-start(bf16[128,256]{1,0:T(8,128)(2,1)} %constant.452.clone.table_w_ref) | copy-start | bytes 196612
  21.6 1.5 %copy-start.3 = (bf16[128,256]{1,0:T(8,128)(2,1)S(1)}, bf16[128,256]{1,0:T(8,128)(2,1)}, u32[]{:S(2)}) copy-start(bf16[128,256]{1,0:T(8,128)(2,1)} %constant.455.clone.table_x_ref) | copy-start | bytes 196612
  23.2 2.4 %copy-start.5 = (f32[8,16,256]{2,1,0:T(8,128)S(1)}, f32[8,16,256]{2,1,0:T(8,128)}, u32[]{:S(2)}) copy-start(f32[8,16,256]{2,1,0:T(8,128)} %rhs_hbm.1) | copy-start | bytes 393220

commit v6 on v5

--- a/solution.py
+++ b/solution.py
@@ -741,8 +741,6 @@
         left_a[line + 24 : line + 40, half] = (
             rows_g[k, pl.ds(0, 16, stride=2), :] + rows_g[k, pl.ds(1, 16, stride=2), :]
         )
-    for copy in copies[3:]:
-        copy.wait()
     out_a = split_dot(left_a[...], table_a)
     lane24 = lane_iota((24, LANES))
     main = []
@@ -795,6 +793,8 @@
     root_lanes = 16 * sub_count
     root_part = split_dot(root_left, table_r)
     root_part = pltpu.roll(root_part, 2 * sub_here + root_lanes - 1, 1)
+    for copy in copies[3:]:
+        copy.wait()
     own_code = of_own(child_ref, codes, blocks, sub_count, sub_here, blk_here)
     good = lists_agree(
         sub_count, blk_count, leaf_ref, leaf_out, parent_ref, child_ref, place_ref, codes, own_code
@@ -1342,12 +1342,13 @@
         scratch_shapes=[pltpu.VMEM((root_parts, 4 * blk_count + 8, LANES), f32)],
         compiler_params=params,
     )(own, cross_faces, *received)
-    block = [joined]
+    ring = []
     for d in range(2, sub_count, 2):
-        block.append(lax.ppermute(joined, "sub", paired(sub_count, d)))
-    block = jnp.stack(block)
-    other = lax.ppermute(block, "sub", paired(sub_count, 1))
-    gathered = jnp.concatenate([block, other], axis=0)
+        ring.append(lax.ppermute(joined, "sub", paired(sub_count, d)))
+    partner = lax.ppermute(joined, "sub", paired(sub_count, 1))
+    ring = jnp.stack(ring)
+    other = lax.ppermute(ring, "sub", paired(sub_count, 1))
+    gathered = jnp.concatenate([joined[None], ring, partner[None], other], axis=0)
     leaf_solution, parent_solution, good = pl.pallas_call(
         functools.partial(solve_kernel, sub_count, blk_count, PMOST),
         name="solve",

time: 26.7 us -> 26.8 us (level)
    ppermute x4 -> x5, waiting for transfers between devices: 6.11 us -> 5.98 us  [the longest x3 4.67 us: local(): ring.append(lax.ppermute(joined, 'sub', paired(sub_count, d)))]
    ppermute x4 -> x5, starting transfers between devices: 3.58 us -> 3.58 us  [the longest x3 3.51 us: local(): ring.append(lax.ppermute(joined, 'sub', paired(sub_count, d)))]
  transfers between devices with their start and end apart: 8 -> 9, of which waited for: 5 -> 5; matrix products, arithmetic and copies ran while one was open for 0% -> 0% of each run, Pallas kernels for 5% -> 5%
where the time goes in v6:
time: 26.8 us; the launch traced here: 26.6 us
  starting transfers between devices  9.36 us (35%)
  waiting for transfers between devices  9.19 us (34%)
  Pallas kernels  6.17 us (23%)
  between operations  1 us (4%)
  loops' own time  0.79 us (3%)
    ppermute x3, starting transfers between devices, local(): received.append(lax.ppermute(message, 'blk', paired(blk_count, d)))  5.71 us
    ppermute x3, waiting for transfers between devices, local(): ring.append(lax.ppermute(joined, 'sub', paired(sub_count, d)))  4.67 us
    ppermute x3, starting transfers between devices, local(): ring.append(lax.ppermute(joined, 'sub', paired(sub_count, d)))  3.51 us
    ppermute x3, waiting for transfers between devices, local(): received.append(lax.ppermute(message, 'blk', paired(blk_count, d)))  3.2 us
    pallas_call x1, Pallas kernels, local(): pl.pallas_call(functools.partial(push_kernel, sub_count, blk_count, blk_b...  2.55 us
    pallas_call x1, Pallas kernels, local(): pl.pallas_call(functools.partial(solve_kernel, sub_count, blk_count, PMOS...  2.38 us
    ppermute x1, waiting for transfers between devices, local(): other = lax.ppermute(ring, 'sub', paired(sub_count, 1))  1.31 us
    pallas_call x1, Pallas kernels, local(): pl.pallas_call(functools.partial(side_kernel, sub_count, blk_count, PMOST...  1.15 us
  transfers between devices with their start and end apart: 9, of which 5 were waited for; matrix products, arithmetic and copies ran while one was open for 0% of the time, Pallas kernels for 5%

profile of v6, /device:TPU:0, one launch (start us, length us, event | category | flops | bytes accessed | tf_op | source)
XLA Modules:
  0.0 26.6 jit_solution(1122189563282944308)
XLA Ops:
  0.6 0.0 copy-start.4
  0.6 2.5 %push.1 = (f32[8,16,256]{2,1,0:T(8,128)S(1)}, f32[56,256]{1,0:T(8,128)S(1)}, f32[8,256]{1,0:T(8,128)S(1)}, s32[8,6]{1,0:T(8,128)S(1)}, s32[6,32]{1,0:T(8,128)S(1...) custom-call(s32[8,6]{1,0:T(8,128)} %leaf_hbm.1, ...), custom_call_target="tpu_custom_call" | custom-call | tf_op jit(solution)/shard_map/push/pallas_call | solution.py:1276
  3.2 3.1 %collective-permute-start.18 = (f32[24,256]{1,0:T(8,128)S(1)}, f32[24,256]{1,0:T(8,128)S(1)}, u32[]{:S(2)}, u32[]{:S(2)}) collective-permute-start(f32[24,256]{1,0:T(8,128)S(1)} %get-tuple-element.92), channel_id=1, source_target_pairs={{0,8},{8,0},{16,24},{24,16},{1,9},{9,1},{17,25},{25,17},{2,10},{10... | collective-permute-start | bytes 73736 | tf_op jit(solution)/shard_map/ppermute | solution.py:1315
  6.3 2.5 %collective-permute-start.20 = (f32[24,256]{1,0:T(8,128)S(1)}, f32[24,256]{1,0:T(8,128)S(1)}, u32[]{:S(2)}, u32[]{:S(2)}) collective-permute-start(f32[24,256]{1,0:T(8,128)S(1)} %get-tuple-element.94), channel_id=1, source_target_pairs={{0,24},{8,16},{16,8},{24,0},{1,25},{9,17},{17,9},{25,1},{2,26},{10... | collective-permute-start | bytes 73736 | tf_op jit(solution)/shard_map/ppermute | solution.py:1315
  8.8 0.1 collective-permute-start.19
  8.9 1.1 %side.1 = (s32[8]{0:T(128)S(1)}, s32[9]{0:T(128)S(1)}, f32[8,16,256]{2,1,0:T(8,128)S(1)}, f32[32,128]{1,0:T(8,128)S(1)}, f32[32,128]{1,0:T(8,128)S(1)}) custom-call(s32[8,32]{1,0:T(8,128)S(1)} %get-tuple-element.84.child_ref, s32[1,32]{1,0:T(1,128)S(1)} %get-tuple-element.348.owner_ref, s32[1,32]{1,0:T(1,128)S(1)} %get-tuple-element.86.place_ref, ...), custom_call_target="tpu_custom_call" | custom-call | tf_op jit(solution)/shard_map/side/pallas_call | solution.py:1316
  10.1 0.1 collective-permute-start.26
  10.1 3.2 %collective-permute-done.19.rest_1_ = f32[8,256]{1,0:T(8,128)S(1)} collective-permute-done((f32[8,256]{1,0:T(8,128)S(1)}, f32[8,256]{1,0:T(8,128)S(1)}, u32[]{:S(2)}, u32[]{:S(2)}) %collective-permute-start.19) | collective-permute-done | bytes 8224 | tf_op jit(solution)/shard_map/ppermute | solution.py:1315
  13.3 0.1 join.1
  13.4 1.5 %collective-permute-start.21 = (f32[64,256]{1,0:T(8,128)S(1)}, f32[64,256]{1,0:T(8,128)S(1)}, u32[]{:S(2)}, u32[]{:S(2)}) collective-permute-start(f32[64,256]{1,0:T(8,128)S(1)} %get-tuple-element.95), channel_id=1, source_target_pairs={{0,2},{1,3},{2,0},{3,1},{4,6},{5,7},{6,4},{7,5},{8,10},{9,11},{10,... | collective-permute-start | bytes 196616 | tf_op jit(solution)/shard_map/ppermute | solution.py:1347
  15.0 1.5 %collective-permute-start.22 = (f32[64,256]{1,0:T(8,128)S(1)}, f32[64,256]{1,0:T(8,128)S(1)}, u32[]{:S(2)}, u32[]{:S(2)}) collective-permute-start(f32[64,256]{1,0:T(8,128)S(1)} %get-tuple-element.95), channel_id=1, source_target_pairs={{0,4},{1,5},{2,6},{3,7},{4,0},{5,1},{6,2},{7,3},{8,12},{9,13},{10,... | collective-permute-start | bytes 196616 | tf_op jit(solution)/shard_map/ppermute | solution.py:1347
  16.5 0.5 %collective-permute-start.23 = (f32[64,256]{1,0:T(8,128)S(1)}, f32[64,256]{1,0:T(8,128)S(1)}, u32[]{:S(2)}, u32[]{:S(2)}) collective-permute-start(f32[64,256]{1,0:T(8,128)S(1)} %get-tuple-element.95), channel_id=1, source_target_pairs={{0,6},{1,7},{2,4},{3,5},{4,2},{5,3},{6,0},{7,1},{8,14},{9,15},{10,... | collective-permute-start | bytes 196616 | tf_op jit(solution)/shard_map/ppermute | solution.py:1347
  17.0 1.3 %collective-permute-done.21 = f32[64,256]{1,0:T(8,128)S(1)} collective-permute-done((f32[64,256]{1,0:T(8,128)S(1)}, f32[64,256]{1,0:T(8,128)S(1)}, u32[]{:S(2)}, u32[]{:S(2)}) %collective-permute-start.21) | collective-permute-done | bytes 65568 | tf_op jit(solution)/shard_map/ppermute | solution.py:1347
  18.3 1.2 %collective-permute-done.22 = f32[64,256]{1,0:T(8,128)S(1)} collective-permute-done((f32[64,256]{1,0:T(8,128)S(1)}, f32[64,256]{1,0:T(8,128)S(1)}, u32[]{:S(2)}, u32[]{:S(2)}) %collective-permute-start.22) | collective-permute-done | bytes 65568 | tf_op jit(solution)/shard_map/ppermute | solution.py:1347
  19.5 2.1 %collective-permute-done.23 = f32[64,256]{1,0:T(8,128)S(1)} collective-permute-done((f32[64,256]{1,0:T(8,128)S(1)}, f32[64,256]{1,0:T(8,128)S(1)}, u32[]{:S(2)}, u32[]{:S(2)}) %collective-permute-start.23) | collective-permute-done | bytes 65568 | tf_op jit(solution)/shard_map/ppermute | solution.py:1347
  21.7 0.1 collective-permute-start.25
  21.8 0.0 copy-start
  21.8 0.0 copy-start.1
  21.8 0.0 copy-start.2
  21.8 0.0 copy-start.3
  21.9 1.3 %collective-permute-done.25 = f32[3,64,256]{2,1,0:T(8,128)S(1)} collective-permute-done((f32[3,64,256]{2,1,0:T(8,128)S(1)}, f32[3,64,256]{2,1,0:T(8,128)S(1)}, u32[]{:S(2)}, u32[]{:S(2)}) %collective-permute-start.25) | collective-permute-done | bytes 196640 | tf_op jit(solution)/shard_map/ppermute | solution.py:1350
  23.2 0.0 copy-start.5
  23.2 2.4 %solve.1 = (f32[8,16,256]{2,1,0:T(8,128)}, f32[3,16,256]{2,1,0:T(8,128)}, s32[1]{0:T(128)}) custom-call(s32[8]{0:T(128)S(1)} %get-tuple-element.88.positions_in, s32[9]{0:T(128)S(1)} %get-tuple-element.89.owned_in, f32[8,64,256]{2,1,0:T(8,128)S(1)} %constant_dynamic-update-slice_fusion.15.all_ref, f32[32,128]{1,0:T(8,128)S(1)} %collective-permute-done.26.pair_ref, ...), custom_call_target="tpu_custom_call" | custom-call | tf_op jit(solution)/shard_map/solve/pallas_call | solution.py:1352
  25.6 0.8 %while.13 = (f32[8,16,256]{2,1,0:T(8,128)}, f32[3,16,256]{2,1,0:T(8,128)}, s32[1]{0:T(128)}, f32[8,16,256]{2,1,0:T(8,128)S(1)}, s32[8,6]{1,0:T(8,128)S(1)}, /*in...) while((f32[8,16,256]{2,1,0:T(8,128)}, ...), condition=%region_9.12_spmd.clone.clone, body=%region_0.11_spmd.sunk.clone.clone | while | flops 309503840 | bytes 22817100 | solution.py:1382
  (18 shorter events, 0.1 us)
Async XLA Ops:
  0.6 8.3 %copy-start.4 = (bf16[256,128]{1,0:T(8,128)(2,1)S(1)}, bf16[256,128]{1,0:T(8,128)(2,1)}, u32[]{:S(2)}) copy-start(bf16[256,128]{1,0:T(8,128)(2,1)} %constant.451.clone.table_ref) | copy-start | bytes 196612
  3.2 10.1 %collective-permute-start.18 = (f32[24,256]{1,0:T(8,128)S(1)}, f32[24,256]{1,0:T(8,128)S(1)}, u32[]{:S(2)}, u32[]{:S(2)}) collective-permute-start(f32[24,256]{1,0:T(8,128)S(1)} %get-tuple-element.92), channel_id=1, source_target_pairs={{0,8},{8,0},{16,24},{24,16},{1,9},{9,1},{17,25},{25,17},{2,10},{10... | collective-permute-start | bytes 73736 | tf_op jit(solution)/shard_map/ppermute | solution.py:1315
  6.3 7.0 %collective-permute-start.20 = (f32[24,256]{1,0:T(8,128)S(1)}, f32[24,256]{1,0:T(8,128)S(1)}, u32[]{:S(2)}, u32[]{:S(2)}) collective-permute-start(f32[24,256]{1,0:T(8,128)S(1)} %get-tuple-element.94), channel_id=1, source_target_pairs={{0,24},{8,16},{16,8},{24,0},{1,25},{9,17},{17,9},{25,1},{2,26},{10... | collective-permute-start | bytes 73736 | tf_op jit(solution)/shard_map/ppermute | solution.py:1315
  8.8 4.5 %collective-permute-start.19 = (f32[8,256]{1,0:T(8,128)S(1)}, f32[8,256]{1,0:T(8,128)S(1)}, u32[]{:S(2)}, u32[]{:S(2)}) collective-permute-start(f32[8,256]{1,0:T(8,128)S(1)} %get-tuple-element.93), channel_id=1, source_target_pairs={{0,16},{8,24},{16,0},{24,8},{1,17},{9,25},{17,1},{25,9},{2,18},{10... | collective-permute-start | bytes 24584 | tf_op jit(solution)/shard_map/ppermute | solution.py:1315
  10.1 13.1 %collective-permute-start.26 = (f32[32,128]{1,0:T(8,128)S(1)}, f32[32,128]{1,0:T(8,128)S(1)}, u32[]{:S(2)}, u32[]{:S(2)}) collective-permute-start(f32[32,128]{1,0:T(8,128)S(1)} %get-tuple-element.96), channel_id=1, source_target_pairs={{0,1},{1,0},{2,3},{3,2},{4,5},{5,4},{6,7},{7,6},{8,9},{9,8},{10,11... | collective-permute-start | bytes 49160 | tf_op jit(solution)/shard_map/ppermute | solution.py:1330
  13.4 4.8 %collective-permute-start.21 = (f32[64,256]{1,0:T(8,128)S(1)}, f32[64,256]{1,0:T(8,128)S(1)}, u32[]{:S(2)}, u32[]{:S(2)}) collective-permute-start(f32[64,256]{1,0:T(8,128)S(1)} %get-tuple-element.95), channel_id=1, source_target_pairs={{0,2},{1,3},{2,0},{3,1},{4,6},{5,7},{6,4},{7,5},{8,10},{9,11},{10,... | collective-permute-start | bytes 196616 | tf_op jit(solution)/shard_map/ppermute | solution.py:1347
  15.0 4.5 %collective-permute-start.22 = (f32[64,256]{1,0:T(8,128)S(1)}, f32[64,256]{1,0:T(8,128)S(1)}, u32[]{:S(2)}, u32[]{:S(2)}) collective-permute-start(f32[64,256]{1,0:T(8,128)S(1)} %get-tuple-element.95), channel_id=1, source_target_pairs={{0,4},{1,5},{2,6},{3,7},{4,0},{5,1},{6,2},{7,3},{8,12},{9,13},{10,... | collective-permute-start | bytes 196616 | tf_op jit(solution)/shard_map/ppermute | solution.py:1347
  16.5 5.2 %collective-permute-start.23 = (f32[64,256]{1,0:T(8,128)S(1)}, f32[64,256]{1,0:T(8,128)S(1)}, u32[]{:S(2)}, u32[]{:S(2)}) collective-permute-start(f32[64,256]{1,0:T(8,128)S(1)} %get-tuple-element.95), channel_id=1, source_target_pairs={{0,6},{1,7},{2,4},{3,5},{4,2},{5,3},{6,0},{7,1},{8,14},{9,15},{10,... | collective-permute-start | bytes 196616 | tf_op jit(solution)/shard_map/ppermute | solution.py:1347
  17.0 4.8 %collective-permute-start.24 = (f32[64,256]{1,0:T(8,128)S(1)}, f32[64,256]{1,0:T(8,128)S(1)}, u32[]{:S(2)}, u32[]{:S(2)}) collective-permute-start(f32[64,256]{1,0:T(8,128)S(1)} %get-tuple-element.95), channel_id=1, source_target_pairs={{0,1},{1,0},{2,3},{3,2},{4,5},{5,4},{6,7},{7,6},{8,9},{9,8},{10,11... | collective-permute-start | bytes 196616 | tf_op jit(solution)/shard_map/ppermute | solution.py:1348
  21.7 1.5 %collective-permute-start.25 = (f32[3,64,256]{2,1,0:T(8,128)S(1)}, f32[3,64,256]{2,1,0:T(8,128)S(1)}, u32[]{:S(2)}, u32[]{:S(2)}) collective-permute-start(f32[3,64,256]{2,1,0:T(8,128)S(1)} %pad_maximum_fusion.3), channel_id=1, source_target_pairs={{0,1},{1,0},{2,3},{3,2},{4,5},{5,4},{6,7},{7,6},{8,9},{9,8},{10,11... | collective-permute-start | bytes 589832 | tf_op jit(solution)/shard_map/ppermute | solution.py:1350
  21.8 1.4 %copy-start = (bf16[256,256]{1,0:T(8,128)(2,1)S(1)}, bf16[256,256]{1,0:T(8,128)(2,1)}, u32[]{:S(2)}) copy-start(bf16[256,256]{1,0:T(8,128)(2,1)} %constant.453.clone.table_p_ref) | copy-start | bytes 393220
  21.8 1.4 %copy-start.1 = (bf16[256,256]{1,0:T(8,128)(2,1)S(1)}, bf16[256,256]{1,0:T(8,128)(2,1)}, u32[]{:S(2)}) copy-start(bf16[256,256]{1,0:T(8,128)(2,1)} %constant.454.clone.table_l_ref) | copy-start | bytes 393220
  21.8 1.4 %copy-start.2 = (bf16[128,256]{1,0:T(8,128)(2,1)S(1)}, bf16[128,256]{1,0:T(8,128)(2,1)}, u32[]{:S(2)}) copy-start(bf16[128,256]{1,0:T(8,128)(2,1)} %constant.452.clone.table_w_ref) | copy-start | bytes 196612
  21.8 1.4 %copy-start.3 = (bf16[128,256]{1,0:T(8,128)(2,1)S(1)}, bf16[128,256]{1,0:T(8,128)(2,1)}, u32[]{:S(2)}) copy-start(bf16[128,256]{1,0:T(8,128)(2,1)} %constant.455.clone.table_x_ref) | copy-start | bytes 196612
  23.2 2.4 %copy-start.5 = (f32[8,16,256]{2,1,0:T(8,128)S(1)}, f32[8,16,256]{2,1,0:T(8,128)}, u32[]{:S(2)}) copy-start(f32[8,16,256]{2,1,0:T(8,128)} %rhs_hbm.1) | copy-start | bytes 393220
